TPU v7x, 256 devices: a whole 4x4x8 slice. The times are simulated.
256 devices in a mesh: pipe: 2 (over core), ctx: 128 (over z, y, x).
Axes of the slice: x: 4, y: 4, z: 8, core: 2. Of those that a mesh axis runs over, the one named last changes fastest.
Arguments:
- t_query: bfloat16 [2, 16384, 4096], P('pipe', 'ctx'), may hold values from -33 to 33
- t_key: bfloat16 [2, 16384, 512], P('pipe', 'ctx'), may hold values from -6 to 6
- t_value: bfloat16 [2, 16384, 512], P('pipe', 'ctx'), may hold values from -6 to 6
- s_query: bfloat16 [2, 16384, 4096], P('pipe', 'ctx'), may hold values from -33 to 33
- s_key: bfloat16 [2, 16384, 512], P('pipe', 'ctx'), may hold values from -6 to 6
- s_value: bfloat16 [2, 16384, 512], P('pipe', 'ctx'), may hold values from -6 to 6
- segment_ids: int32 [16384], replicated, may hold values from 0 to 127, never falling along the last dimension, each value on 1 to 256 neighbouring positions
Outputs:
- loss: float32 [], replicated
- query_grad: float32 [2, 16384, 4096], P('pipe', 'ctx')
- key_grad: float32 [2, 16384, 512], P('pipe', 'ctx')
- value_grad: float32 [2, 16384, 512], P('pipe', 'ctx')
Inputs may be any that keep to these rules, and one draw needn't show every extreme that they name: `segment_ids`: segment ids never fall along the tokens; a document holds at most 256 tokens, and one holds exactly that many.
All inputs are finite; a program needn't handle non-finite values.
Results may differ from a plain program's by a relative error of at most 0.006.
Values may be sent and summed in bfloat16 or wider, within the bound.
No kernel may reach another device: no remote copies, remote signals or barrier semaphores. Data moves between devices by JAX's collectives and lax.ppermute only.
A program may use at most 128 MiB of HBM per device.

v0:
```python
import jax
import jax.numpy as jnp
from jax import lax
from jax.sharding import PartitionSpec as P

REACH = 2
HEADS = 32
KV_HEADS = 4
HEAD_DIM = 128


NEG_FILL = -1e30


def shifted(block, axis, distance):
    devices = range(lax.axis_size(axis))
    route = [(i - distance, i) for i in devices if i - distance in devices]
    return lax.ppermute(block, axis, route)


def entering(array, axis, combine, identity):
    count, index = (lax.axis_size(axis), lax.axis_index(axis))
    everything = jax.tree.map(
        lambda part, kind: lax.all_gather(part.astype(kind), axis),
        array,
        (jnp.bfloat16, jnp.bfloat16),
    )
    start = jax.tree.map(
        lambda part, zero: jnp.broadcast_to(jnp.asarray(zero, part.dtype), part.shape),
        array,
        identity,
    )

    def entering_step(k, before):
        reached = k < index
        new = combine(
            before, jax.tree.map(lambda part, own: part[k].astype(own.dtype), everything, array)
        )
        return jax.tree.map(lambda a, b: jnp.where(reached, a, b), new, before)

    return lax.fori_loop(0, count, entering_step, start)


def prefix(value, axis, join, neutral):
    count, mine = (lax.axis_size(axis), lax.axis_index(axis))
    pieces = lax.all_gather(value, axis)
    pieces = pieces[::-1]
    mine = count - 1 - mine
    total = jnp.full_like(value, 0) + jnp.asarray(neutral, value.dtype)

    def prefix_step(position, total):
        longer = join(total, pieces[position])
        return jnp.where(position < mine, longer, total)

    return lax.fori_loop(0, count - 1, prefix_step, total)


def scores_of(query_half, keys_half):
    tok_rows = query_half.shape[0]
    key_count = keys_half.shape[0]
    grouped = query_half.reshape(tok_rows, KV_HEADS, HEADS // KV_HEADS, HEAD_DIM)
    key_heads = keys_half.reshape(key_count, KV_HEADS, HEAD_DIM)
    return jnp.einsum(
        "rkgd,wkd->kgrw", grouped, key_heads, preferred_element_type=jnp.float32
    ) * HEAD_DIM ** (-0.5)


def forward(query_half, keys_half, values_half, allowed):
    tok_rows = query_half.shape[0]
    scores = jnp.where(allowed[None, None], scores_of(query_half, keys_half), NEG_FILL)
    row_peak = jnp.max(scores, axis=-1, keepdims=True)
    expo = jnp.exp(scores - row_peak)
    row_total = jnp.sum(expo, axis=-1, keepdims=True)
    value_heads = values_half.reshape(values_half.shape[0], KV_HEADS, HEAD_DIM)
    mixed = jnp.einsum(
        "kgrw,wkd->rkgd", expo.astype(jnp.bfloat16), value_heads, preferred_element_type=jnp.float32
    )
    mixed = mixed / jnp.transpose(row_total, (2, 0, 1, 3))
    return (mixed.reshape(tok_rows, HEADS * HEAD_DIM).astype(jnp.bfloat16), row_peak, row_total)


def add_pair(earlier, later):
    return (earlier[0] + later[0], earlier[1] + later[1])


def add_single(earlier, later):
    return earlier + later


def per_device(t_query, t_key, t_value, s_query, s_key, s_value, segment_ids):
    tok_rows = t_query.shape[1]
    group = HEADS // KV_HEADS
    scale = HEAD_DIM ** (-0.5)
    key_pad = REACH * tok_rows
    key_span = key_pad + tok_rows
    device_pos = lax.axis_index("ctx")
    own_blocks = (t_key[0], t_value[0], s_key[0], s_value[0])
    collected = [own_blocks]
    for step_by in range(1, REACH + 1):
        collected.append(
            shifted((own_blocks[0], own_blocks[1], own_blocks[2], own_blocks[3]), "ctx", step_by)
        )
    ordered = collected[::-1]
    windows = [
        jnp.concatenate([blocks[member] for blocks in ordered], axis=0) for member in range(4)
    ]
    seg_front = jnp.concatenate([jnp.full((key_pad,), -1, jnp.int32), segment_ids])
    key_seg = lax.dynamic_slice_in_dim(seg_front, device_pos * tok_rows, key_span)
    query_seg = lax.dynamic_slice_in_dim(segment_ids, device_pos * tok_rows, tok_rows)
    causal = jnp.arange(key_span)[None, :] <= jnp.arange(tok_rows)[:, None] + key_pad
    allowed = (key_seg[None, :] == query_seg[:, None]) & causal
    teacher_out, unused_peak, unused_total = forward(t_query[0], windows[0], windows[1], allowed)
    student_out, row_peak, row_total = forward(s_query[0], windows[2], windows[3], allowed)
    zeros_full = jnp.zeros((tok_rows, HEADS * HEAD_DIM), jnp.float32)
    student_f = student_out.astype(jnp.float32)
    teacher_f = teacher_out.astype(jnp.float32)
    before_student, before_teacher = entering(
        (student_f, teacher_f), "pipe", add_pair, (zeros_full, zeros_full)
    )
    ahead = shifted(teacher_out, "pipe", -1)
    student_sum = before_student + student_f
    teacher_sum = before_teacher + teacher_f + ahead.astype(jnp.float32)
    gap = student_sum - teacher_sum
    total_squares = lax.psum(jnp.sum(gap * gap), ("pipe", "ctx"))
    loss = total_squares / float(
        lax.axis_size("pipe") * lax.axis_size("ctx") * tok_rows * HEADS * HEAD_DIM
    )
    after_gap = prefix(gap, "pipe", add_single, zeros_full)
    out_grad = after_gap + gap
    grad_half = out_grad.astype(jnp.bfloat16)
    grad_heads = grad_half.reshape(tok_rows, KV_HEADS, group, HEAD_DIM)
    query_heads = s_query[0].reshape(tok_rows, KV_HEADS, group, HEAD_DIM)
    key_heads = windows[2].reshape(key_span, KV_HEADS, HEAD_DIM)
    value_heads = windows[3].reshape(key_span, KV_HEADS, HEAD_DIM)
    scores = jnp.where(allowed[None, None], scores_of(s_query[0], windows[2]), NEG_FILL)
    prob = jnp.exp(scores - row_peak) / row_total
    prob_half = prob.astype(jnp.bfloat16)
    dprob = jnp.einsum(
        "rkgd,wkd->kgrw", grad_heads, value_heads, preferred_element_type=jnp.float32
    )
    out_heads = student_out.reshape(tok_rows, KV_HEADS, group, HEAD_DIM)
    delta = jnp.einsum("rkgd,rkgd->kgr", grad_heads, out_heads, preferred_element_type=jnp.float32)
    dscore = (prob * (dprob - delta[..., None])).astype(jnp.bfloat16)
    query_grad = (
        jnp.einsum("kgrw,wkd->rkgd", dscore, key_heads, preferred_element_type=jnp.float32).reshape(
            tok_rows, HEADS * HEAD_DIM
        )
        * scale
    )
    key_width = KV_HEADS * HEAD_DIM
    key_win = (
        jnp.einsum(
            "kgrw,rkgd->wkd", dscore, query_heads, preferred_element_type=jnp.float32
        ).reshape(key_span, key_width)
        * scale
    )
    value_win = jnp.einsum(
        "kgrw,rkgd->wkd", prob_half, grad_heads, preferred_element_type=jnp.float32
    ).reshape(key_span, key_width)
    key_grad = key_win[key_pad:]
    value_grad = value_win[key_pad:]
    for step_by in range(1, REACH + 1):
        first = (REACH - step_by) * tok_rows
        outgoing = (key_win[first : first + tok_rows], value_win[first : first + tok_rows])
        returned = shifted((outgoing[0], outgoing[1]), "ctx", -step_by)
        key_grad = key_grad + returned[0]
        value_grad = value_grad + returned[1]
    return (loss, query_grad[None], key_grad[None], value_grad[None])


def solution(mesh):
    placed = (
        P("pipe", "ctx", None),
        P("pipe", "ctx", None),
        P("pipe", "ctx", None),
        P("pipe", "ctx", None),
        P("pipe", "ctx", None),
        P("pipe", "ctx", None),
        P(),
    )
    return jax.shard_map(
        per_device,
        mesh=mesh,
        in_specs=placed,
        out_specs=(P(), P("pipe", "ctx", None), P("pipe", "ctx", None), P("pipe", "ctx", None)),
        check_vma=False,
    )
```

profile of v0, /device:TPU:1, one launch (start us, length us, event | category | flops | bytes accessed | tf_op | source)
XLA Modules:
  0.0 255.8 jit_solution(8808484663741850094)
XLA Ops:
  8.3 6.1 %collective-permute-start.2 = (bf16[128,512]{0,1:T(8,128)(2,1)S(1)}, bf16[128,512]{0,1:T(8,128)(2,1)}, u32[]{:S(2)}, u32[]{:S(2)}) collective-permute-start(bf16[128,512]{0,1:T(8,128)(2,1)S(1)} %bitcast.180), channel_id=1, source_target_pairs={{0,2},{1,3},{2,4},{3,5},{4,6},{5,7},{6,8},{7,9},{8,10},{9,11},{10,... | collective-permute-start | bytes 393224 | tf_op jit(solution)/shard_map/ppermute | solution.py:18
  14.5 2.9 %collective-permute-start.3 = (bf16[128,512]{0,1:T(8,128)(2,1)S(1)}, bf16[128,512]{0,1:T(8,128)(2,1)}, u32[]{:S(2)}, u32[]{:S(2)}) collective-permute-start(bf16[128,512]{0,1:T(8,128)(2,1)S(1)} %bitcast.181), channel_id=1, source_target_pairs={{0,1},{1,2},{2,3},{3,4},{4,5},{5,6},{6,7},{7,8},{8,9},{9,10},{10,1... | collective-permute-start | bytes 393224 | tf_op jit(solution)/shard_map/ppermute | solution.py:18
  19.0 4.0 %collective-permute-start.6 = (bf16[128,512]{0,1:T(8,128)(2,1)}, bf16[128,512]{0,1:T(8,128)(2,1)}, u32[]{:S(2)}, u32[]{:S(2)}) collective-permute-start(bf16[128,512]{0,1:T(8,128)(2,1)} %bitcast.26), channel_id=1, source_target_pairs={{0,2},{1,3},{2,4},{3,5},{4,6},{5,7},{6,8},{7,9},{8,10},{9,11},{10,... | collective-permute-start | bytes 393224 | tf_op jit(solution)/shard_map/ppermute | solution.py:18
  23.0 3.8 %collective-permute-start.7 = (bf16[128,512]{0,1:T(8,128)(2,1)}, bf16[128,512]{0,1:T(8,128)(2,1)}, u32[]{:S(2)}, u32[]{:S(2)}) collective-permute-start(bf16[128,512]{0,1:T(8,128)(2,1)} %bitcast.26), channel_id=1, source_target_pairs={{0,1},{1,2},{2,3},{3,4},{4,5},{5,6},{6,7},{7,8},{8,9},{9,10},{10,1... | collective-permute-start | bytes 393224 | tf_op jit(solution)/shard_map/ppermute | solution.py:18
  26.8 2.5 collective-permute-start
  37.2 3.7 %collective-permute-start.1 = (bf16[128,512]{1,0:T(8,128)(2,1)}, bf16[128,512]{1,0:T(8,128)(2,1)S(1)}, u32[]{:S(2)}, u32[]{:S(2)}) collective-permute-start(bf16[128,512]{1,0:T(8,128)(2,1)} %bitcast.2), channel_id=1, source_target_pairs={{0,1},{1,2},{2,3},{3,4},{4,5},{5,6},{6,7},{7,8},{8,9},{9,10},{10,1... | collective-permute-start | bytes 393224 | tf_op jit(solution)/shard_map/ppermute | solution.py:18
  42.0 3.5 %collective-permute-start.4 = (bf16[128,512]{1,0:T(8,128)(2,1)}, bf16[128,512]{1,0:T(8,128)(2,1)}, u32[]{:S(2)}, u32[]{:S(2)}) collective-permute-start(bf16[128,512]{1,0:T(8,128)(2,1)} %bitcast.183), channel_id=1, source_target_pairs={{0,2},{1,3},{2,4},{3,5},{4,6},{5,7},{6,8},{7,9},{8,10},{9,11},{10,... | collective-permute-start | bytes 393224 | tf_op jit(solution)/shard_map/ppermute | solution.py:18
  46.6 3.2 %collective-permute-start.5 = (bf16[128,512]{1,0:T(8,128)(2,1)}, bf16[128,512]{1,0:T(8,128)(2,1)}, u32[]{:S(2)}, u32[]{:S(2)}) collective-permute-start(bf16[128,512]{1,0:T(8,128)(2,1)} %bitcast.184), channel_id=1, source_target_pairs={{0,1},{1,2},{2,3},{3,4},{4,5},{5,6},{6,7},{7,8},{8,9},{9,10},{10,1... | collective-permute-start | bytes 393224 | tf_op jit(solution)/shard_map/ppermute | solution.py:18
  52.9 5.3 %fusion.7 = (f32[4,8,128]{2,1,0:T(8,128)S(1)}, f32[4,8,128]{2,1,0:T(8,128)}, f32[4,384,128,8]{2,1,3,0:T(8,128)}) fusion(f32[4,384,128,8]{2,1,3,0:T(8,128)S(1)} %get-tuple-element.191, f32[4,8,128]{2,1,0:T(8,128)S(1)} %get-tuple-element.190, pred[128,384]{0,1:T(8,128)(4,1)S(1)} %fusion.45, bf16[128,4,8,128]{3,2,1,0:T(8,128)(2,1)S(1)} %bitcast.173, ...), kind=kOutput, calls=%fused_computation.14 | convolution fusion | flops 414834688 | bytes 14123008 | tf_op jit(solution)/shard_map/rkgd,wkd->kgrw/dot_general | solution.py:63
  59.4 4.6 %fusion.24 = bf16[128,4,8,128]{0,3,2,1:T(8,128)(2,1)S(1)} fusion(f32[4,384,128,8]{2,1,3,0:T(8,128)} %copy-done, f32[4,8,128]{2,1,0:T(8,128)S(1)} %get-tuple-element.190, pred[128,384]{0,1:T(8,128)(4,1)S(1)} %fusion.45, f32[128,4,8]{0,2,1:T(8,128)S(1)} %bitcast.194, bf16[128,4,128]{0,2,1:T(8,128)(2,1)S(1)} %bitcast.185, ...), kind=kOutput, calls=%fused_computation.32 | convolution fusion | flops 411172864 | bytes 7815168 | tf_op jit(solution)/shard_map/kgrw,wkd->rkgd/dot_general | solution.py:75
  69.0 8.5 %fusion.35 = (bf16[4,8,128,384]{2,3,1,0:T(8,128)(2,1)}, f32[4,8,128]{2,1,0:T(8,128)S(1)}) fusion(f32[4,8,128]{2,1,0:T(8,128)} %copy-done.21, f32[4,8,128]{2,1,0:T(8,128)S(1)} %get-tuple-element.190, f32[4,384,128,8]{2,1,3,0:T(8,128)} %copy-done, pred[128,384]{0,1:T(8,128)(4,1)} %copy-done.7, f32[4,8,128]{2,1,0:T(8,128)} %get-tuple-element.165, ...), kind=kLoop, calls=%fused_computation.47 | loop fusion | flops 14151680 | bytes 15843328 | tf_op jit(solution)/shard_map/convert_element_type | solution.py:137
  77.5 2.8 %fusion.23 = bf16[128,4,8,128]{0,3,2,1:T(8,128)(2,1)} fusion(f32[4,384,128,8]{2,1,3,0:T(8,128)S(1)} %bitcast.169, f32[4,8,128]{2,1,0:T(8,128)S(1)} %copy-done.23, pred[128,384]{0,1:T(8,128)(4,1)S(1)} %copy-done.8, f32[128,4,8]{0,2,1:T(8,128)S(1)} %bitcast.195, bf16[128,4,128]{0,2,1:T(8,128)(2,1)S(1)} %bitcast.191, bf16[128,4,128]{0,2,1:T(8,128)(2,1)S(1)} %bitcast.193, ...), kind=kOutput, calls=%fused_computation.30 | convolution fusion | flops 411172864 | bytes 7815168 | tf_op jit(solution)/shard_map/kgrw,wkd->rkgd/dot_general | solution.py:75
  84.3 2.9 %copy.103 = f32[128,4096]{1,0:T(8,128)} copy(f32[128,4096]{0,1:T(8,128)} %bitcast_convert_fusion) | data formatting | bytes 4194304 | tf_op jit(solution)/shard_map/convert_element_type | solution.py:115
  89.5 6.0 %collective-permute-start.8 = (bf16[128,4096]{1,0:T(8,128)(2,1)}, bf16[128,4096]{1,0:T(8,128)(2,1)}, u32[]{:S(2)}, u32[]{:S(2)}) collective-permute-start(bf16[128,4096]{1,0:T(8,128)(2,1)} %copy.104), channel_id=1, source_target_pairs={{128,0},{129,1},{130,2},{131,3},{132,4},{133,5},{134,6},{135,7},{1... | collective-permute-start | bytes 3145736 | tf_op jit(solution)/shard_map/ppermute | solution.py:18
  95.5 8.8 %all-gather.7.cloned.1.call-done = bf16[2,128,4096]{2,1,0:T(8,128)(2,1)} async-done(((bf16[1,128,4096]{2,1,0:T(8,128)(2,1)}), bf16[2,128,4096]{2,1,0:T(8,128)(2,1)}) %all-gather.7.cloned.1.call-update) | async-done | bytes 2097168 | tf_op jit(solution)/shard_map/all_gather | solution.py:24
  104.3 9.4 %while.10 = (s32[]{:T(128)}, f32[128,4096]{1,0:T(8,128)S(1)}, f32[128,4096]{1,0:T(8,128)}, s32[]{:T(128)}, bf16[2,128,4096]{2,1,0:T(8,128)(2,1)}, /*index=5*/bf16[2,128,4096]{2,1,0:T(8,128)(2,1)}, s32[]{:T(128)}, s32[]{:T(128)}) while((s32[]{:T(128)}, f32[128,4096]{1,0:T(8,128)S(1)}, f32[128,4096]{1,0:T(8,128)}, s32[]{:T(128)}, ...), condition=%wide.region_5.6_spmd.clone, body=%wide.region_4.5_spmd.clone.sunk | while | flops 4194308 | bytes 10485869 | solution.py:41
  104.3 4.4 %add_select_fusion.3 = (f32[128,4096]{1,0:T(8,128)}, f32[128,4096]{1,0:T(8,128)S(1)}) fusion(f32[128,4096]{1,0:T(8,128)} %get-tuple-element.244, bf16[2,128,4096]{2,1,0:T(8,128)(2,1)} %get-tuple-element.255, s32[]{:T(128)} %get-tuple-element.242, pred[]{:T(512)S(6)} %compare.4, pred[]{:T(512)S(6)} %lt.35, bf16[2,128,4096]{2,1,0:T(8,128)(2,1)} %get-tuple-element.254, ...), kind=kLoop, calls=%fused_computation.clone.1 | loop fusion | flops 4194304 | bytes 10485766 | tf_op jit(solution)/shard_map/while/body/eval_jaxpr/jit(_where)/select_n | solution.py:39
  108.7 5.0 %add_select_fusion.3 = (f32[128,4096]{1,0:T(8,128)}, f32[128,4096]{1,0:T(8,128)S(1)}) fusion(f32[128,4096]{1,0:T(8,128)} %get-tuple-element.244, bf16[2,128,4096]{2,1,0:T(8,128)(2,1)} %get-tuple-element.255, s32[]{:T(128)} %get-tuple-element.242, pred[]{:T(512)S(6)} %compare.4, pred[]{:T(512)S(6)} %lt.35, bf16[2,128,4096]{2,1,0:T(8,128)(2,1)} %get-tuple-element.254, ...), kind=kLoop, calls=%fused_computation.clone.1 | loop fusion | flops 4194304 | bytes 10485766 | tf_op jit(solution)/shard_map/while/body/eval_jaxpr/jit(_where)/select_n | solution.py:39
  113.7 5.4 %multiply_reduce_fusion.1 = (f32[]{:T(128)}, f32[128,4096]{1,0:T(8,128)}) fusion(bf16[128,4096]{1,0:T(8,128)(2,1)} %collective-permute-done.8, f32[128,4096]{1,0:T(8,128)} %get-tuple-element.130, bf16[128,4096]{1,0:T(8,128)(2,1)} %copy.104, f32[128,4096]{1,0:T(8,128)S(1)} %get-tuple-element.129, f32[128,4096]{1,0:T(8,128)} %copy.103), kind=kLoop, calls=%fused_computation.34 | loop fusion | flops 4194303 | bytes 10485764 | tf_op jit(solution)/shard_map/reduce_sum | solution.py:124
  119.2 5.3 %copy.115 = bf16[4,8,128,384]{3,1,0,2:T(8,128)(2,1)} copy(bf16[4,8,128,384]{2,3,1,0:T(8,128)(2,1)} %get-tuple-element.188) | data formatting | bytes 6291456 | tf_op jit(solution)/shard_map/convert_element_type | solution.py:137
  124.5 77.4 %psum.7 = f32[]{:T(128)} all-reduce(f32[]{:T(128)} %get-tuple-element.178), channel_id=1, replica_groups=mesh['pipe'=2,'ctx'=128] {'pipe','ctx'}, use_global_device_ids=true, to_apply=%region_7.8 | all-reduce | flops 1 | bytes 8 | tf_op jit(solution)/shard_map/psum | solution.py:124
  218.5 5.7 %fusion.1 = bf16[4,8,128,384]{2,3,1,0:T(8,128)(2,1)S(1)} fusion(f32[4,8,128]{2,1,0:T(8,128)S(1)} %multiply_reduce_fusion, bf16[128,4,8,128]{3,2,1,0:T(8,128)(2,1)} %bitcast.166, f32[4,8,128]{2,1,0:T(8,128)S(1)} %copy-done.22, f32[4,8,128]{2,1,0:T(8,128)S(1)} %get-tuple-element.190, f32[4,384,128,8]{2,1,3,0:T(8,128)} %copy-done, ...), kind=kOutput, calls=%fused_computation.4 | convolution fusion | flops 414842880 | bytes 10977280 | tf_op jit(solution)/shard_map/rkgd,wkd->kgrw/dot_general | solution.py:138
  236.6 2.9 %copy.119 = f32[1,128,4096]{2,1,0:T(8,128)} copy(f32[1,128,4096]{1,2,0:T(8,128)} %bitcast.167) | data formatting | bytes 4194304
  241.2 5.1 %collective-permute-done.9 = f32[128,512]{1,0:T(8,128)} collective-permute-done((f32[128,512]{1,0:T(8,128)}, f32[128,512]{1,0:T(8,128)}, u32[]{:S(2)}, u32[]{:S(2)}) %collective-permute-start.9) | collective-permute-done | bytes 262176 | tf_op jit(solution)/shard_map/ppermute | solution.py:18
  (122 shorter events, 59.8 us)
Async XLA Ops:
  7.2 28.9 %copy-start.6 = (bf16[1,128,4096]{2,1,0:T(8,128)(2,1)S(1)}, bf16[1,128,4096]{2,1,0:T(8,128)(2,1)}, u32[]{:S(2)}) copy-start(bf16[1,128,4096]{2,1,0:T(8,128)(2,1)} %param.9) | copy-start | bytes 3145732
  7.2 29.2 %copy-start.10 = (bf16[1,128,512]{2,1,0:T(8,128)(2,1)S(1)}, bf16[1,128,512]{2,1,0:T(8,128)(2,1)}, u32[]{:S(2)}) copy-start(bf16[1,128,512]{2,1,0:T(8,128)(2,1)} %param.11) | copy-start | bytes 393220
  7.2 88.3 %all-gather.5.cloned.1.call-start = ((), (), s32[]{:S(2)}) async-start(), calls=%async_computation | async-start | bytes 3145728 | tf_op jit(solution)/shard_map/all_gather | solution.py:24
  8.3 28.9 %collective-permute-start.2 = (bf16[128,512]{0,1:T(8,128)(2,1)S(1)}, bf16[128,512]{0,1:T(8,128)(2,1)}, u32[]{:S(2)}, u32[]{:S(2)}) collective-permute-start(bf16[128,512]{0,1:T(8,128)(2,1)S(1)} %bitcast.180), channel_id=1, source_target_pairs={{0,2},{1,3},{2,4},{3,5},{4,6},{5,7},{6,8},{7,9},{8,10},{9,11},{10,... | collective-permute-start | bytes 393224 | tf_op jit(solution)/shard_map/ppermute | solution.py:18
  14.5 27.5 %collective-permute-start.3 = (bf16[128,512]{0,1:T(8,128)(2,1)S(1)}, bf16[128,512]{0,1:T(8,128)(2,1)}, u32[]{:S(2)}, u32[]{:S(2)}) collective-permute-start(bf16[128,512]{0,1:T(8,128)(2,1)S(1)} %bitcast.181), channel_id=1, source_target_pairs={{0,1},{1,2},{2,3},{3,4},{4,5},{5,6},{6,7},{7,8},{8,9},{9,10},{10,1... | collective-permute-start | bytes 393224 | tf_op jit(solution)/shard_map/ppermute | solution.py:18
  19.0 27.6 %collective-permute-start.6 = (bf16[128,512]{0,1:T(8,128)(2,1)}, bf16[128,512]{0,1:T(8,128)(2,1)}, u32[]{:S(2)}, u32[]{:S(2)}) collective-permute-start(bf16[128,512]{0,1:T(8,128)(2,1)} %bitcast.26), channel_id=1, source_target_pairs={{0,2},{1,3},{2,4},{3,5},{4,6},{5,7},{6,8},{7,9},{8,10},{9,11},{10,... | collective-permute-start | bytes 393224 | tf_op jit(solution)/shard_map/ppermute | solution.py:18
  23.0 27.8 %collective-permute-start.7 = (bf16[128,512]{0,1:T(8,128)(2,1)}, bf16[128,512]{0,1:T(8,128)(2,1)}, u32[]{:S(2)}, u32[]{:S(2)}) collective-permute-start(bf16[128,512]{0,1:T(8,128)(2,1)} %bitcast.26), channel_id=1, source_target_pairs={{0,1},{1,2},{2,3},{3,4},{4,5},{5,6},{6,7},{7,8},{8,9},{9,10},{10,1... | collective-permute-start | bytes 393224 | tf_op jit(solution)/shard_map/ppermute | solution.py:18
  26.8 31.4 %collective-permute-start = (bf16[128,512]{1,0:T(8,128)(2,1)}, bf16[128,512]{1,0:T(8,128)(2,1)}, u32[]{:S(2)}, u32[]{:S(2)}) collective-permute-start(bf16[128,512]{1,0:T(8,128)(2,1)} %bitcast.2), channel_id=1, source_target_pairs={{0,2},{1,3},{2,4},{3,5},{4,6},{5,7},{6,8},{7,9},{8,10},{9,11},{10,... | collective-permute-start | bytes 393224 | tf_op jit(solution)/shard_map/ppermute | solution.py:18
  34.3 18.6 %copy-start.2 = (bf16[1,128,4096]{1,2,0:T(8,128)(2,1)}, bf16[1,128,4096]{1,2,0:T(8,128)(2,1)S(1)}, u32[]{:S(2)}) copy-start(bf16[1,128,4096]{1,2,0:T(8,128)(2,1)S(1)} %copy.141) | copy-start | bytes 3145732
  37.2 22.2 %copy-start.7 = (pred[128,384]{0,1:T(8,128)(4,1)}, pred[128,384]{0,1:T(8,128)(4,1)S(1)}, u32[]{:S(2)}) copy-start(pred[128,384]{0,1:T(8,128)(4,1)S(1)} %fusion.45) | copy-start | bytes 147460
  37.2 22.0 %collective-permute-start.1 = (bf16[128,512]{1,0:T(8,128)(2,1)}, bf16[128,512]{1,0:T(8,128)(2,1)S(1)}, u32[]{:S(2)}, u32[]{:S(2)}) collective-permute-start(bf16[128,512]{1,0:T(8,128)(2,1)} %bitcast.2), channel_id=1, source_target_pairs={{0,1},{1,2},{2,3},{3,4},{4,5},{5,6},{6,7},{7,8},{8,9},{9,10},{10,1... | collective-permute-start | bytes 393224 | tf_op jit(solution)/shard_map/ppermute | solution.py:18
  42.0 23.4 %collective-permute-start.4 = (bf16[128,512]{1,0:T(8,128)(2,1)}, bf16[128,512]{1,0:T(8,128)(2,1)}, u32[]{:S(2)}, u32[]{:S(2)}) collective-permute-start(bf16[128,512]{1,0:T(8,128)(2,1)} %bitcast.183), channel_id=1, source_target_pairs={{0,2},{1,3},{2,4},{3,5},{4,6},{5,7},{6,8},{7,9},{8,10},{9,11},{10,... | collective-permute-start | bytes 393224 | tf_op jit(solution)/shard_map/ppermute | solution.py:18
  46.6 20.7 %collective-permute-start.5 = (bf16[128,512]{1,0:T(8,128)(2,1)}, bf16[128,512]{1,0:T(8,128)(2,1)}, u32[]{:S(2)}, u32[]{:S(2)}) collective-permute-start(bf16[128,512]{1,0:T(8,128)(2,1)} %bitcast.184), channel_id=1, source_target_pairs={{0,1},{1,2},{2,3},{3,4},{4,5},{5,6},{6,7},{7,8},{8,9},{9,10},{10,1... | collective-permute-start | bytes 393224 | tf_op jit(solution)/shard_map/ppermute | solution.py:18
  65.4 38.9 %all-gather.7.cloned.1.call-start = ((), (), s32[]{:S(2)}) async-start(), calls=%async_computation.1 | async-start | bytes 3145728 | tf_op jit(solution)/shard_map/all_gather | solution.py:24
  65.4 12.0 %slice-start = ((s8[6291456]{0:T(1024)(128)(4,1)}), s8[2097152]{0:T(1024)(128)(4,1)S(1)}, s32[]{:S(2)}) async-start(s8[6291456]{0:T(1024)(128)(4,1)} %bitcast.168), calls=%async_computation.3 | async-start | bytes 4194304
  68.9 8.5 %copy-start.20 = (bf16[128,512]{0,1:T(8,128)(2,1)S(1)}, bf16[128,512]{0,1:T(8,128)(2,1)}, u32[]{:S(2)}) copy-start(bf16[128,512]{0,1:T(8,128)(2,1)} %copy.93) | copy-start | bytes 393220
  68.9 8.5 %copy-start.23 = (f32[4,8,128]{2,1,0:T(8,128)S(1)}, f32[4,8,128]{2,1,0:T(8,128)}, u32[]{:S(2)}) copy-start(f32[4,8,128]{2,1,0:T(8,128)} %get-tuple-element.165) | copy-start | bytes 49156
  82.7 119.9 %all-gather.9.cloned.1.call-start = ((), (), s32[]{:S(2)}) async-start(), calls=%async_computation.2 | async-start | bytes 6291456 | tf_op jit(solution)/shard_map/all_gather | solution.py:46
  89.5 24.2 %collective-permute-start.8 = (bf16[128,4096]{1,0:T(8,128)(2,1)}, bf16[128,4096]{1,0:T(8,128)(2,1)}, u32[]{:S(2)}, u32[]{:S(2)}) collective-permute-start(bf16[128,4096]{1,0:T(8,128)(2,1)} %copy.104), channel_id=1, source_target_pairs={{128,0},{129,1},{130,2},{131,3},{132,4},{133,5},{134,6},{135,7},{1... | collective-permute-start | bytes 3145736 | tf_op jit(solution)/shard_map/ppermute | solution.py:18
  119.2 83.4 %copy-start.1 = (f32[128,4096]{1,0:T(8,128)S(1)}, f32[128,4096]{1,0:T(8,128)}, u32[]{:S(2)}) copy-start(f32[128,4096]{1,0:T(8,128)} %get-tuple-element.179) | copy-start | bytes 6291460
  210.2 29.3 %collective-permute-start.11 = (f32[128,512]{1,0:T(8,128)}, f32[128,512]{1,0:T(8,128)}, u32[]{:S(2)}, u32[]{:S(2)}) collective-permute-start(f32[128,512]{1,0:T(8,128)} %copy.116), channel_id=1, source_target_pairs={{1,0},{2,1},{3,2},{4,3},{5,4},{6,5},{7,6},{8,7},{9,8},{10,9},{11,1... | collective-permute-start | bytes 786440 | tf_op jit(solution)/shard_map/ppermute | solution.py:18
  213.3 26.2 %collective-permute-start.12 = (f32[128,512]{1,0:T(8,128)}, f32[128,512]{1,0:T(8,128)}, u32[]{:S(2)}, u32[]{:S(2)}) collective-permute-start(f32[128,512]{1,0:T(8,128)} %copy.118), channel_id=1, source_target_pairs={{2,0},{3,1},{4,2},{5,3},{6,4},{7,5},{8,6},{9,7},{10,8},{11,9},{12,... | collective-permute-start | bytes 786440 | tf_op jit(solution)/shard_map/ppermute | solution.py:18
  227.9 13.3 %collective-permute-start.10 = (f32[128,512]{1,0:T(8,128)}, f32[128,512]{1,0:T(8,128)}, u32[]{:S(2)}, u32[]{:S(2)}) collective-permute-start(f32[128,512]{1,0:T(8,128)} %copy.114), channel_id=1, source_target_pairs={{2,0},{3,1},{4,2},{5,3},{6,4},{7,5},{8,6},{9,7},{10,8},{11,9},{12,... | collective-permute-start | bytes 786440 | tf_op jit(solution)/shard_map/ppermute | solution.py:18
  231.0 15.4 %collective-permute-start.9 = (f32[128,512]{1,0:T(8,128)}, f32[128,512]{1,0:T(8,128)}, u32[]{:S(2)}, u32[]{:S(2)}) collective-permute-start(f32[128,512]{1,0:T(8,128)} %copy.112), channel_id=1, source_target_pairs={{1,0},{2,1},{3,2},{4,3},{5,4},{6,5},{7,6},{8,7},{9,8},{10,9},{11,1... | collective-permute-start | bytes 786440 | tf_op jit(solution)/shard_map/ppermute | solution.py:18
  (18 other events, 82.9 us)
Sparse Core Ops, SparseCore 0:
  65.5 19.7 all-gather.4
  87.1 17.1 all-gather.6
  119.3 20.2 all-gather.8
where the time goes:
time: 259 us; the launch traced here: 256 us
  blocking collectives  77.4 us (30%)
  local copies, waits for them, and re-layouts  51.4 us (20%)
  starting transfers between devices  40.9 us (16%)
  other arithmetic  32.6 us (13%)
  matrix products  23.3 us (9%)
  between operations  16.1 us (6%)
  waiting for transfers between devices  14 us (5%)
    psum x1, blocking collectives, per_device(): total_squares = lax.psum(jnp.sum(gap * gap), ('pipe', 'ctx'))  77.4 us
    ppermute x13, starting transfers between devices, shifted(): return lax.ppermute(block, axis, route)  40.8 us
    unnamed x60, local copies, waits for them, and re-layouts  12.3 us
    select_n x2, other arithmetic, entering_step(): return jax.tree.map(lambda a, b: jnp.where(reached, a, b), new, before)  9.41 us
    all_gather x2, waiting for transfers between devices, entering(): lax.all_gather(part.astype(kind), axis)  8.84 us
    convert_element_type x1, other arithmetic, per_device(): prob_half = prob.astype(jnp.bfloat16)  8.47 us
    dot_general x2, matrix products, forward(): jnp.einsum('kgrw,wkd->rkgd', expo.astype(jnp.bfloat16), value_heads, pref...  7.43 us
    dot_general x2, matrix products, scores_of(): jnp.einsum('rkgd,wkd->kgrw', grouped, key_heads, preferred_element_type=j...  6.29 us
  transfers between devices with their start and end apart: 16, of which 2 were waited for; matrix products, arithmetic and copies ran while one was open for 36% of the time, Pallas kernels for 0%

commit v1 on v0

v1 whole, which is shorter than its diff:
```python
import functools
import jax
import jax.numpy as jnp
from jax import lax
from jax.experimental import pallas as pl
from jax.experimental.pallas import tpu as pltpu
from jax.sharding import PartitionSpec as P

REACH = 2
HEADS = 32
KV_HEADS = 4
HEAD_DIM = 128
GROUP = HEADS // KV_HEADS
TOK = 128
SPAN = (REACH + 1) * TOK
PARTS = 2
PGROUPS = KV_HEADS // PARTS
PW = PGROUPS * HEAD_DIM
PQ = PGROUPS * GROUP * HEAD_DIM
PAIR = 2

NEG_FILL = -1e30
SCALE = HEAD_DIM ** (-0.5)
LOG2E = 1.4426950408889634
EXP_SCALE = SCALE * LOG2E
NT = (((1,), (1,)), ((), ()))
NN = (((1,), (0,)), ((), ()))
TN = (((0,), (0,)), ((), ()))


def mm(a, b, dims):
    return lax.dot_general(a, b, dims, preferred_element_type=jnp.float32)


def rotate(block, axis, distance):
    count = lax.axis_size(axis)
    return lax.ppermute(block, axis, [(i, (i + distance) % count) for i in range(count)])


def pack_body(pos_ref, tk, tv, sk, sv, seg0, seg1, seg2, *outs):
    packs, bias = outs[:PARTS], outs[PARTS]
    for p in range(PARTS):
        for m, src in enumerate((tk, tv, sk, sv)):
            packs[p][m] = src[0, :, p * PW : (p + 1) * PW]
    own = seg0[0].astype(jnp.float32)
    queries = jnp.broadcast_to(own, (TOK, TOK))
    for k, seg in enumerate((seg2, seg1, seg0)):
        keys = jnp.broadcast_to(seg[0].astype(jnp.float32), (TOK, TOK)).T
        ok = keys == queries
        if k == REACH:
            row = lax.broadcasted_iota(jnp.int32, (TOK, TOK), 0)
            col = lax.broadcasted_iota(jnp.int32, (TOK, TOK), 1)
            ok = ok & (row <= col)
        bias[k * TOK : (k + 1) * TOK, :] = jnp.where(ok, 0.0, NEG_FILL)


def pack(pos, blocks, segment_ids):
    count = segment_ids.shape[0] // TOK
    seg = segment_ids.reshape(count, 1, TOK)
    kv = pl.BlockSpec((1, TOK, KV_HEADS * HEAD_DIM), lambda i, pos: (0, 0, 0))
    segs = [
        pl.BlockSpec((1, 1, TOK), lambda i, pos, d=d: (lax.rem(pos[0] + count - d, count), 0, 0))
        for d in range(REACH + 1)
    ]
    whole = lambda *shape: pl.BlockSpec(shape, lambda i, pos: (0,) * len(shape))
    return pl.pallas_call(
        pack_body,
        grid_spec=pltpu.PrefetchScalarGridSpec(
            num_scalar_prefetch=1,
            grid=(1,),
            in_specs=[kv] * 4 + segs,
            out_specs=[whole(4, TOK, PW)] * PARTS + [whole(SPAN, TOK)],
        ),
        out_shape=[jax.ShapeDtypeStruct((4, TOK, PW), jnp.bfloat16)] * PARTS
        + [jax.ShapeDtypeStruct((SPAN, TOK), jnp.float32)],
        name="pack",
    )(pos, *blocks, seg, seg, seg)


def stacked(q_ref, pair):
    first = pair * PAIR
    return jnp.concatenate(
        [q_ref[0, :, (first + j) * HEAD_DIM : (first + j + 1) * HEAD_DIM] for j in range(PAIR)],
        axis=0,
    )


def forward_body(stage_ref, tq, sq, own, nb1, nb2, bias, s_out, t_out, send, lse):
    ahead = stage_ref[0].astype(jnp.float32) + 1.0
    mask = jnp.concatenate([bias[...]] * PAIR, axis=1)
    models = []
    for base in (0, 2):
        keys = jnp.concatenate([nb2[base], nb1[base], own[base]], axis=0)
        values = jnp.concatenate(
            [nb2[base + 1].T, nb1[base + 1].T, own[base + 1].T], axis=1
        )
        models.append((keys, values))
    for pair in range(GROUP // PAIR):
        outs = []
        for model, q_ref in enumerate((tq, sq)):
            keys, values = models[model]
            scores = mm(keys, stacked(q_ref, pair), NT) + mask
            peak = jnp.max(scores, axis=0, keepdims=True)
            expo = jnp.exp2((scores - peak) * EXP_SCALE)
            total = jnp.sum(expo, axis=0, keepdims=True)
            mixed = mm(values, expo.astype(jnp.bfloat16), NN) / total
            outs.append(mixed.astype(jnp.bfloat16))
            if model == 1:
                level = peak * EXP_SCALE + jnp.log2(total)
        t_half, s_half = outs
        diff = (s_half.astype(jnp.float32) - ahead * t_half.astype(jnp.float32)).astype(jnp.bfloat16)
        for j in range(PAIR):
            h = pair * PAIR + j
            rows, cols = pl.ds(h * HEAD_DIM, HEAD_DIM), slice(j * TOK, (j + 1) * TOK)
            s_out[rows, :] = s_half[:, cols]
            t_out[rows, :] = t_half[:, cols]
            send[rows, :] = diff[:, cols]
            lse[h : h + 1, :] = level[:, cols]


def forward(part, stage, t_query, s_query, own, nb1, nb2, bias):
    width = GROUP * HEAD_DIM
    query = pl.BlockSpec((1, TOK, width), lambda g, st: (0, 0, part * PGROUPS + g))
    kv = pl.BlockSpec((4, TOK, HEAD_DIM), lambda g, st: (0, 0, g))
    flipped = pl.BlockSpec((width, TOK), lambda g, st: (g, 0))
    half = jax.ShapeDtypeStruct((PQ, TOK), jnp.bfloat16)
    return pl.pallas_call(
        forward_body,
        grid_spec=pltpu.PrefetchScalarGridSpec(
            num_scalar_prefetch=1,
            grid=(PGROUPS,),
            in_specs=[query, query, kv, kv, kv, pl.BlockSpec((SPAN, TOK), lambda g, st: (0, 0))],
            out_specs=[flipped] * 3 + [pl.BlockSpec((GROUP, TOK), lambda g, st: (g, 0))],
        ),
        out_shape=[half] * 3 + [jax.ShapeDtypeStruct((PGROUPS * GROUP, TOK), jnp.float32)],
        cost_estimate=pl.CostEstimate(flops=8 * PQ * TOK * SPAN, bytes_accessed=6 * PQ * TOK * 2, transcendentals=2 * PQ * SPAN),
        name="forward",
    )(stage, t_query, s_query, own, nb1, nb2, bias)


def gap_body(stage_ref, s_out, t_out, recv, grad, delta, loss):
    stage = stage_ref[0].astype(jnp.float32)
    squares = jnp.zeros((8, TOK), jnp.float32)
    for h in range(PGROUPS * GROUP):
        rows = pl.ds(h * HEAD_DIM, HEAD_DIM)
        s = s_out[rows, :].astype(jnp.float32)
        t = t_out[rows, :].astype(jnp.float32)
        r = recv[rows, :].astype(jnp.float32)
        out_grad = (2.0 - stage) * (s - t) + r
        first = r - t
        sq = out_grad * out_grad + first * first
        squares = squares + jnp.sum(sq.reshape(HEAD_DIM // 8, 8, TOK), axis=0)
        half = out_grad.astype(jnp.bfloat16)
        grad[rows, :] = half
        delta[h : h + 1, :] = jnp.sum(half.astype(jnp.float32) * s, axis=0, keepdims=True)
    loss[...] = squares * stage


def gaps(stage, s_out, t_out, recv):
    heads = PGROUPS * GROUP
    whole = lambda *shape: pl.BlockSpec(shape, lambda i, st: (0,) * len(shape))
    return pl.pallas_call(
        gap_body,
        grid_spec=pltpu.PrefetchScalarGridSpec(
            num_scalar_prefetch=1,
            grid=(1,),
            in_specs=[whole(PQ, TOK)] * 3,
            out_specs=[whole(PQ, TOK), whole(heads, TOK), whole(8, TOK)],
        ),
        out_shape=[
            jax.ShapeDtypeStruct((PQ, TOK), jnp.bfloat16),
            jax.ShapeDtypeStruct((heads, TOK), jnp.float32),
            jax.ShapeDtypeStruct((8, TOK), jnp.float32),
        ],
        cost_estimate=pl.CostEstimate(flops=12 * PQ * TOK, bytes_accessed=4 * PQ * TOK * 2, transcendentals=0),
        name="gaps",
    )(stage, s_out, t_out, recv)


def backward_body(sq, own, nb1, nb2, bias, grad, delta, lse, *rest):
    dq, local, back1, back2 = rest[-4:]
    mask = jnp.concatenate([bias[...]] * PAIR, axis=1)
    keys = jnp.concatenate([nb2[0], nb1[0], own[0]], axis=0)
    values = jnp.concatenate([nb2[1], nb1[1], own[1]], axis=0)
    key_win = jnp.zeros((SPAN, HEAD_DIM), jnp.float32)
    value_win = jnp.zeros((SPAN, HEAD_DIM), jnp.float32)
    for pair in range(GROUP // PAIR):
        first = pair * PAIR
        queries = stacked(sq, pair)
        side = lambda ref, size: jnp.concatenate(
            [ref[(first + j) * size : (first + j + 1) * size, :] for j in range(PAIR)], axis=1
        )
        out_grad = side(grad, HEAD_DIM)
        scores = mm(keys, queries, NT) + mask
        prob = jnp.exp2(scores * EXP_SCALE - side(lse, 1))
        dprob = mm(values, out_grad, NN)
        dscore = (prob * (dprob - side(delta, 1))).astype(jnp.bfloat16)
        value_win = value_win + mm(prob.astype(jnp.bfloat16), out_grad, NT)
        key_win = key_win + mm(dscore, queries, NN)
        query_part = mm(dscore, keys, TN) * SCALE
        for j in range(PAIR):
            h = first + j
            dq[0, :, h * HEAD_DIM : (h + 1) * HEAD_DIM] = query_part[j * TOK : (j + 1) * TOK, :]
    key_win = key_win * SCALE
    for m, win in enumerate((key_win, value_win)):
        back2[m] = win[:TOK].astype(jnp.bfloat16)
        back1[m] = win[TOK : 2 * TOK].astype(jnp.bfloat16)
        local[m] = win[2 * TOK :]


def backward(part, s_query, own, nb1, nb2, bias, grad, delta, lse, dq):
    width = GROUP * HEAD_DIM
    query = pl.BlockSpec((1, TOK, width), lambda g: (0, 0, part * PGROUPS + g))
    kv = pl.BlockSpec((2, TOK, HEAD_DIM), lambda g: (1, 0, g))
    stat = pl.BlockSpec((GROUP, TOK), lambda g: (g, 0))
    in_specs = [query, kv, kv, kv, pl.BlockSpec((SPAN, TOK), lambda g: (0, 0))]
    in_specs += [pl.BlockSpec((width, TOK), lambda g: (g, 0)), stat, stat]
    args = [s_query, own, nb1, nb2, bias, grad, delta, lse]
    aliases = {}
    if dq is not None:
        in_specs.append(pl.BlockSpec(memory_space=pl.ANY))
        args.append(dq)
        aliases = {len(args) - 1: 0}
    pair = pl.BlockSpec((2, TOK, HEAD_DIM), lambda g: (0, 0, g))
    return pl.pallas_call(
        backward_body,
        grid=(PGROUPS,),
        in_specs=in_specs,
        out_specs=[query, pair, pair, pair],
        out_shape=[
            jax.ShapeDtypeStruct((1, TOK, HEADS * HEAD_DIM), jnp.float32),
            jax.ShapeDtypeStruct((2, TOK, PW), jnp.float32),
            jax.ShapeDtypeStruct((2, TOK, PW), jnp.bfloat16),
            jax.ShapeDtypeStruct((2, TOK, PW), jnp.bfloat16),
        ],
        input_output_aliases=aliases,
        cost_estimate=pl.CostEstimate(flops=10 * PQ * TOK * SPAN, bytes_accessed=8 * PQ * TOK, transcendentals=PQ * SPAN),
        name="backward",
    )(*args)


def finish_body(*refs):
    key_grad, value_grad = refs[-2:]
    for p in range(PARTS):
        local, ret1, ret2 = refs[3 * p : 3 * p + 3]
        cols = slice(p * PW, (p + 1) * PW)
        for m, out in enumerate((key_grad, value_grad)):
            out[0, :, cols] = local[m] + ret1[m].astype(jnp.float32) + ret2[m].astype(jnp.float32)


def finish(parts):
    shape = jax.ShapeDtypeStruct((1, TOK, KV_HEADS * HEAD_DIM), jnp.float32)
    return pl.pallas_call(finish_body, out_shape=[shape, shape], name="finish")(
        *[array for part in parts for array in part]
    )


def total_of(partial):
    value = partial
    distance = 1
    while distance < lax.axis_size("ctx"):
        value = value + rotate(value, "ctx", distance)
        distance *= 2
    value = value + rotate(value, "pipe", 1)
    return jnp.sum(value)


def per_device(t_query, t_key, t_value, s_query, s_key, s_value, segment_ids):
    pos = lax.axis_index("ctx").astype(jnp.int32).reshape(1)
    stage = lax.axis_index("pipe").astype(jnp.int32).reshape(1)
    *packs, bias = pack(pos, (t_key, t_value, s_key, s_value), segment_ids)
    near = [(rotate(block, "ctx", 1), rotate(block, "ctx", 2)) for block in packs]
    partial = jnp.zeros((8, TOK), jnp.float32)
    dq = None
    parts = []
    for part in range(PARTS):
        own, (nb1, nb2) = packs[part], near[part]
        s_out, t_out, send, lse = forward(part, stage, t_query, s_query, own, nb1, nb2, bias)
        recv = rotate(send, "pipe", 1)
        grad, delta, squares = gaps(stage, s_out, t_out, recv)
        partial = partial + squares
        dq, local, back1, back2 = backward(
            part, s_query, own, nb1, nb2, bias, grad, delta, lse, dq
        )
        parts.append((local, rotate(back1, "ctx", -1), rotate(back2, "ctx", -2)))
    sections, tokens = lax.axis_size("pipe"), lax.axis_size("ctx") * TOK
    loss = total_of(partial) / float(sections * tokens * HEADS * HEAD_DIM)
    key_grad, value_grad = finish(parts)
    return (loss, dq, key_grad, value_grad)


def solution(mesh):
    placed = P("pipe", "ctx", None)
    return jax.shard_map(
        per_device,
        mesh=mesh,
        in_specs=(placed,) * 6 + (P(),),
        out_specs=(P(), placed, placed, placed),
        check_vma=False,
    )
```

time: 259 us -> 122 us (0.47); the launches traced: 256 us -> 122 us
  blocking collectives: 77.4 us -> 0 us
  local copies, waits for them, and re-layouts: 51.4 us -> 4.4 us
  Pallas kernels: 0 us -> 36.7 us
  waiting for transfers between devices: 14 us -> 47 us
  other arithmetic: 32.6 us -> 1.31 us
  matrix products: 23.3 us -> 0 us
  between operations: 16.1 us -> 2.57 us
  starting transfers between devices: 40.9 us -> 29.9 us
    psum x1 -> x0, blocking collectives: 77.4 us -> none  [per_device(): total_squares = lax.psum(jnp.sum(gap * gap), ('pipe', 'ctx'))]
    ppermute x13 -> x18, waiting for transfers between devices: 5.13 us -> 47 us  [rotate(): lax.ppermute(block, axis, [(i, (i + distance) % count) for i in range(cou...]
    pallas_call x0 -> x8, Pallas kernels: none -> 36.7 us  [the longest x2 16.8 us: forward(): pl.pallas_call(forward_body, grid_spec=pltpu.PrefetchScalarGridSpec(num_s...]
    dot_general x8 -> x0, matrix products: 23.3 us -> none  [the longest x2 7.43 us: forward(): jnp.einsum('kgrw,wkd->rkgd', expo.astype(jnp.bfloat16), value_heads, pref...]
    convert_element_type x5 -> x0, local copies, waits for them, and re-layouts: 14.2 us -> none  [the longest x3 5.9 us: forward(): mixed.reshape(tok_rows, HEADS * HEAD_DIM).astype(jnp.bfloat16)]
    slice x8 -> x0, local copies, waits for them, and re-layouts: 11.1 us -> none  [the longest x3 4.51 us: per_device(): value_win[first:first + tok_rows]]
    ppermute x13 -> x18, starting transfers between devices: 40.8 us -> 29.9 us  [rotate(): lax.ppermute(block, axis, [(i, (i + distance) % count) for i in range(cou...]
    convert_element_type x2 -> x0, other arithmetic: 10 us -> none  [the longest x1 8.47 us: per_device(): prob_half = prob.astype(jnp.bfloat16)]
  transfers between devices with their start and end apart: 16 -> 18, of which waited for: 2 -> 9; matrix products, arithmetic and copies ran while one was open for 36% -> 1% of each run, Pallas kernels for 0% -> 25%
where the time goes in v1:
time: 122 us
  waiting for transfers between devices  47 us (39%)
  Pallas kernels  36.7 us (30%)
  starting transfers between devices  29.9 us (25%)
  local copies, waits for them, and re-layouts  4.4 us (4%)
  between operations  2.57 us (2%)
  other arithmetic  1.31 us (1%)
    ppermute x18, waiting for transfers between devices, rotate(): lax.ppermute(block, axis, [(i, (i + distance) % count) for i in range(cou...  47 us
    ppermute x18, starting transfers between devices, rotate(): lax.ppermute(block, axis, [(i, (i + distance) % count) for i in range(cou...  29.9 us
    pallas_call x2, Pallas kernels, forward(): pl.pallas_call(forward_body, grid_spec=pltpu.PrefetchScalarGridSpec(num_s...  16.8 us
    pallas_call x2, Pallas kernels, backward(): pl.pallas_call(backward_body, grid=(PGROUPS,), in_specs=in_specs, out_spe...  10.4 us
    pallas_call x2, Pallas kernels, gaps(): pl.pallas_call(gap_body, grid_spec=pltpu.PrefetchScalarGridSpec(num_scala...  5.39 us
    unnamed x24, local copies, waits for them, and re-layouts  4.4 us
  transfers between devices with their start and end apart: 18, of which 9 were waited for; matrix products, arithmetic and copies ran while one was open for 1% of the time, Pallas kernels for 25%

profile of v1, /device:TPU:1, one launch (start us, length us, event | category | flops | bytes accessed | tf_op | source)
XLA Modules:
  0.0 121.9 jit_solution(6401175324079655955)
XLA Ops:
  0.6 2.0 %pack.1 = (bf16[4,128,256]{2,1,0:T(8,128)(2,1)}, bf16[4,128,256]{2,1,0:T(8,128)(2,1)}, f32[384,128]{1,0:T(8,128)}) custom-call(s32[1]{0:T(128)} %bitcast.1.pos_ref, bf16[1,128,512]{2,1,0:T(8,128)(2,1)} %tk.1, bf16[1,128,512]{2,1,0:T(8,128)(2,1)} %tv.1, bf16[1,128,512]{2,1,0:T(8,128)(2,1)} %sk.1, bf16[1,128,512]{2,1,0:T(8,128)(2,1)} %sv.1, ...), custom_call_target="tpu_custom_call" | custom-call | tf_op jit(solution)/shard_map/pack/pallas_call | solution.py:66
  2.7 3.6 %collective-permute-start.4 = (bf16[4,128,256]{2,1,0:T(8,128)(2,1)}, bf16[4,128,256]{2,1,0:T(8,128)(2,1)S(1)}, u32[]{:S(2)}, u32[]{:S(2)}) collective-permute-start(bf16[4,128,256]{2,1,0:T(8,128)(2,1)} %get-tuple-element.37.own), channel_id=1, source_target_pairs={{0,2},{1,3},{2,4},{3,5},{4,6},{5,7},{6,8},{7,9},{8,10},{9,11},{10,... | collective-permute-start | bytes 786440 | tf_op jit(solution)/shard_map/ppermute | solution.py:37
  6.5 2.7 %collective-permute-start.1 = (bf16[4,128,256]{2,1,0:T(8,128)(2,1)}, bf16[4,128,256]{2,1,0:T(8,128)(2,1)S(1)}, u32[]{:S(2)}, u32[]{:S(2)}) collective-permute-start(bf16[4,128,256]{2,1,0:T(8,128)(2,1)} %get-tuple-element.31.own), channel_id=1, source_target_pairs={{0,2},{1,3},{2,4},{3,5},{4,6},{5,7},{6,8},{7,9},{8,10},{9,11},{10,... | collective-permute-start | bytes 786440 | tf_op jit(solution)/shard_map/ppermute | solution.py:37
  9.3 1.2 collective-permute-start
  10.5 9.7 %collective-permute-done.4.nb2 = bf16[4,128,256]{2,1,0:T(8,128)(2,1)S(1)} collective-permute-done((bf16[4,128,256]{2,1,0:T(8,128)(2,1)}, bf16[4,128,256]{2,1,0:T(8,128)(2,1)S(1)}, u32[]{:S(2)}, u32[]{:S(2)}) %collective-permute-start.4) | collective-permute-done | bytes 262176 | tf_op jit(solution)/shard_map/ppermute | solution.py:37
  20.2 9.3 %collective-permute-done.3.nb1 = bf16[4,128,256]{2,1,0:T(8,128)(2,1)S(1)} collective-permute-done((bf16[4,128,256]{2,1,0:T(8,128)(2,1)}, bf16[4,128,256]{2,1,0:T(8,128)(2,1)S(1)}, u32[]{:S(2)}, u32[]{:S(2)}) %collective-permute-start.3) | collective-permute-done | bytes 262176 | tf_op jit(solution)/shard_map/ppermute | solution.py:37
  30.2 8.4 %forward.3 = (bf16[2048,128]{1,0:T(8,128)(2,1)}, bf16[2048,128]{1,0:T(8,128)(2,1)}, bf16[2048,128]{1,0:T(8,128)(2,1)}, f32[16,128]{1,0:T(8,128)}) custom-call(s32[1]{0:T(128)} %bitcast.stage_ref, bf16[1,128,4096]{2,1,0:T(8,128)(2,1)} %tq.3, bf16[1,128,4096]{2,1,0:T(8,128)(2,1)} %sq.7, bf16[4,128,256]{2,1,0:T(8,128)(2,1)} %get-tuple-element.37.own, ...), custom_call_target="tpu_custom_call" | custom-call | flops 805306368 | bytes 3145728 | tf_op jit(solution)/shard_map/forward/pallas_call | solution.py:127
  38.6 2.5 %collective-permute-start.5 = (bf16[2048,128]{1,0:T(8,128)(2,1)}, bf16[2048,128]{1,0:T(8,128)(2,1)S(1)}, u32[]{:S(2)}, u32[]{:S(2)}) collective-permute-start(bf16[2048,128]{1,0:T(8,128)(2,1)} %get-tuple-element.40), channel_id=1, source_target_pairs={{0,128},{128,0},{1,129},{129,1},{2,130},{130,2},{3,131},{131,3},{4... | collective-permute-start | bytes 1572872 | tf_op jit(solution)/shard_map/ppermute | solution.py:37
  42.5 8.4 %forward.2 = (bf16[2048,128]{1,0:T(8,128)(2,1)}, bf16[2048,128]{1,0:T(8,128)(2,1)}, bf16[2048,128]{1,0:T(8,128)(2,1)}, f32[16,128]{1,0:T(8,128)}) custom-call(s32[1]{0:T(128)} %bitcast.stage_ref, bf16[1,128,4096]{2,1,0:T(8,128)(2,1)} %tq.3, bf16[1,128,4096]{2,1,0:T(8,128)(2,1)} %sq.7, bf16[4,128,256]{2,1,0:T(8,128)(2,1)} %get-tuple-element.31.own, ...), custom_call_target="tpu_custom_call" | custom-call | flops 805306368 | bytes 3145728 | tf_op jit(solution)/shard_map/forward/pallas_call | solution.py:127
  51.8 2.7 %gaps.3 = (bf16[2048,128]{1,0:T(8,128)(2,1)}, f32[16,128]{1,0:T(8,128)}, f32[8,128]{1,0:T(8,128)}) custom-call(s32[1]{0:T(128)} %bitcast.stage_ref, bf16[2048,128]{1,0:T(8,128)(2,1)} %get-tuple-element.38.s_out, bf16[2048,128]{1,0:T(8,128)(2,1)} %get-tuple-element.39.t_out, bf16[2048,128]{1,0:T(8,128)(2,1)} %copy-done.2), custom_call_target="tpu_custom_call" | custom-call | flops 3145728 | bytes 2097152 | tf_op jit(solution)/shard_map/gaps/pallas_call | solution.py:162
  54.5 0.8 copy-done.3
  55.3 2.7 %gaps.2 = (bf16[2048,128]{1,0:T(8,128)(2,1)}, f32[16,128]{1,0:T(8,128)}, f32[8,128]{1,0:T(8,128)}) custom-call(s32[1]{0:T(128)} %bitcast.stage_ref, bf16[2048,128]{1,0:T(8,128)(2,1)} %get-tuple-element.33.s_out, bf16[2048,128]{1,0:T(8,128)(2,1)} %get-tuple-element.34.t_out, bf16[2048,128]{1,0:T(8,128)(2,1)} %copy-done.3), custom_call_target="tpu_custom_call" | custom-call | flops 3145728 | bytes 2097152 | tf_op jit(solution)/shard_map/gaps/pallas_call | solution.py:162
  58.7 7.9 %collective-permute-done.6 = f32[8,128]{1,0:T(8,128)S(1)} collective-permute-done((f32[8,128]{1,0:T(8,128)S(1)}, f32[8,128]{1,0:T(8,128)S(1)}, u32[]{:S(2)}, u32[]{:S(2)}) %collective-permute-start.6) | collective-permute-done | bytes 4128 | tf_op jit(solution)/shard_map/ppermute | solution.py:37
  66.5 8.2 %collective-permute-done.7 = f32[8,128]{1,0:T(8,128)S(1)} collective-permute-done((f32[8,128]{1,0:T(8,128)S(1)}, f32[8,128]{1,0:T(8,128)S(1)}, u32[]{:S(2)}, u32[]{:S(2)}) %collective-permute-start.7) | collective-permute-done | bytes 4128 | tf_op jit(solution)/shard_map/ppermute | solution.py:37
  74.7 5.2 %backward.2 = (f32[1,128,4096]{2,1,0:T(8,128)}, f32[2,128,256]{2,1,0:T(8,128)}, bf16[2,128,256]{2,1,0:T(8,128)(2,1)}, bf16[2,128,256]{2,1,0:T(8,128)(2,1)}) custom-call(bf16[1,128,4096]{2,1,0:T(8,128)(2,1)} %sq.7, bf16[4,128,256]{2,1,0:T(8,128)(2,1)} %get-tuple-element.31.own, bf16[4,128,256]{2,1,0:T(8,128)(2,1)} %copy-done.5, ...), custom_call_target="tpu_custom_call" | custom-call | flops 1006632960 | bytes 2097152 | tf_op jit(solution)/shard_map/backward/pallas_call | solution.py:225
  80.5 5.3 %backward.3 = (f32[1,128,4096]{2,1,0:T(8,128)}, f32[2,128,256]{2,1,0:T(8,128)}, bf16[2,128,256]{2,1,0:T(8,128)(2,1)}, bf16[2,128,256]{2,1,0:T(8,128)(2,1)}) custom-call(bf16[1,128,4096]{2,1,0:T(8,128)(2,1)} %sq.7, bf16[4,128,256]{2,1,0:T(8,128)(2,1)} %get-tuple-element.37.own, bf16[4,128,256]{2,1,0:T(8,128)(2,1)} %copy-done.1, ...), custom_call_target="tpu_custom_call", output_to_operand_aliasing={{0}: (8, {})} | custom-call | flops 1006632960 | bytes 2097152 | tf_op jit(solution)/shard_map/backward/pallas_call | solution.py:225
  86.3 7.5 %collective-permute-start.14 = (bf16[2,128,256]{2,1,0:T(8,128)(2,1)S(1)}, bf16[2,128,256]{2,1,0:T(8,128)(2,1)S(1)}, u32[]{:S(2)}, u32[]{:S(2)}) collective-permute-start(bf16[2,128,256]{2,1,0:T(8,128)(2,1)S(1)} %copy-done.11), channel_id=1, source_target_pairs={{0,127},{1,0},{2,1},{3,2},{4,3},{5,4},{6,5},{7,6},{8,7},{9,8},{10,... | collective-permute-start | bytes 393224 | tf_op jit(solution)/shard_map/ppermute | solution.py:37
  93.9 3.7 %collective-permute-done.10 = f32[8,128]{1,0:T(8,128)S(1)} collective-permute-done((f32[8,128]{1,0:T(8,128)S(1)}, f32[8,128]{1,0:T(8,128)S(1)}, u32[]{:S(2)}, u32[]{:S(2)}) %collective-permute-start.10) | collective-permute-done | bytes 4128 | tf_op jit(solution)/shard_map/ppermute | solution.py:37
  97.5 4.9 %collective-permute-done.11 = f32[8,128]{1,0:T(8,128)S(1)} collective-permute-done((f32[8,128]{1,0:T(8,128)S(1)}, f32[8,128]{1,0:T(8,128)S(1)}, u32[]{:S(2)}, u32[]{:S(2)}) %collective-permute-start.11) | collective-permute-done | bytes 4128 | tf_op jit(solution)/shard_map/ppermute | solution.py:37
  102.4 4.5 %collective-permute-start.12 = (f32[8,128]{1,0:T(8,128)S(1)}, f32[8,128]{1,0:T(8,128)S(1)}, u32[]{:S(2)}, u32[]{:S(2)}) collective-permute-start(f32[8,128]{1,0:T(8,128)S(1)} %add.33), channel_id=1, source_target_pairs={{0,64},{1,65},{2,66},{3,67},{4,68},{5,69},{6,70},{7,71},{8,72},{9,... | collective-permute-start | bytes 12296 | tf_op jit(solution)/shard_map/ppermute | solution.py:37
  106.8 1.9 %collective-permute-done.12 = f32[8,128]{1,0:T(8,128)S(1)} collective-permute-done((f32[8,128]{1,0:T(8,128)S(1)}, f32[8,128]{1,0:T(8,128)S(1)}, u32[]{:S(2)}, u32[]{:S(2)}) %collective-permute-start.12) | collective-permute-done | bytes 4128 | tf_op jit(solution)/shard_map/ppermute | solution.py:37
  108.8 7.1 %collective-permute-start.13 = (f32[8,128]{1,0:T(8,128)S(1)}, f32[8,128]{1,0:T(8,128)S(1)}, u32[]{:S(2)}, u32[]{:S(2)}) collective-permute-start(f32[8,128]{1,0:T(8,128)S(1)} %add.34), channel_id=1, source_target_pairs={{0,128},{128,0},{1,129},{129,1},{2,130},{130,2},{3,131},{131,3},{4... | collective-permute-start | bytes 12296 | tf_op jit(solution)/shard_map/ppermute | solution.py:37
  115.8 0.8 collective-permute-done.13
  118.7 2.1 %finish.1 = (f32[1,128,512]{2,1,0:T(8,128)}, f32[1,128,512]{2,1,0:T(8,128)}) custom-call(f32[2,128,256]{2,1,0:T(8,128)} %get-tuple-element.50.refs_0_, bf16[2,128,256]{2,1,0:T(8,128)(2,1)} %copy-done.8, bf16[2,128,256]{2,1,0:T(8,128)(2,1)} %copy-done.9, f32[2,128,256]{2,1,0:T(8,128)} %get-tuple-element.53.refs_3_, bf16[2,128,256]{2,1,0:T(8,128)(2,1)} %copy-done.6, ...), custom_call_target="tpu_custom_call" | custom-call | tf_op jit(solution)/shard_map/finish/pallas_call | solution.py:253
  (53 shorter events, 6.5 us)
Async XLA Ops:
  2.7 17.6 %collective-permute-start.4 = (bf16[4,128,256]{2,1,0:T(8,128)(2,1)}, bf16[4,128,256]{2,1,0:T(8,128)(2,1)S(1)}, u32[]{:S(2)}, u32[]{:S(2)}) collective-permute-start(bf16[4,128,256]{2,1,0:T(8,128)(2,1)} %get-tuple-element.37.own), channel_id=1, source_target_pairs={{0,2},{1,3},{2,4},{3,5},{4,6},{5,7},{6,8},{7,9},{8,10},{9,11},{10,... | collective-permute-start | bytes 786440 | tf_op jit(solution)/shard_map/ppermute | solution.py:37
  6.2 23.3 %collective-permute-start.3 = (bf16[4,128,256]{2,1,0:T(8,128)(2,1)}, bf16[4,128,256]{2,1,0:T(8,128)(2,1)S(1)}, u32[]{:S(2)}, u32[]{:S(2)}) collective-permute-start(bf16[4,128,256]{2,1,0:T(8,128)(2,1)} %get-tuple-element.37.own), channel_id=1, source_target_pairs={{0,1},{1,2},{2,3},{3,4},{4,5},{5,6},{6,7},{7,8},{8,9},{9,10},{10,1... | collective-permute-start | bytes 786440 | tf_op jit(solution)/shard_map/ppermute | solution.py:37
  6.5 34.5 %collective-permute-start.1 = (bf16[4,128,256]{2,1,0:T(8,128)(2,1)}, bf16[4,128,256]{2,1,0:T(8,128)(2,1)S(1)}, u32[]{:S(2)}, u32[]{:S(2)}) collective-permute-start(bf16[4,128,256]{2,1,0:T(8,128)(2,1)} %get-tuple-element.31.own), channel_id=1, source_target_pairs={{0,2},{1,3},{2,4},{3,5},{4,6},{5,7},{6,8},{7,9},{8,10},{9,11},{10,... | collective-permute-start | bytes 786440 | tf_op jit(solution)/shard_map/ppermute | solution.py:37
  9.3 31.8 %collective-permute-start = (bf16[4,128,256]{2,1,0:T(8,128)(2,1)}, bf16[4,128,256]{2,1,0:T(8,128)(2,1)S(1)}, u32[]{:S(2)}, u32[]{:S(2)}) collective-permute-start(bf16[4,128,256]{2,1,0:T(8,128)(2,1)} %get-tuple-element.31.own), channel_id=1, source_target_pairs={{0,1},{1,2},{2,3},{3,4},{4,5},{5,6},{6,7},{7,8},{8,9},{9,10},{10,1... | collective-permute-start | bytes 786440 | tf_op jit(solution)/shard_map/ppermute | solution.py:37
  20.2 9.3 %copy-start = (bf16[4,128,256]{2,1,0:T(8,128)(2,1)}, bf16[4,128,256]{2,1,0:T(8,128)(2,1)S(1)}, u32[]{:S(2)}) copy-start(bf16[4,128,256]{2,1,0:T(8,128)(2,1)S(1)} %collective-permute-done.4.nb2) | copy-start | bytes 786436
  38.6 12.4 %collective-permute-start.5 = (bf16[2048,128]{1,0:T(8,128)(2,1)}, bf16[2048,128]{1,0:T(8,128)(2,1)S(1)}, u32[]{:S(2)}, u32[]{:S(2)}) collective-permute-start(bf16[2048,128]{1,0:T(8,128)(2,1)} %get-tuple-element.40), channel_id=1, source_target_pairs={{0,128},{128,0},{1,129},{129,1},{2,130},{130,2},{3,131},{131,3},{4... | collective-permute-start | bytes 1572872 | tf_op jit(solution)/shard_map/ppermute | solution.py:37
  50.9 3.6 %collective-permute-start.2 = (bf16[2048,128]{1,0:T(8,128)(2,1)}, bf16[2048,128]{1,0:T(8,128)(2,1)S(1)}, u32[]{:S(2)}, u32[]{:S(2)}) collective-permute-start(bf16[2048,128]{1,0:T(8,128)(2,1)} %get-tuple-element.35), channel_id=1, source_target_pairs={{0,128},{128,0},{1,129},{129,1},{2,130},{130,2},{3,131},{131,3},{4... | collective-permute-start | bytes 1572872 | tf_op jit(solution)/shard_map/ppermute | solution.py:37
  51.0 0.8 copy-start.2
  54.5 0.8 copy-start.3
  58.6 7.9 %collective-permute-start.6 = (f32[8,128]{1,0:T(8,128)S(1)}, f32[8,128]{1,0:T(8,128)S(1)}, u32[]{:S(2)}, u32[]{:S(2)}) collective-permute-start(f32[8,128]{1,0:T(8,128)S(1)} %add.27), channel_id=1, source_target_pairs={{0,1},{1,2},{2,3},{3,4},{4,5},{5,6},{6,7},{7,8},{8,9},{9,10},{10,1... | collective-permute-start | bytes 12296 | tf_op jit(solution)/shard_map/ppermute | solution.py:37
  66.5 8.2 %collective-permute-start.7 = (f32[8,128]{1,0:T(8,128)S(1)}, f32[8,128]{1,0:T(8,128)S(1)}, u32[]{:S(2)}, u32[]{:S(2)}) collective-permute-start(f32[8,128]{1,0:T(8,128)S(1)} %add.28), channel_id=1, source_target_pairs={{0,2},{1,3},{2,4},{3,5},{4,6},{5,7},{6,8},{7,9},{8,10},{9,11},{10,... | collective-permute-start | bytes 12296 | tf_op jit(solution)/shard_map/ppermute | solution.py:37
  74.7 5.8 %collective-permute-start.8 = (f32[8,128]{1,0:T(8,128)S(1)}, f32[8,128]{1,0:T(8,128)S(1)}, u32[]{:S(2)}, u32[]{:S(2)}) collective-permute-start(f32[8,128]{1,0:T(8,128)S(1)} %add.29), channel_id=1, source_target_pairs={{0,4},{1,5},{2,6},{3,7},{4,8},{5,9},{6,10},{7,11},{8,12},{9,13},{1... | collective-permute-start | bytes 12296 | tf_op jit(solution)/shard_map/ppermute | solution.py:37
  80.5 13.3 %collective-permute-start.9 = (f32[8,128]{1,0:T(8,128)S(1)}, f32[8,128]{1,0:T(8,128)S(1)}, u32[]{:S(2)}, u32[]{:S(2)}) collective-permute-start(f32[8,128]{1,0:T(8,128)S(1)} %add.30), channel_id=1, source_target_pairs={{0,8},{1,9},{2,10},{3,11},{4,12},{5,13},{6,14},{7,15},{8,16},{9,17... | collective-permute-start | bytes 12296 | tf_op jit(solution)/shard_map/ppermute | solution.py:37
  80.5 5.7 %copy-start.11 = (bf16[2,128,256]{2,1,0:T(8,128)(2,1)S(1)}, bf16[2,128,256]{2,1,0:T(8,128)(2,1)}, u32[]{:S(2)}) copy-start(bf16[2,128,256]{2,1,0:T(8,128)(2,1)} %get-tuple-element.51) | copy-start | bytes 393220
  80.5 13.2 %copy-start.10 = (bf16[2,128,256]{2,1,0:T(8,128)(2,1)S(1)}, bf16[2,128,256]{2,1,0:T(8,128)(2,1)}, u32[]{:S(2)}) copy-start(bf16[2,128,256]{2,1,0:T(8,128)(2,1)} %get-tuple-element.52) | copy-start | bytes 393220
  85.8 32.1 %collective-permute-start.16 = (bf16[2,128,256]{2,1,0:T(8,128)(2,1)}, bf16[2,128,256]{2,1,0:T(8,128)(2,1)S(1)}, u32[]{:S(2)}, u32[]{:S(2)}) collective-permute-start(bf16[2,128,256]{2,1,0:T(8,128)(2,1)} %get-tuple-element.54), channel_id=1, source_target_pairs={{0,127},{1,0},{2,1},{3,2},{4,3},{5,4},{6,5},{7,6},{8,7},{9,8},{10,... | collective-permute-start | bytes 393224 | tf_op jit(solution)/shard_map/ppermute | solution.py:37
  85.9 32.0 %collective-permute-start.17 = (bf16[2,128,256]{2,1,0:T(8,128)(2,1)}, bf16[2,128,256]{2,1,0:T(8,128)(2,1)S(1)}, u32[]{:S(2)}, u32[]{:S(2)}) collective-permute-start(bf16[2,128,256]{2,1,0:T(8,128)(2,1)} %get-tuple-element.55), channel_id=1, source_target_pairs={{0,126},{1,127},{2,0},{3,1},{4,2},{5,3},{6,4},{7,5},{8,6},{9,7},{1... | collective-permute-start | bytes 393224 | tf_op jit(solution)/shard_map/ppermute | solution.py:37
  86.3 31.7 %collective-permute-start.14 = (bf16[2,128,256]{2,1,0:T(8,128)(2,1)S(1)}, bf16[2,128,256]{2,1,0:T(8,128)(2,1)S(1)}, u32[]{:S(2)}, u32[]{:S(2)}) collective-permute-start(bf16[2,128,256]{2,1,0:T(8,128)(2,1)S(1)} %copy-done.11), channel_id=1, source_target_pairs={{0,127},{1,0},{2,1},{3,2},{4,3},{5,4},{6,5},{7,6},{8,7},{9,8},{10,... | collective-permute-start | bytes 393224 | tf_op jit(solution)/shard_map/ppermute | solution.py:37
  93.8 24.2 %collective-permute-start.15 = (bf16[2,128,256]{2,1,0:T(8,128)(2,1)S(1)}, bf16[2,128,256]{2,1,0:T(8,128)(2,1)S(1)}, u32[]{:S(2)}, u32[]{:S(2)}) collective-permute-start(bf16[2,128,256]{2,1,0:T(8,128)(2,1)S(1)} %copy-done.10), channel_id=1, source_target_pairs={{0,126},{1,127},{2,0},{3,1},{4,2},{5,3},{6,4},{7,5},{8,6},{9,7},{1... | collective-permute-start | bytes 393224 | tf_op jit(solution)/shard_map/ppermute | solution.py:37
  93.8 3.7 %collective-permute-start.10 = (f32[8,128]{1,0:T(8,128)S(1)}, f32[8,128]{1,0:T(8,128)S(1)}, u32[]{:S(2)}, u32[]{:S(2)}) collective-permute-start(f32[8,128]{1,0:T(8,128)S(1)} %add.31), channel_id=1, source_target_pairs={{0,16},{1,17},{2,18},{3,19},{4,20},{5,21},{6,22},{7,23},{8,24},{9,... | collective-permute-start | bytes 12296 | tf_op jit(solution)/shard_map/ppermute | solution.py:37
  97.5 4.9 %collective-permute-start.11 = (f32[8,128]{1,0:T(8,128)S(1)}, f32[8,128]{1,0:T(8,128)S(1)}, u32[]{:S(2)}, u32[]{:S(2)}) collective-permute-start(f32[8,128]{1,0:T(8,128)S(1)} %add.32), channel_id=1, source_target_pairs={{0,32},{1,33},{2,34},{3,35},{4,36},{5,37},{6,38},{7,39},{8,40},{9,... | collective-permute-start | bytes 12296 | tf_op jit(solution)/shard_map/ppermute | solution.py:37
  102.4 6.4 %collective-permute-start.12 = (f32[8,128]{1,0:T(8,128)S(1)}, f32[8,128]{1,0:T(8,128)S(1)}, u32[]{:S(2)}, u32[]{:S(2)}) collective-permute-start(f32[8,128]{1,0:T(8,128)S(1)} %add.33), channel_id=1, source_target_pairs={{0,64},{1,65},{2,66},{3,67},{4,68},{5,69},{6,70},{7,71},{8,72},{9,... | collective-permute-start | bytes 12296 | tf_op jit(solution)/shard_map/ppermute | solution.py:37
  108.8 7.9 %collective-permute-start.13 = (f32[8,128]{1,0:T(8,128)S(1)}, f32[8,128]{1,0:T(8,128)S(1)}, u32[]{:S(2)}, u32[]{:S(2)}) collective-permute-start(f32[8,128]{1,0:T(8,128)S(1)} %add.34), channel_id=1, source_target_pairs={{0,128},{128,0},{1,129},{129,1},{2,130},{130,2},{3,131},{131,3},{4... | collective-permute-start | bytes 12296 | tf_op jit(solution)/shard_map/ppermute | solution.py:37
  118.0 0.7 copy-start.9
  (6 other events, 4.1 us)

commit v2 on v1

v2 whole, which is shorter than its diff:
```python
import functools
import jax
import jax.numpy as jnp
from jax import lax
from jax.experimental import pallas as pl
from jax.experimental.pallas import tpu as pltpu
from jax.sharding import PartitionSpec as P

REACH = 2
HEADS = 32
KV_HEADS = 4
HEAD_DIM = 128
GROUP = HEADS // KV_HEADS
TOK = 128
SPAN = (REACH + 1) * TOK
SPLIT = (1, 1, 2)
PARTS = len(SPLIT)
OFFSET = tuple(sum(SPLIT[:p]) for p in range(PARTS))
PAIR = 2

NEG_FILL = -1e30
SCALE = HEAD_DIM ** (-0.5)
LOG2E = 1.4426950408889634
EXP_SCALE = SCALE * LOG2E
NT = (((1,), (1,)), ((), ()))
NN = (((1,), (0,)), ((), ()))
TN = (((0,), (0,)), ((), ()))


def mm(a, b, dims):
    return lax.dot_general(a, b, dims, preferred_element_type=jnp.float32)


def rotate(block, axis, distance):
    count = lax.axis_size(axis)
    return lax.ppermute(block, axis, [(i, (i + distance) % count) for i in range(count)])


def in_hbm(array):
    return pltpu.with_memory_space_constraint(array, pltpu.HBM)


def pack_body(pos_ref, tk, tv, sk, sv, seg0, seg1, seg2, *outs):
    packs, (bias, first_rows, first_cols) = outs[:PARTS], outs[PARTS:]
    for p in range(PARTS):
        for m, src in enumerate((tk, tv, sk, sv)):
            packs[p][m] = src[0, :, OFFSET[p] * HEAD_DIM : (OFFSET[p] + SPLIT[p]) * HEAD_DIM]
    square = lambda seg: jnp.broadcast_to(seg[0].astype(jnp.float32), (TOK, TOK))
    queries = square(seg0)
    keys0, keys1, keys2 = queries.T, square(seg1).T, square(seg2).T
    first = jnp.broadcast_to(keys0[0:1, :], (TOK, TOK))
    in_first = queries == first
    key_in_first = keys0 == first
    row = lax.broadcasted_iota(jnp.int32, (TOK, TOK), 0)
    col = lax.broadcasted_iota(jnp.int32, (TOK, TOK), 1)
    own_ok = (keys0 == queries) & (row <= col)
    near_ok = in_first & (keys1 == queries)
    far_ok = in_first & (keys2 == queries) & jnp.logical_not(key_in_first)
    bias[:TOK, :] = jnp.where(near_ok, 0.0, NEG_FILL)
    bias[TOK:, :] = jnp.where(own_ok | far_ok, 0.0, NEG_FILL)
    first_rows[...] = jnp.where(key_in_first, 1.0, 0.0)
    first_cols[...] = jnp.where(in_first, 1.0, 0.0)


def pack(pos, blocks, segment_ids):
    count = segment_ids.shape[0] // TOK
    seg = segment_ids.reshape(count, 1, TOK)
    kv = pl.BlockSpec((1, TOK, KV_HEADS * HEAD_DIM), lambda i, pos: (0, 0, 0))
    segs = [
        pl.BlockSpec((1, 1, TOK), lambda i, pos, d=d: (lax.rem(pos[0] + count - d, count), 0, 0))
        for d in range(REACH + 1)
    ]
    whole = lambda *shape: pl.BlockSpec(shape, lambda i, pos: (0,) * len(shape))
    flat = jax.ShapeDtypeStruct((TOK, TOK), jnp.float32)
    return pl.pallas_call(
        pack_body,
        grid_spec=pltpu.PrefetchScalarGridSpec(
            num_scalar_prefetch=1,
            grid=(1,),
            in_specs=[kv] * 4 + segs,
            out_specs=[whole(4, TOK, n * HEAD_DIM) for n in SPLIT] + [whole(2 * TOK, TOK)] + [whole(TOK, TOK)] * 2,
        ),
        out_shape=[jax.ShapeDtypeStruct((4, TOK, n * HEAD_DIM), jnp.bfloat16) for n in SPLIT]
        + [jax.ShapeDtypeStruct((2 * TOK, TOK), jnp.float32), flat, flat],
        name="pack",
    )(pos, *blocks, seg, seg, seg)


def window(own, nb1, nb2, rows):
    mixed = own * rows + nb2 * (1 - rows)
    upper = jnp.concatenate([nb1, jnp.zeros_like(nb1)], axis=1)
    return jnp.concatenate([upper, jnp.concatenate([mixed, own], axis=1)], axis=0)


def query_pair(q_ref, pair, rows):
    parts = []
    for j in range(PAIR):
        h = pair * PAIR + j
        q = q_ref[0, :, h * HEAD_DIM : (h + 1) * HEAD_DIM]
        early = q * rows
        parts.append(jnp.concatenate([early, q - early], axis=1))
    return jnp.concatenate(parts, axis=0)


def forward_body(stage_ref, tq, sq, own, nb1, nb2, bias, frow, fcol, s_out, t_out, send, lse):
    ahead = stage_ref[0].astype(jnp.float32) + 1.0
    rows = frow[...].astype(jnp.bfloat16)
    early = fcol[0:1, :] > 0.5
    models = []
    for base in (0, 2):
        keys = window(own[base], nb1[base], nb2[base], rows)
        v0, v1, v2 = own[base + 1], nb1[base + 1], nb2[base + 1]
        mixed = (v0 * rows + v2 * (1 - rows)).T
        values = jnp.concatenate(
            [
                jnp.concatenate([v1.T, mixed], axis=1),
                jnp.concatenate([jnp.zeros((HEAD_DIM, TOK), jnp.bfloat16), v0.T], axis=1),
            ],
            axis=0,
        )
        models.append((keys, values))
    items = [(pair, model) for pair in range(GROUP // PAIR) for model in (0, 1)]

    def score(item):
        pair, model = item
        return mm(models[model][0], query_pair((tq, sq)[model], pair, rows), NT)

    def soften(scores):
        halves, inverses, levels = [], [], []
        for j in range(PAIR):
            s = scores[:, j * TOK : (j + 1) * TOK] + bias[...]
            peak = jnp.max(s, axis=0, keepdims=True)
            expo = jnp.exp2((s - peak) * EXP_SCALE)
            total = jnp.sum(expo, axis=0, keepdims=True)
            halves.append(expo.astype(jnp.bfloat16))
            inverses.append(1.0 / total)
            levels.append(peak * EXP_SCALE + jnp.log2(total))
        return jnp.concatenate(halves, axis=1), inverses, levels

    def mix(item, weights, inverses):
        both = mm(models[item[1]][1], weights, NN)
        outs = []
        for j in range(PAIR):
            cols = slice(j * TOK, (j + 1) * TOK)
            picked = jnp.where(early, both[:HEAD_DIM, cols], both[HEAD_DIM:, cols])
            outs.append((picked * inverses[j]).astype(jnp.bfloat16))
        return outs

    ready = score(items[0])
    teacher = None
    for n, item in enumerate(items):
        following = score(items[n + 1]) if n + 1 < len(items) else None
        weights, inverses, levels = soften(ready)
        outs = mix(item, weights, inverses)
        ready = following
        if item[1] == 0:
            teacher = outs
            continue
        for j in range(PAIR):
            h = item[0] * PAIR + j
            at = pl.ds(h * HEAD_DIM, HEAD_DIM)
            s_out[at, :] = outs[j]
            t_out[at, :] = teacher[j]
            send[at, :] = (
                outs[j].astype(jnp.float32) - ahead * teacher[j].astype(jnp.float32)
            ).astype(jnp.bfloat16)
            lse[h : h + 1, :] = levels[j]


def forward(part, stage, t_query, s_query, own, nb1, nb2, masks):
    width = GROUP * HEAD_DIM
    groups = SPLIT[part]
    total = groups * width
    query = pl.BlockSpec((1, TOK, width), lambda g, st: (0, 0, OFFSET[part] + g))
    kv = pl.BlockSpec((4, TOK, HEAD_DIM), lambda g, st: (0, 0, g))
    flipped = pl.BlockSpec((width, TOK), lambda g, st: (g, 0))
    half = jax.ShapeDtypeStruct((total, TOK), jnp.bfloat16)
    fixed = [pl.BlockSpec(m.shape, lambda g, st: (0, 0)) for m in masks]
    return pl.pallas_call(
        forward_body,
        grid_spec=pltpu.PrefetchScalarGridSpec(
            num_scalar_prefetch=1,
            grid=(groups,),
            in_specs=[query, query, kv, kv, kv] + fixed,
            out_specs=[flipped] * 3 + [pl.BlockSpec((GROUP, TOK), lambda g, st: (g, 0))],
        ),
        out_shape=[half] * 3 + [jax.ShapeDtypeStruct((groups * GROUP, TOK), jnp.float32)],
        cost_estimate=pl.CostEstimate(flops=8 * total * TOK * SPAN, bytes_accessed=6 * total * TOK * 2, transcendentals=2 * total * SPAN),
        name="forward",
    )(stage, t_query, s_query, own, nb1, nb2, *masks)


def backward_body(several, chained, stage_ref, sq, own, nb1, nb2, bias, frow, fcol, s_out, t_out, recv, lse, *rest):
    dq, local, back1, back2, loss, all_query, all_grad, all_prob, all_score = rest[-9:]
    stage = stage_ref[0].astype(jnp.float32)
    rows = frow[...].astype(jnp.bfloat16)
    cols_mask = fcol[...].astype(jnp.bfloat16)
    keys = window(own[0], nb1[0], nb2[0], rows)
    values = window(own[1], nb1[1], nb2[1], rows)
    width = PAIR * TOK
    squares = [jnp.zeros((8, TOK), jnp.float32)]

    def out_grad_of(h):
        at = slice(h * HEAD_DIM, (h + 1) * HEAD_DIM)
        s = s_out[at, :].astype(jnp.float32)
        t = t_out[at, :].astype(jnp.float32)
        r = recv[at, :].astype(jnp.float32)
        grad = (2.0 - stage) * (s - t) + r
        first = r - t
        both = grad * grad + first * first
        squares[0] = squares[0] + jnp.sum(both.reshape(HEAD_DIM // 8, 8, TOK), axis=0)
        half = grad.astype(jnp.bfloat16)
        return half, jnp.sum(half.astype(jnp.float32) * s, axis=0, keepdims=True)

    def start(pair):
        at = slice(pair * width, (pair + 1) * width)
        queries = query_pair(sq, pair, rows)
        all_query[at, :] = queries
        stacked, deltas = [], []
        for j in range(PAIR):
            g, delta = out_grad_of(pair * PAIR + j)
            early = g * cols_mask
            stacked.append(jnp.concatenate([early, g - early], axis=0))
            deltas.append(delta)
        out_grad = jnp.concatenate(stacked, axis=1)
        all_grad[:, at] = out_grad
        return mm(keys, queries, NT), mm(values, out_grad, NN), deltas

    ready = start(0)
    for pair in range(GROUP // PAIR):
        scores, dprob, deltas = ready
        if pair + 1 < GROUP // PAIR:
            ready = start(pair + 1)
        for j in range(PAIR):
            h = pair * PAIR + j
            part = slice(j * TOK, (j + 1) * TOK)
            at = slice(h * TOK, (h + 1) * TOK)
            prob = jnp.exp2((scores[:, part] + bias[...]) * EXP_SCALE - lse[h : h + 1, :])
            dscore = prob * (dprob[:, part] - deltas[j])
            all_prob[:, at] = prob.astype(jnp.bfloat16)
            all_score[:, at] = dscore.astype(jnp.bfloat16)
        at = slice(pair * width, (pair + 1) * width)
        query_part = mm(all_score[:, at], keys, TN)
        for j in range(PAIR):
            h = pair * PAIR + j
            both = query_part[j * TOK : (j + 1) * TOK, :]
            picked = jnp.where(frow[...] > 0.5, both[:, :HEAD_DIM], both[:, HEAD_DIM:])
            dq[0, :, h * HEAD_DIM : (h + 1) * HEAD_DIM] = picked * SCALE
    key_win = mm(all_score[...], all_query[...], NN) * SCALE
    value_win = mm(all_prob[...], all_grad[...], NT)
    for m, win in enumerate((key_win, value_win)):
        back1[m] = win[:TOK, :HEAD_DIM].astype(jnp.bfloat16)
        mixed = win[TOK:, :HEAD_DIM]
        kept = mixed * frow[...]
        back2[m] = (mixed - kept).astype(jnp.bfloat16)
        local[m] = win[TOK:, HEAD_DIM:] + kept
    total = jnp.sum(squares[0], axis=0, keepdims=True) * stage
    step = pl.program_id(0)
    before = rest[0][0:1, :] if chained else jnp.zeros((1, TOK), jnp.float32)
    if several:
        before = jnp.where(step == 0, before, loss[0:1, :])
    loss[...] = jnp.broadcast_to(total + before, loss.shape)


def backward(part, stage, s_query, own, nb1, nb2, masks, outs, recv, lse, carried, senders):
    width = GROUP * HEAD_DIM
    groups = SPLIT[part]
    total = groups * width
    last = part == PARTS - 1
    flat = senders if last else 8
    query = pl.BlockSpec((1, TOK, width), lambda g, st: (0, 0, OFFSET[part] + g))
    kv = pl.BlockSpec((2, TOK, HEAD_DIM), lambda g, st: (1, 0, g))
    flipped = pl.BlockSpec((width, TOK), lambda g, st: (g, 0))
    fixed = lambda shape: pl.BlockSpec(shape, lambda g, st: (0,) * len(shape))
    in_specs = [query, kv, kv, kv] + [fixed(m.shape) for m in masks]
    in_specs += [flipped] * 3 + [pl.BlockSpec((GROUP, TOK), lambda g, st: (g, 0))]
    args = [stage, s_query, own, nb1, nb2, *masks, *outs, recv, lse]
    aliases = {}
    if carried is not None:
        *buffers, squares = carried
        in_specs.append(fixed(squares.shape))
        args.append(squares)
        for n, buffer in enumerate(buffers):
            aliases[len(args)] = n
            in_specs.append(pl.BlockSpec(memory_space=pl.ANY))
            args.append(buffer)
    pair = pl.BlockSpec((2, TOK, HEAD_DIM), lambda g, st: (0, 0, OFFSET[part] + g))
    wide = (2, TOK, KV_HEADS * HEAD_DIM)
    return pl.pallas_call(
        functools.partial(backward_body, groups > 1, carried is not None),
        grid_spec=pltpu.PrefetchScalarGridSpec(
            num_scalar_prefetch=1,
            grid=(groups,),
            in_specs=in_specs,
            out_specs=[query, pair, pair, pair, fixed((flat, TOK))],
            scratch_shapes=[
                pltpu.VMEM((GROUP * TOK, 2 * HEAD_DIM), jnp.bfloat16),
                pltpu.VMEM((2 * HEAD_DIM, GROUP * TOK), jnp.bfloat16),
                pltpu.VMEM((2 * TOK, GROUP * TOK), jnp.bfloat16),
                pltpu.VMEM((2 * TOK, GROUP * TOK), jnp.bfloat16),
            ],
        ),
        out_shape=[
            jax.ShapeDtypeStruct((1, TOK, HEADS * HEAD_DIM), jnp.float32),
            jax.ShapeDtypeStruct(wide, jnp.float32),
            jax.ShapeDtypeStruct(wide, jnp.bfloat16),
            jax.ShapeDtypeStruct(wide, jnp.bfloat16),
            jax.ShapeDtypeStruct((flat, TOK), jnp.float32),
        ],
        input_output_aliases=aliases,
        cost_estimate=pl.CostEstimate(flops=10 * total * TOK * SPAN, bytes_accessed=12 * total * TOK, transcendentals=total * SPAN),
        name="backward",
    )(*args)


def finish_body(local, ret1, ret2, squares, loss, key_grad, value_grad):
    for m, out in enumerate((key_grad, value_grad)):
        out[0] = local[m] + ret1[m].astype(jnp.float32) + ret2[m].astype(jnp.float32)
    count = squares.shape[0] * TOK * HEADS * HEAD_DIM
    rows = jnp.sum(squares[...], axis=0, keepdims=True)
    loss[...] = jnp.sum(rows, axis=1, keepdims=True) * (1.0 / count)


def finish(local, ret1, ret2, squares):
    shape = jax.ShapeDtypeStruct((1, TOK, KV_HEADS * HEAD_DIM), jnp.float32)
    return pl.pallas_call(
        finish_body,
        out_shape=[jax.ShapeDtypeStruct((1, 1), jnp.float32), shape, shape],
        name="finish",
    )(local, ret1, ret2, squares)


def per_device(t_query, t_key, t_value, s_query, s_key, s_value, segment_ids):
    pos = lax.axis_index("ctx").astype(jnp.int32).reshape(1)
    stage = lax.axis_index("pipe").astype(jnp.int32).reshape(1)
    senders = lax.axis_size("pipe") * lax.axis_size("ctx")
    packed = pack(pos, (t_key, t_value, s_key, s_value), segment_ids)
    packs, masks = packed[:PARTS], packed[PARTS:]
    near = []
    for block in packs:
        pair = []
        for d in (1, 2):
            pair.append(in_hbm(rotate(block, "ctx", d)))
        near.append(pair)
    carried = None
    waiting = []

    def close(carried):
        part, outs, recv, lse = waiting.pop(0)
        own, (nb1, nb2) = packs[part], near[part]
        return backward(
            part, stage, s_query, own, nb1, nb2, masks, outs, recv, lse, carried, senders
        )

    for part in range(PARTS):
        own, (nb1, nb2) = packs[part], near[part]
        mark = stage
        if carried is not None:
            mark, held = lax.optimization_barrier((stage, carried[-1]))
            carried = (*carried[:-1], held)
        s_out, t_out, send, lse = forward(part, mark, t_query, s_query, own, nb1, nb2, masks)
        waiting.append((part, (s_out, t_out), in_hbm(rotate(send, "pipe", 1)), lse))
        carried = close(carried)
    dq, local, back1, back2, squares = carried
    ret1, ret2 = in_hbm(rotate(back1, "ctx", -1)), in_hbm(rotate(back2, "ctx", -2))
    gathered = lax.all_to_all(squares, ("ctx", "pipe"), 0, 0, tiled=True)
    loss, key_grad, value_grad = finish(local, ret1, ret2, gathered)
    return (loss.reshape(()), dq, key_grad, value_grad)


def solution(mesh):
    placed = P("pipe", "ctx", None)
    return jax.shard_map(
        per_device,
        mesh=mesh,
        in_specs=(placed,) * 6 + (P(),),
        out_specs=(P(), placed, placed, placed),
        check_vma=False,
    )
```

time: 122 us -> 104 us (0.85)
  blocking collectives: 0 us -> 23.3 us
  starting transfers between devices: 29.9 us -> 8.91 us
  Pallas kernels: 36.7 us -> 27.3 us
  waiting for transfers between devices: 47 us -> 38.3 us
  between operations: 2.57 us -> 0.7 us
  other arithmetic: 1.31 us -> 0 us
    all_to_all x0 -> x1, blocking collectives: none -> 23.3 us  [per_device(): gathered = lax.all_to_all(squares, ('ctx', 'pipe'), 0, 0, tiled=True)]
    ppermute x18 -> x11, starting transfers between devices: 29.9 us -> 8.91 us  [rotate(): lax.ppermute(block, axis, [(i, (i + distance) % count) for i in range(cou...]
    ppermute x18 -> x11, waiting for transfers between devices: 47 us -> 38.3 us  [rotate(): lax.ppermute(block, axis, [(i, (i + distance) % count) for i in range(cou...]
    pallas_call x2 -> x3, Pallas kernels: 16.8 us -> 11.1 us  [forward(): pl.pallas_call(forward_body, grid_spec=pltpu.PrefetchScalarGridSpec(num_s...]
    pallas_call x5 -> x4, Pallas kernels: 17.9 us -> 14.2 us  [the longest x3 12.1 us: backward(): pl.pallas_call(functools.partial(backward_body, groups > 1, carried is no...]
    unnamed x24 -> x26, local copies, waits for them, and re-layouts: 4.4 us -> 5.43 us
  transfers between devices with their start and end apart: 18 -> 11, of which waited for: 9 -> 9; matrix products, arithmetic and copies ran while one was open for 1% -> 0% of each run, Pallas kernels for 25% -> 7%
where the time goes in v2:
time: 104 us
  waiting for transfers between devices  38.3 us (37%)
  Pallas kernels  27.3 us (26%)
  blocking collectives  23.3 us (22%)
  starting transfers between devices  8.91 us (9%)
  local copies, waits for them, and re-layouts  5.43 us (5%)
    ppermute x11, waiting for transfers between devices, rotate(): lax.ppermute(block, axis, [(i, (i + distance) % count) for i in range(cou...  38.3 us
    all_to_all x1, blocking collectives, per_device(): gathered = lax.all_to_all(squares, ('ctx', 'pipe'), 0, 0, tiled=True)  23.3 us
    pallas_call x3, Pallas kernels, backward(): pl.pallas_call(functools.partial(backward_body, groups > 1, carried is no...  12.1 us
    pallas_call x3, Pallas kernels, forward(): pl.pallas_call(forward_body, grid_spec=pltpu.PrefetchScalarGridSpec(num_s...  11.1 us
    ppermute x11, starting transfers between devices, rotate(): lax.ppermute(block, axis, [(i, (i + distance) % count) for i in range(cou...  8.91 us
    unnamed x26, local copies, waits for them, and re-layouts  5.43 us
  transfers between devices with their start and end apart: 11, of which 9 were waited for; matrix products, arithmetic and copies ran while one was open for 0% of the time, Pallas kernels for 7%

profile of v2, /device:TPU:1, one launch (start us, length us, event | category | flops | bytes accessed | tf_op | source)
XLA Modules:
  0.0 104.0 jit_solution(1276983625421827057)
XLA Ops:
  0.6 2.1 %pack.1 = (bf16[4,128,128]{2,1,0:T(8,128)(2,1)}, bf16[4,128,128]{2,1,0:T(8,128)(2,1)}, bf16[4,128,256]{2,1,0:T(8,128)(2,1)}, f32[256,128]{1,0:T(8,128)}, f32[128,128]{1,0:T(8,128)}, /*index=5*/f32[128,128]{1,0:T(8,128)}) custom-call(s32[1]{0:T(128)} %bitcast.1.pos_ref, bf16[1,128,512]{2,1,0:T(8,128)(2,1)} %tk.1, bf16[1,128,512]{2,1,0:T(8,128)(2,1)} %tv.1, ...), custom_call_target="tpu_custom_call" | custom-call | tf_op jit(solution)/shard_map/pack/pallas_call | solution.py:75
  2.7 3.6 %collective-permute-start.5 = (bf16[4,128,128]{2,1,0:T(8,128)(2,1)}, bf16[4,128,128]{2,1,0:T(8,128)(2,1)S(1)}, u32[]{:S(2)}, u32[]{:S(2)}) collective-permute-start(bf16[4,128,128]{2,1,0:T(8,128)(2,1)} %get-tuple-element.49.own), channel_id=1, source_target_pairs={{0,2},{1,3},{2,4},{3,5},{4,6},{5,7},{6,8},{7,9},{8,10},{9,11},{10,... | collective-permute-start | bytes 393224 | tf_op jit(solution)/shard_map/ppermute | solution.py:36
  6.6 10.8 %collective-permute-done.5.nb2 = bf16[4,128,128]{2,1,0:T(8,128)(2,1)S(1)} collective-permute-done((bf16[4,128,128]{2,1,0:T(8,128)(2,1)}, bf16[4,128,128]{2,1,0:T(8,128)(2,1)S(1)}, u32[]{:S(2)}, u32[]{:S(2)}) %collective-permute-start.5) | collective-permute-done | bytes 131104 | tf_op jit(solution)/shard_map/ppermute | solution.py:36
  17.5 2.6 %collective-permute-done.4.nb1 = bf16[4,128,128]{2,1,0:T(8,128)(2,1)S(1)} collective-permute-done((bf16[4,128,128]{2,1,0:T(8,128)(2,1)}, bf16[4,128,128]{2,1,0:T(8,128)(2,1)S(1)}, u32[]{:S(2)}, u32[]{:S(2)}) %collective-permute-start.4) | collective-permute-done | bytes 131104 | tf_op jit(solution)/shard_map/ppermute | solution.py:36
  20.7 3.2 %forward.3 = (bf16[1024,128]{1,0:T(8,128)(2,1)}, bf16[1024,128]{1,0:T(8,128)(2,1)}, bf16[1024,128]{1,0:T(8,128)(2,1)}, f32[8,128]{1,0:T(8,128)}) custom-call(s32[1]{0:T(128)} %bitcast.stage_ref, bf16[1,128,4096]{2,1,0:T(8,128)(2,1)} %tq.5, bf16[1,128,4096]{2,1,0:T(8,128)(2,1)} %sq.11, bf16[4,128,128]{2,1,0:T(8,128)(2,1)} %get-tuple-element.49.own, ...), custom_call_target="tpu_custom_call" | custom-call | flops 402653184 | bytes 1572864 | tf_op jit(solution)/shard_map/forward/pallas_call | solution.py:179
  23.9 1.5 %collective-permute-start.6 = (bf16[1024,128]{1,0:T(8,128)(2,1)}, bf16[1024,128]{1,0:T(8,128)(2,1)S(1)}, u32[]{:S(2)}, u32[]{:S(2)}) collective-permute-start(bf16[1024,128]{1,0:T(8,128)(2,1)} %get-tuple-element.52), channel_id=1, source_target_pairs={{0,128},{128,0},{1,129},{129,1},{2,130},{130,2},{3,131},{131,3},{4... | collective-permute-start | bytes 786440 | tf_op jit(solution)/shard_map/ppermute | solution.py:36
  25.5 1.4 %collective-permute-done.6.recv = bf16[1024,128]{1,0:T(8,128)(2,1)S(1)} collective-permute-done((bf16[1024,128]{1,0:T(8,128)(2,1)}, bf16[1024,128]{1,0:T(8,128)(2,1)S(1)}, u32[]{:S(2)}, u32[]{:S(2)}) %collective-permute-start.6) | collective-permute-done | bytes 262176 | tf_op jit(solution)/shard_map/ppermute | solution.py:36
  26.8 0.7 copy-done.12
  27.6 3.5 %backward.3 = (f32[1,128,4096]{2,1,0:T(8,128)}, f32[2,128,512]{2,1,0:T(8,128)}, bf16[2,128,512]{2,1,0:T(8,128)(2,1)}, bf16[2,128,512]{2,1,0:T(8,128)(2,1)}, f32[8,128]{1,0:T(8,128)}) custom-call(s32[1]{0:T(128)} %bitcast.stage_ref, bf16[1,128,4096]{2,1,0:T(8,128)(2,1)} %sq.11, bf16[4,128,128]{2,1,0:T(8,128)(2,1)} %get-tuple-element.49.own, ...), custom_call_target="tpu_custom_call" | custom-call | flops 503316480 | bytes 1572864 | tf_op jit(solution)/shard_map/backward/pallas_call | solution.py:289
  31.1 6.9 %collective-permute-done.3.nb2 = bf16[4,128,128]{2,1,0:T(8,128)(2,1)S(1)} collective-permute-done((bf16[4,128,128]{2,1,0:T(8,128)(2,1)S(1)}, bf16[4,128,128]{2,1,0:T(8,128)(2,1)S(1)}, u32[]{:S(2)}, u32[]{:S(2)}) %collective-permute-start.3) | collective-permute-done | bytes 131104 | tf_op jit(solution)/shard_map/ppermute | solution.py:36
  39.3 3.2 %forward.4 = (bf16[1024,128]{1,0:T(8,128)(2,1)}, bf16[1024,128]{1,0:T(8,128)(2,1)}, bf16[1024,128]{1,0:T(8,128)(2,1)}, f32[8,128]{1,0:T(8,128)}) custom-call(s32[1]{0:T(128)} %bitcast.stage_ref, bf16[1,128,4096]{2,1,0:T(8,128)(2,1)} %tq.5, bf16[1,128,4096]{2,1,0:T(8,128)(2,1)} %sq.11, bf16[4,128,128]{2,1,0:T(8,128)(2,1)} %get-tuple-element.48.own, ...), custom_call_target="tpu_custom_call" | custom-call | flops 402653184 | bytes 1572864 | tf_op jit(solution)/shard_map/forward/pallas_call | solution.py:179
  42.5 1.8 %collective-permute-start.7 = (bf16[1024,128]{1,0:T(8,128)(2,1)}, bf16[1024,128]{1,0:T(8,128)(2,1)S(1)}, u32[]{:S(2)}, u32[]{:S(2)}) collective-permute-start(bf16[1024,128]{1,0:T(8,128)(2,1)} %get-tuple-element.58), channel_id=1, source_target_pairs={{0,128},{128,0},{1,129},{129,1},{2,130},{130,2},{3,131},{131,3},{4... | collective-permute-start | bytes 786440 | tf_op jit(solution)/shard_map/ppermute | solution.py:36
  44.3 1.4 %collective-permute-done.7.recv = bf16[1024,128]{1,0:T(8,128)(2,1)S(1)} collective-permute-done((bf16[1024,128]{1,0:T(8,128)(2,1)}, bf16[1024,128]{1,0:T(8,128)(2,1)S(1)}, u32[]{:S(2)}, u32[]{:S(2)}) %collective-permute-start.7) | collective-permute-done | bytes 262176 | tf_op jit(solution)/shard_map/ppermute | solution.py:36
  45.6 0.7 copy-done.9
  46.3 3.5 %backward.4 = (f32[1,128,4096]{2,1,0:T(8,128)}, f32[2,128,512]{2,1,0:T(8,128)}, bf16[2,128,512]{2,1,0:T(8,128)(2,1)}, bf16[2,128,512]{2,1,0:T(8,128)(2,1)}, f32[8,128]{1,0:T(8,128)}) custom-call(s32[1]{0:T(128)} %bitcast.stage_ref, bf16[1,128,4096]{2,1,0:T(8,128)(2,1)} %sq.11, ...), custom_call_target="tpu_custom_call", output_to_operand_aliasing={{0}: (13, {}), {1}: (14, {}), {2}: (15, {}), {3}: (16, {})} | custom-call | flops 503316480 | bytes 1572864 | tf_op jit(solution)/shard_map/backward/pallas_call | solution.py:289
  49.8 11.8 %collective-permute-done.1.nb2 = bf16[4,128,256]{2,1,0:T(8,128)(2,1)S(1)} collective-permute-done((bf16[4,128,256]{2,1,0:T(8,128)(2,1)S(1)}, bf16[4,128,256]{2,1,0:T(8,128)(2,1)S(1)}, u32[]{:S(2)}, u32[]{:S(2)}) %collective-permute-start.1) | collective-permute-done | bytes 262176 | tf_op jit(solution)/shard_map/ppermute | solution.py:36
  61.6 1.5 %collective-permute-done.nb1 = bf16[4,128,256]{2,1,0:T(8,128)(2,1)S(1)} collective-permute-done((bf16[4,128,256]{2,1,0:T(8,128)(2,1)S(1)}, bf16[4,128,256]{2,1,0:T(8,128)(2,1)S(1)}, u32[]{:S(2)}, u32[]{:S(2)}) %collective-permute-start) | collective-permute-done | bytes 262176 | tf_op jit(solution)/shard_map/ppermute | solution.py:36
  63.8 4.7 %forward.5 = (bf16[2048,128]{1,0:T(8,128)(2,1)}, bf16[2048,128]{1,0:T(8,128)(2,1)}, bf16[2048,128]{1,0:T(8,128)(2,1)}, f32[16,128]{1,0:T(8,128)}) custom-call(s32[1]{0:T(128)} %bitcast.stage_ref, bf16[1,128,4096]{2,1,0:T(8,128)(2,1)} %tq.5, bf16[1,128,4096]{2,1,0:T(8,128)(2,1)} %sq.11, bf16[4,128,256]{2,1,0:T(8,128)(2,1)} %get-tuple-element.44.own, ...), custom_call_target="tpu_custom_call" | custom-call | flops 805306368 | bytes 3145728 | tf_op jit(solution)/shard_map/forward/pallas_call | solution.py:179
  68.4 1.5 %collective-permute-start.8 = (bf16[2048,128]{1,0:T(8,128)(2,1)}, bf16[2048,128]{1,0:T(8,128)(2,1)S(1)}, u32[]{:S(2)}, u32[]{:S(2)}) collective-permute-start(bf16[2048,128]{1,0:T(8,128)(2,1)} %get-tuple-element.69), channel_id=1, source_target_pairs={{0,128},{128,0},{1,129},{129,1},{2,130},{130,2},{3,131},{131,3},{4... | collective-permute-start | bytes 1572872 | tf_op jit(solution)/shard_map/ppermute | solution.py:36
  69.9 1.7 %collective-permute-done.8.recv = bf16[2048,128]{1,0:T(8,128)(2,1)S(1)} collective-permute-done((bf16[2048,128]{1,0:T(8,128)(2,1)}, bf16[2048,128]{1,0:T(8,128)(2,1)S(1)}, u32[]{:S(2)}, u32[]{:S(2)}) %collective-permute-start.8) | collective-permute-done | bytes 524320 | tf_op jit(solution)/shard_map/ppermute | solution.py:36
  71.7 0.8 copy-done.3
  72.5 5.1 %backward.5 = (f32[1,128,4096]{2,1,0:T(8,128)}, f32[2,128,512]{2,1,0:T(8,128)}, bf16[2,128,512]{2,1,0:T(8,128)(2,1)}, bf16[2,128,512]{2,1,0:T(8,128)(2,1)}, f32[256,128]{1,0:T(8,128)}) custom-call(s32[1]{0:T(128)} %bitcast.stage_ref, bf16[1,128,4096]{2,1,0:T(8,128)(2,1)} %sq.11, ...), custom_call_target="tpu_custom_call", output_to_operand_aliasing={{0}: (13, {}), {1}: (14, {}), {2}: (15, {}), {3}: (16, {})} | custom-call | flops 1006632960 | bytes 3145728 | tf_op jit(solution)/shard_map/backward/pallas_call | solution.py:289
  77.8 23.3 %all_to_all.11 = f32[256,1,128]{2,1,0:T(1,128)} all-to-all(f32[256,1,128]{2,1,0:T(1,128)} %bitcast.12), channel_id=1, replica_groups=mesh['pipe'=2,'ctx'=128] {'ctx','pipe'}, dimensions={0} | all-to-all | bytes 262144 | tf_op jit(solution)/shard_map/all_to_all | solution.py:366
  101.9 2.1 %finish.1 = (f32[1,1]{1,0:T(1,128)}, f32[1,128,512]{2,1,0:T(8,128)}, f32[1,128,512]{2,1,0:T(8,128)}) custom-call(f32[2,128,512]{2,1,0:T(8,128)} %get-tuple-element.76.local, bf16[2,128,512]{2,1,0:T(8,128)(2,1)} %copy-done.10, bf16[2,128,512]{2,1,0:T(8,128)(2,1)} %copy-done.11, f32[256,128]{1,0:T(8,128)} %bitcast.11), custom_call_target="tpu_custom_call" | custom-call | tf_op jit(solution)/shard_map/finish/pallas_call | solution.py:326
  (33 shorter events, 3.9 us)
Async XLA Ops:
  2.7 22.8 %copy-start.4 = (bf16[4,128,128]{2,1,0:T(8,128)(2,1)S(1)}, bf16[4,128,128]{2,1,0:T(8,128)(2,1)}, u32[]{:S(2)}) copy-start(bf16[4,128,128]{2,1,0:T(8,128)(2,1)} %get-tuple-element.48.own) | copy-start | bytes 393220
  2.7 14.8 %collective-permute-start.5 = (bf16[4,128,128]{2,1,0:T(8,128)(2,1)}, bf16[4,128,128]{2,1,0:T(8,128)(2,1)S(1)}, u32[]{:S(2)}, u32[]{:S(2)}) collective-permute-start(bf16[4,128,128]{2,1,0:T(8,128)(2,1)} %get-tuple-element.49.own), channel_id=1, source_target_pairs={{0,2},{1,3},{2,4},{3,5},{4,6},{5,7},{6,8},{7,9},{8,10},{9,11},{10,... | collective-permute-start | bytes 393224 | tf_op jit(solution)/shard_map/ppermute | solution.py:36
  6.3 13.8 %collective-permute-start.4 = (bf16[4,128,128]{2,1,0:T(8,128)(2,1)}, bf16[4,128,128]{2,1,0:T(8,128)(2,1)S(1)}, u32[]{:S(2)}, u32[]{:S(2)}) collective-permute-start(bf16[4,128,128]{2,1,0:T(8,128)(2,1)} %get-tuple-element.49.own), channel_id=1, source_target_pairs={{0,1},{1,2},{2,3},{3,4},{4,5},{5,6},{6,7},{7,8},{8,9},{9,10},{10,1... | collective-permute-start | bytes 393224 | tf_op jit(solution)/shard_map/ppermute | solution.py:36
  17.5 2.6 %copy-start.7 = (bf16[4,128,128]{2,1,0:T(8,128)(2,1)}, bf16[4,128,128]{2,1,0:T(8,128)(2,1)S(1)}, u32[]{:S(2)}) copy-start(bf16[4,128,128]{2,1,0:T(8,128)(2,1)S(1)} %collective-permute-done.5.nb2) | copy-start | bytes 393220
  20.1 0.6 copy-start.8
  23.9 2.9 %collective-permute-start.6 = (bf16[1024,128]{1,0:T(8,128)(2,1)}, bf16[1024,128]{1,0:T(8,128)(2,1)S(1)}, u32[]{:S(2)}, u32[]{:S(2)}) collective-permute-start(bf16[1024,128]{1,0:T(8,128)(2,1)} %get-tuple-element.52), channel_id=1, source_target_pairs={{0,128},{128,0},{1,129},{129,1},{2,130},{130,2},{3,131},{131,3},{4... | collective-permute-start | bytes 786440 | tf_op jit(solution)/shard_map/ppermute | solution.py:36
  25.5 12.5 %collective-permute-start.3 = (bf16[4,128,128]{2,1,0:T(8,128)(2,1)S(1)}, bf16[4,128,128]{2,1,0:T(8,128)(2,1)S(1)}, u32[]{:S(2)}, u32[]{:S(2)}) collective-permute-start(bf16[4,128,128]{2,1,0:T(8,128)(2,1)S(1)} %copy-done.4), channel_id=1, source_target_pairs={{0,2},{1,3},{2,4},{3,5},{4,6},{5,7},{6,8},{7,9},{8,10},{9,11},{10,... | collective-permute-start | bytes 393224 | tf_op jit(solution)/shard_map/ppermute | solution.py:36
  25.5 12.7 %collective-permute-start.2 = (bf16[4,128,128]{2,1,0:T(8,128)(2,1)S(1)}, bf16[4,128,128]{2,1,0:T(8,128)(2,1)S(1)}, u32[]{:S(2)}, u32[]{:S(2)}) collective-permute-start(bf16[4,128,128]{2,1,0:T(8,128)(2,1)S(1)} %copy-done.4), channel_id=1, source_target_pairs={{0,1},{1,2},{2,3},{3,4},{4,5},{5,6},{6,7},{7,8},{8,9},{9,10},{10,1... | collective-permute-start | bytes 393224 | tf_op jit(solution)/shard_map/ppermute | solution.py:36
  26.8 0.7 copy-start.12
  27.6 16.7 %copy-start = (bf16[4,128,256]{2,1,0:T(8,128)(2,1)S(1)}, bf16[4,128,256]{2,1,0:T(8,128)(2,1)}, u32[]{:S(2)}) copy-start(bf16[4,128,256]{2,1,0:T(8,128)(2,1)} %get-tuple-element.44.own) | copy-start | bytes 786436
  38.0 0.6 copy-start.5
  38.6 0.6 copy-start.6
  42.5 3.1 %collective-permute-start.7 = (bf16[1024,128]{1,0:T(8,128)(2,1)}, bf16[1024,128]{1,0:T(8,128)(2,1)S(1)}, u32[]{:S(2)}, u32[]{:S(2)}) collective-permute-start(bf16[1024,128]{1,0:T(8,128)(2,1)} %get-tuple-element.58), channel_id=1, source_target_pairs={{0,128},{128,0},{1,129},{129,1},{2,130},{130,2},{3,131},{131,3},{4... | collective-permute-start | bytes 786440 | tf_op jit(solution)/shard_map/ppermute | solution.py:36
  44.2 17.3 %collective-permute-start.1 = (bf16[4,128,256]{2,1,0:T(8,128)(2,1)S(1)}, bf16[4,128,256]{2,1,0:T(8,128)(2,1)S(1)}, u32[]{:S(2)}, u32[]{:S(2)}) collective-permute-start(bf16[4,128,256]{2,1,0:T(8,128)(2,1)S(1)} %copy-done), channel_id=1, source_target_pairs={{0,2},{1,3},{2,4},{3,5},{4,6},{5,7},{6,8},{7,9},{8,10},{9,11},{10,... | collective-permute-start | bytes 786440 | tf_op jit(solution)/shard_map/ppermute | solution.py:36
  44.2 18.8 %collective-permute-start = (bf16[4,128,256]{2,1,0:T(8,128)(2,1)S(1)}, bf16[4,128,256]{2,1,0:T(8,128)(2,1)S(1)}, u32[]{:S(2)}, u32[]{:S(2)}) collective-permute-start(bf16[4,128,256]{2,1,0:T(8,128)(2,1)S(1)} %copy-done), channel_id=1, source_target_pairs={{0,1},{1,2},{2,3},{3,4},{4,5},{5,6},{6,7},{7,8},{8,9},{9,10},{10,1... | collective-permute-start | bytes 786440 | tf_op jit(solution)/shard_map/ppermute | solution.py:36
  45.6 0.7 copy-start.9
  61.6 1.5 %copy-start.1 = (bf16[4,128,256]{2,1,0:T(8,128)(2,1)}, bf16[4,128,256]{2,1,0:T(8,128)(2,1)S(1)}, u32[]{:S(2)}) copy-start(bf16[4,128,256]{2,1,0:T(8,128)(2,1)S(1)} %collective-permute-done.1.nb2) | copy-start | bytes 786436
  63.1 0.7 copy-start.2
  68.4 3.2 %collective-permute-start.8 = (bf16[2048,128]{1,0:T(8,128)(2,1)}, bf16[2048,128]{1,0:T(8,128)(2,1)S(1)}, u32[]{:S(2)}, u32[]{:S(2)}) collective-permute-start(bf16[2048,128]{1,0:T(8,128)(2,1)} %get-tuple-element.69), channel_id=1, source_target_pairs={{0,128},{128,0},{1,129},{129,1},{2,130},{130,2},{3,131},{131,3},{4... | collective-permute-start | bytes 1572872 | tf_op jit(solution)/shard_map/ppermute | solution.py:36
  71.7 0.8 copy-start.3
  77.6 23.5 %collective-permute-start.9 = (bf16[2,128,512]{2,1,0:T(8,128)(2,1)}, bf16[2,128,512]{2,1,0:T(8,128)(2,1)S(1)}, u32[]{:S(2)}, u32[]{:S(2)}) collective-permute-start(bf16[2,128,512]{2,1,0:T(8,128)(2,1)} %get-tuple-element.77), channel_id=1, source_target_pairs={{0,127},{1,0},{2,1},{3,2},{4,3},{5,4},{6,5},{7,6},{8,7},{9,8},{10,... | collective-permute-start | bytes 786440 | tf_op jit(solution)/shard_map/ppermute | solution.py:36
  77.7 23.4 %collective-permute-start.10 = (bf16[2,128,512]{2,1,0:T(8,128)(2,1)}, bf16[2,128,512]{2,1,0:T(8,128)(2,1)S(1)}, u32[]{:S(2)}, u32[]{:S(2)}) collective-permute-start(bf16[2,128,512]{2,1,0:T(8,128)(2,1)} %get-tuple-element.78), channel_id=1, source_target_pairs={{0,126},{1,127},{2,0},{3,1},{4,2},{5,3},{6,4},{7,5},{8,6},{9,7},{1... | collective-permute-start | bytes 786440 | tf_op jit(solution)/shard_map/ppermute | solution.py:36
  101.1 0.7 copy-start.10
  101.1 0.8 copy-start.11

commit v3 on v2

--- a/solution.py
+++ b/solution.py
@@ -17,6 +17,9 @@
 PARTS = len(SPLIT)
 OFFSET = tuple(sum(SPLIT[:p]) for p in range(PARTS))
 PAIR = 2
+VMEM_LIMIT = 16 << 20
+X_CHIPS = 4
+RELAYED = (2,)
 
 NEG_FILL = -1e30
 SCALE = HEAD_DIM ** (-0.5)
@@ -82,8 +85,9 @@
         ),
         out_shape=[jax.ShapeDtypeStruct((4, TOK, n * HEAD_DIM), jnp.bfloat16) for n in SPLIT]
         + [jax.ShapeDtypeStruct((2 * TOK, TOK), jnp.float32), flat, flat],
+        compiler_params=pltpu.CompilerParams(vmem_limit_bytes=VMEM_LIMIT),
         name="pack",
-    )(pos, *blocks, seg, seg, seg)
+    )(pos, *[in_hbm(b) for b in blocks], *[in_hbm(seg)] * 3)
 
 
 def window(own, nb1, nb2, rows):
@@ -186,8 +190,9 @@
         ),
         out_shape=[half] * 3 + [jax.ShapeDtypeStruct((groups * GROUP, TOK), jnp.float32)],
         cost_estimate=pl.CostEstimate(flops=8 * total * TOK * SPAN, bytes_accessed=6 * total * TOK * 2, transcendentals=2 * total * SPAN),
+        compiler_params=pltpu.CompilerParams(vmem_limit_bytes=VMEM_LIMIT),
         name="forward",
-    )(stage, t_query, s_query, own, nb1, nb2, *masks)
+    )(stage, in_hbm(t_query), in_hbm(s_query), own, nb1, nb2, *masks)
 
 
 def backward_body(several, chained, stage_ref, sq, own, nb1, nb2, bias, frow, fcol, s_out, t_out, recv, lse, *rest):
@@ -274,7 +279,7 @@
     fixed = lambda shape: pl.BlockSpec(shape, lambda g, st: (0,) * len(shape))
     in_specs = [query, kv, kv, kv] + [fixed(m.shape) for m in masks]
     in_specs += [flipped] * 3 + [pl.BlockSpec((GROUP, TOK), lambda g, st: (g, 0))]
-    args = [stage, s_query, own, nb1, nb2, *masks, *outs, recv, lse]
+    args = [stage, in_hbm(s_query), own, nb1, nb2, *masks, *outs, recv, lse]
     aliases = {}
     if carried is not None:
         *buffers, squares = carried
@@ -309,6 +314,7 @@
         ],
         input_output_aliases=aliases,
         cost_estimate=pl.CostEstimate(flops=10 * total * TOK * SPAN, bytes_accessed=12 * total * TOK, transcendentals=total * SPAN),
+        compiler_params=pltpu.CompilerParams(vmem_limit_bytes=VMEM_LIMIT),
         name="backward",
     )(*args)
 
@@ -326,8 +332,18 @@
     return pl.pallas_call(
         finish_body,
         out_shape=[jax.ShapeDtypeStruct((1, 1), jnp.float32), shape, shape],
+        compiler_params=pltpu.CompilerParams(vmem_limit_bytes=VMEM_LIMIT),
         name="finish",
     )(local, ret1, ret2, squares)
+
+
+def relay_routes(count):
+    first, second = [], []
+    for i in range(count):
+        x = i % X_CHIPS
+        first.append((i, i - 1 if x else i + X_CHIPS - 1))
+        second.append((i, i - 1 if x == X_CHIPS - 1 else (i + X_CHIPS - 1) % count))
+    return first, second
 
 
 def per_device(t_query, t_key, t_value, s_query, s_key, s_value, segment_ids):
@@ -337,11 +353,15 @@
     packed = pack(pos, (t_key, t_value, s_key, s_value), segment_ids)
     packs, masks = packed[:PARTS], packed[PARTS:]
     near = []
-    for block in packs:
-        pair = []
-        for d in (1, 2):
-            pair.append(in_hbm(rotate(block, "ctx", d)))
-        near.append(pair)
+    for part, block in enumerate(packs):
+        nb1 = rotate(block, "ctx", 1)
+        if part in RELAYED:
+            first, second = relay_routes(lax.axis_size("ctx"))
+            nb2 = lax.ppermute(block, "ctx", first)
+            nb2 = lax.ppermute(nb2, "ctx", second)
+        else:
+            nb2 = rotate(block, "ctx", 2)
+        near.append((nb1, nb2))
     carried = None
     waiting = []
 
@@ -359,10 +379,10 @@
             mark, held = lax.optimization_barrier((stage, carried[-1]))
             carried = (*carried[:-1], held)
         s_out, t_out, send, lse = forward(part, mark, t_query, s_query, own, nb1, nb2, masks)
-        waiting.append((part, (s_out, t_out), in_hbm(rotate(send, "pipe", 1)), lse))
+        waiting.append((part, (s_out, t_out), (rotate(send, "pipe", 1)), lse))
         carried = close(carried)
     dq, local, back1, back2, squares = carried
-    ret1, ret2 = in_hbm(rotate(back1, "ctx", -1)), in_hbm(rotate(back2, "ctx", -2))
+    ret1, ret2 = (rotate(back1, "ctx", -1)), (rotate(back2, "ctx", -2))
     gathered = lax.all_to_all(squares, ("ctx", "pipe"), 0, 0, tiled=True)
     loss, key_grad, value_grad = finish(local, ret1, ret2, gathered)
     return (loss.reshape(()), dq, key_grad, value_grad)

time: 104 us -> 93.3 us (0.90)
  Pallas kernels: 27.3 us -> 20.1 us
  local copies, waits for them, and re-layouts: 5.43 us -> 0 us
    unnamed x26 -> x0, local copies, waits for them, and re-layouts: 5.43 us -> none
    pallas_call x3, Pallas kernels: 11.1 us -> 7.79 us  [forward(): pl.pallas_call(forward_body, grid_spec=pltpu.PrefetchScalarGridSpec(num_s...]
    pallas_call x3, Pallas kernels: 12.1 us -> 10.2 us  [backward(): pl.pallas_call(functools.partial(backward_body, groups > 1, carried is no...]
    pallas_call x1, Pallas kernels: 2.05 us -> 0.86 us  [finish(): pl.pallas_call(finish_body, out_shape=[jax.ShapeDtypeStruct((1, 1), jnp.f...]
    ppermute x11 -> x10, starting transfers between devices: 8.91 us -> 9.94 us  [rotate(): lax.ppermute(block, axis, [(i, (i + distance) % count) for i in range(cou...]
    ppermute x11 -> x10, waiting for transfers between devices: 38.3 us -> 38.7 us  [rotate(): lax.ppermute(block, axis, [(i, (i + distance) % count) for i in range(cou...]
  transfers between devices with their start and end apart: 11 -> 12, of which waited for: 9 -> 7; matrix products, arithmetic and copies ran while one was open for 0% -> 0% of each run, Pallas kernels for 7% -> 9%
where the time goes in v3:
time: 93.3 us; the launch traced here: 93.1 us
  waiting for transfers between devices  38.7 us (41%)
  blocking collectives  23.6 us (25%)
  Pallas kernels  20.1 us (22%)
  starting transfers between devices  9.95 us (11%)
    ppermute x10, waiting for transfers between devices, rotate(): lax.ppermute(block, axis, [(i, (i + distance) % count) for i in range(cou...  38.7 us
    all_to_all x1, blocking collectives, per_device(): gathered = lax.all_to_all(squares, ('ctx', 'pipe'), 0, 0, tiled=True)  23.6 us
    pallas_call x3, Pallas kernels, backward(): pl.pallas_call(functools.partial(backward_body, groups > 1, carried is no...  10.2 us
    ppermute x10, starting transfers between devices, rotate(): lax.ppermute(block, axis, [(i, (i + distance) % count) for i in range(cou...  9.94 us
    pallas_call x3, Pallas kernels, forward(): pl.pallas_call(forward_body, grid_spec=pltpu.PrefetchScalarGridSpec(num_s...  7.79 us
  transfers between devices with their start and end apart: 12, of which 7 were waited for; matrix products, arithmetic and copies ran while one was open for 0% of the time, Pallas kernels for 9%

profile of v3, /device:TPU:1, one launch (start us, length us, event | category | flops | bytes accessed | tf_op | source)
XLA Modules:
  0.0 93.1 jit_solution(11721186329144366980)
XLA Ops:
  0.6 1.3 %pack.1 = (bf16[4,128,128]{2,1,0:T(8,128)(2,1)S(1)}, bf16[4,128,128]{2,1,0:T(8,128)(2,1)S(1)}, bf16[4,128,256]{2,1,0:T(8,128)(2,1)S(1)}, f32[256,128]{1,0:T(8,12...) custom-call(s32[1]{0:T(128)} %bitcast.1.pos_ref, bf16[1,128,512]{2,1,0:T(8,128)(2,1)} %tk.1, ...), custom_call_target="tpu_custom_call" | custom-call | tf_op jit(solution)/shard_map/pack/pallas_call | solution.py:78
  2.0 3.6 %collective-permute-start.6 = (bf16[4,128,128]{2,1,0:T(8,128)(2,1)S(1)}, bf16[4,128,128]{2,1,0:T(8,128)(2,1)S(1)}, u32[]{:S(2)}, u32[]{:S(2)}) collective-permute-start(bf16[4,128,128]{2,1,0:T(8,128)(2,1)S(1)} %get-tuple-element.49.own), channel_id=1, source_target_pairs={{0,2},{1,3},{2,4},{3,5},{4,6},{5,7},{6,8},{7,9},{8,10},{9,11},{10,... | collective-permute-start | bytes 393224 | tf_op jit(solution)/shard_map/ppermute | solution.py:39
  5.6 0.3 collective-permute-start.5
  5.9 10.6 %collective-permute-done.6.nb2 = bf16[4,128,128]{2,1,0:T(8,128)(2,1)S(1)} collective-permute-done((bf16[4,128,128]{2,1,0:T(8,128)(2,1)S(1)}, bf16[4,128,128]{2,1,0:T(8,128)(2,1)S(1)}, u32[]{:S(2)}, u32[]{:S(2)}) %collective-permute-start.6) | collective-permute-done | bytes 131104 | tf_op jit(solution)/shard_map/ppermute | solution.py:39
  16.5 2.6 %collective-permute-done.5.nb1 = bf16[4,128,128]{2,1,0:T(8,128)(2,1)S(1)} collective-permute-done((bf16[4,128,128]{2,1,0:T(8,128)(2,1)S(1)}, bf16[4,128,128]{2,1,0:T(8,128)(2,1)S(1)}, u32[]{:S(2)}, u32[]{:S(2)}) %collective-permute-start.5) | collective-permute-done | bytes 131104 | tf_op jit(solution)/shard_map/ppermute | solution.py:39
  19.2 2.2 %forward.3 = (bf16[1024,128]{1,0:T(8,128)(2,1)S(1)}, bf16[1024,128]{1,0:T(8,128)(2,1)S(1)}, bf16[1024,128]{1,0:T(8,128)(2,1)S(1)}, f32[8,128]{1,0:T(8,128)S(1)}) custom-call(s32[1]{0:T(128)} %bitcast.stage_ref, bf16[1,128,4096]{2,1,0:T(8,128)(2,1)} %tq.5, bf16[1,128,4096]{2,1,0:T(8,128)(2,1)} %sq.11, bf16[4,128,128]{2,1,0:T(8,128)(2,1)S(1)} %get-tuple-element.49.own, ...), custom_call_target="tpu_custom_call" | custom-call | flops 402653184 | bytes 1572864 | tf_op jit(solution)/shard_map/forward/pallas_call | solution.py:183
  21.4 1.6 %collective-permute-start.7 = (bf16[1024,128]{1,0:T(8,128)(2,1)S(1)}, bf16[1024,128]{1,0:T(8,128)(2,1)S(1)}, u32[]{:S(2)}, u32[]{:S(2)}) collective-permute-start(bf16[1024,128]{1,0:T(8,128)(2,1)S(1)} %get-tuple-element.52), channel_id=1, source_target_pairs={{0,128},{128,0},{1,129},{129,1},{2,130},{130,2},{3,131},{131,3},{4... | collective-permute-start | bytes 786440 | tf_op jit(solution)/shard_map/ppermute | solution.py:39
  23.0 0.0 collective-permute-start.4
  23.0 1.4 %collective-permute-start.3 = (bf16[4,128,128]{2,1,0:T(8,128)(2,1)S(1)}, bf16[4,128,128]{2,1,0:T(8,128)(2,1)S(1)}, u32[]{:S(2)}, u32[]{:S(2)}) collective-permute-start(bf16[4,128,128]{2,1,0:T(8,128)(2,1)S(1)} %get-tuple-element.48.own), channel_id=1, source_target_pairs={{0,1},{1,2},{2,3},{3,4},{4,5},{5,6},{6,7},{7,8},{8,9},{9,10},{10,1... | collective-permute-start | bytes 393224 | tf_op jit(solution)/shard_map/ppermute | solution.py:39
  24.5 2.9 %backward.3 = (f32[1,128,4096]{2,1,0:T(8,128)}, f32[2,128,512]{2,1,0:T(8,128)S(1)}, bf16[2,128,512]{2,1,0:T(8,128)(2,1)S(1)}, bf16[2,128,512]{2,1,0:T(8,128)(2,1)S(1)}, f32[8,128]{1,0:T(8,128)S(1)}) custom-call(s32[1]{0:T(128)} %bitcast.stage_ref, bf16[1,128,4096]{2,1,0:T(8,128)(2,1)} %sq.11, bf16[4,128,128]{2,1,0:T(8,128)(2,1)S(1)} %get-tuple-element.49.own, ...), custom_call_target="tpu_custom_call" | custom-call | flops 503316480 | bytes 1572864 | tf_op jit(solution)/shard_map/backward/pallas_call | solution.py:294
  27.3 6.2 %collective-permute-done.4.nb2 = bf16[4,128,128]{2,1,0:T(8,128)(2,1)S(1)} collective-permute-done((bf16[4,128,128]{2,1,0:T(8,128)(2,1)S(1)}, bf16[4,128,128]{2,1,0:T(8,128)(2,1)S(1)}, u32[]{:S(2)}, u32[]{:S(2)}) %collective-permute-start.4) | collective-permute-done | bytes 131104 | tf_op jit(solution)/shard_map/ppermute | solution.py:39
  33.6 3.5 %collective-permute-done.3.nb1 = bf16[4,128,128]{2,1,0:T(8,128)(2,1)S(1)} collective-permute-done((bf16[4,128,128]{2,1,0:T(8,128)(2,1)S(1)}, bf16[4,128,128]{2,1,0:T(8,128)(2,1)S(1)}, u32[]{:S(2)}, u32[]{:S(2)}) %collective-permute-start.3) | collective-permute-done | bytes 131104 | tf_op jit(solution)/shard_map/ppermute | solution.py:39
  37.1 2.2 %forward.4 = (bf16[1024,128]{1,0:T(8,128)(2,1)S(1)}, bf16[1024,128]{1,0:T(8,128)(2,1)S(1)}, bf16[1024,128]{1,0:T(8,128)(2,1)S(1)}, f32[8,128]{1,0:T(8,128)S(1)}) custom-call(s32[1]{0:T(128)} %bitcast.stage_ref, bf16[1,128,4096]{2,1,0:T(8,128)(2,1)} %tq.5, bf16[1,128,4096]{2,1,0:T(8,128)(2,1)} %sq.11, bf16[4,128,128]{2,1,0:T(8,128)(2,1)S(1)} %get-tuple-element.48.own, ...), custom_call_target="tpu_custom_call" | custom-call | flops 402653184 | bytes 1572864 | tf_op jit(solution)/shard_map/forward/pallas_call | solution.py:183
  39.3 1.3 %collective-permute-start.8 = (bf16[1024,128]{1,0:T(8,128)(2,1)S(1)}, bf16[1024,128]{1,0:T(8,128)(2,1)S(1)}, u32[]{:S(2)}, u32[]{:S(2)}) collective-permute-start(bf16[1024,128]{1,0:T(8,128)(2,1)S(1)} %get-tuple-element.58), channel_id=1, source_target_pairs={{0,128},{128,0},{1,129},{129,1},{2,130},{130,2},{3,131},{131,3},{4... | collective-permute-start | bytes 786440 | tf_op jit(solution)/shard_map/ppermute | solution.py:39
  40.6 0.0 collective-permute-start.2
  40.6 1.1 %collective-permute-done.8.recv = bf16[1024,128]{1,0:T(8,128)(2,1)S(1)} collective-permute-done((bf16[1024,128]{1,0:T(8,128)(2,1)S(1)}, bf16[1024,128]{1,0:T(8,128)(2,1)S(1)}, u32[]{:S(2)}, u32[]{:S(2)}) %collective-permute-start.8) | collective-permute-done | bytes 262176 | tf_op jit(solution)/shard_map/ppermute | solution.py:39
  41.8 2.9 %backward.4 = (f32[1,128,4096]{2,1,0:T(8,128)}, f32[2,128,512]{2,1,0:T(8,128)S(1)}, bf16[2,128,512]{2,1,0:T(8,128)(2,1)S(1)}, bf16[2,128,512]{2,1,0:T(8,128)(2,1)S(1)}, f32[8,128]{1,0:T(8,128)S(1)}) custom-call(s32[1]{0:T(128)} %bitcast.stage_ref, ...), custom_call_target="tpu_custom_call", output_to_operand_aliasing={{0}: (13, {}), {1}: (14, {}), {2}: (15, {}), {3}: (16, {})} | custom-call | flops 503316480 | bytes 1572864 | tf_op jit(solution)/shard_map/backward/pallas_call | solution.py:294
  44.7 13.0 %collective-permute-done.nb1 = bf16[4,128,256]{2,1,0:T(8,128)(2,1)S(1)} collective-permute-done((bf16[4,128,256]{2,1,0:T(8,128)(2,1)S(1)}, bf16[4,128,256]{2,1,0:T(8,128)(2,1)S(1)}, u32[]{:S(2)}, u32[]{:S(2)}) %collective-permute-start) | collective-permute-done | bytes 262176 | tf_op jit(solution)/shard_map/ppermute | solution.py:39
  57.7 3.4 %forward.5 = (bf16[2048,128]{1,0:T(8,128)(2,1)S(1)}, bf16[2048,128]{1,0:T(8,128)(2,1)S(1)}, bf16[2048,128]{1,0:T(8,128)(2,1)S(1)}, f32[16,128]{1,0:T(8,128)S(1)}) custom-call(s32[1]{0:T(128)} %bitcast.stage_ref, bf16[1,128,4096]{2,1,0:T(8,128)(2,1)} %tq.5, bf16[1,128,4096]{2,1,0:T(8,128)(2,1)} %sq.11, bf16[4,128,256]{2,1,0:T(8,128)(2,1)S(1)} %get-tuple-element.44.own, ...), custom_call_target="tpu_custom_call" | custom-call | flops 805306368 | bytes 3145728 | tf_op jit(solution)/shard_map/forward/pallas_call | solution.py:183
  61.1 1.6 %collective-permute-start.9 = (bf16[2048,128]{1,0:T(8,128)(2,1)S(1)}, bf16[2048,128]{1,0:T(8,128)(2,1)S(1)}, u32[]{:S(2)}, u32[]{:S(2)}) collective-permute-start(bf16[2048,128]{1,0:T(8,128)(2,1)S(1)} %get-tuple-element.69), channel_id=1, source_target_pairs={{0,128},{128,0},{1,129},{129,1},{2,130},{130,2},{3,131},{131,3},{4... | collective-permute-start | bytes 1572872 | tf_op jit(solution)/shard_map/ppermute | solution.py:39
  62.7 1.5 %collective-permute-done.9.recv = bf16[2048,128]{1,0:T(8,128)(2,1)S(1)} collective-permute-done((bf16[2048,128]{1,0:T(8,128)(2,1)S(1)}, bf16[2048,128]{1,0:T(8,128)(2,1)S(1)}, u32[]{:S(2)}, u32[]{:S(2)}) %collective-permute-start.9) | collective-permute-done | bytes 524320 | tf_op jit(solution)/shard_map/ppermute | solution.py:39
  64.2 4.4 %backward.5 = (f32[1,128,4096]{2,1,0:T(8,128)}, f32[2,128,512]{2,1,0:T(8,128)S(1)}, bf16[2,128,512]{2,1,0:T(8,128)(2,1)S(1)}, bf16[2,128,512]{2,1,0:T(8,128)(2,1)S(1)}, f32[256,128]{1,0:T(8,128)S(1)}) custom-call(s32[1]{0:T(128)} %bitcast.stage_ref, ...), custom_call_target="tpu_custom_call", output_to_operand_aliasing={{0}: (13, {}), {1}: (14, {}), {2}: (15, {}), {3}: (16, {})} | custom-call | flops 1006632960 | bytes 3145728 | tf_op jit(solution)/shard_map/backward/pallas_call | solution.py:294
  68.6 23.6 %all_to_all.11 = f32[256,1,128]{2,1,0:T(1,128)S(1)} all-to-all(f32[256,1,128]{2,1,0:T(1,128)S(1)} %bitcast.9), channel_id=1, replica_groups=mesh['pipe'=2,'ctx'=128] {'ctx','pipe'}, dimensions={0} | all-to-all | bytes 262144 | tf_op jit(solution)/shard_map/all_to_all | solution.py:386
  92.2 0.9 finish.1
  (9 shorter events, 0.0 us)
Async XLA Ops:
  2.0 14.6 %collective-permute-start.6 = (bf16[4,128,128]{2,1,0:T(8,128)(2,1)S(1)}, bf16[4,128,128]{2,1,0:T(8,128)(2,1)S(1)}, u32[]{:S(2)}, u32[]{:S(2)}) collective-permute-start(bf16[4,128,128]{2,1,0:T(8,128)(2,1)S(1)} %get-tuple-element.49.own), channel_id=1, source_target_pairs={{0,2},{1,3},{2,4},{3,5},{4,6},{5,7},{6,8},{7,9},{8,10},{9,11},{10,... | collective-permute-start | bytes 393224 | tf_op jit(solution)/shard_map/ppermute | solution.py:39
  5.6 13.6 %collective-permute-start.5 = (bf16[4,128,128]{2,1,0:T(8,128)(2,1)S(1)}, bf16[4,128,128]{2,1,0:T(8,128)(2,1)S(1)}, u32[]{:S(2)}, u32[]{:S(2)}) collective-permute-start(bf16[4,128,128]{2,1,0:T(8,128)(2,1)S(1)} %get-tuple-element.49.own), channel_id=1, source_target_pairs={{0,1},{1,2},{2,3},{3,4},{4,5},{5,6},{6,7},{7,8},{8,9},{9,10},{10,1... | collective-permute-start | bytes 393224 | tf_op jit(solution)/shard_map/ppermute | solution.py:39
  21.4 3.1 %collective-permute-start.7 = (bf16[1024,128]{1,0:T(8,128)(2,1)S(1)}, bf16[1024,128]{1,0:T(8,128)(2,1)S(1)}, u32[]{:S(2)}, u32[]{:S(2)}) collective-permute-start(bf16[1024,128]{1,0:T(8,128)(2,1)S(1)} %get-tuple-element.52), channel_id=1, source_target_pairs={{0,128},{128,0},{1,129},{129,1},{2,130},{130,2},{3,131},{131,3},{4... | collective-permute-start | bytes 786440 | tf_op jit(solution)/shard_map/ppermute | solution.py:39
  23.0 17.6 %collective-permute-start.1 = (bf16[4,128,256]{2,1,0:T(8,128)(2,1)S(1)}, bf16[4,128,256]{2,1,0:T(8,128)(2,1)S(1)}, u32[]{:S(2)}, u32[]{:S(2)}) collective-permute-start(bf16[4,128,256]{2,1,0:T(8,128)(2,1)S(1)} %get-tuple-element.44.own), channel_id=1, source_target_pairs={{0,3},{1,0},{2,1},{3,2},{4,7},{5,4},{6,5},{7,6},{8,11},{9,8},{10,9... | collective-permute-start | bytes 786440 | tf_op jit(solution)/shard_map/ppermute | solution.py:360
  23.0 10.6 %collective-permute-start.4 = (bf16[4,128,128]{2,1,0:T(8,128)(2,1)S(1)}, bf16[4,128,128]{2,1,0:T(8,128)(2,1)S(1)}, u32[]{:S(2)}, u32[]{:S(2)}) collective-permute-start(bf16[4,128,128]{2,1,0:T(8,128)(2,1)S(1)} %get-tuple-element.48.own), channel_id=1, source_target_pairs={{0,2},{1,3},{2,4},{3,5},{4,6},{5,7},{6,8},{7,9},{8,10},{9,11},{10,... | collective-permute-start | bytes 393224 | tf_op jit(solution)/shard_map/ppermute | solution.py:39
  23.0 14.1 %collective-permute-start.3 = (bf16[4,128,128]{2,1,0:T(8,128)(2,1)S(1)}, bf16[4,128,128]{2,1,0:T(8,128)(2,1)S(1)}, u32[]{:S(2)}, u32[]{:S(2)}) collective-permute-start(bf16[4,128,128]{2,1,0:T(8,128)(2,1)S(1)} %get-tuple-element.48.own), channel_id=1, source_target_pairs={{0,1},{1,2},{2,3},{3,4},{4,5},{5,6},{6,7},{7,8},{8,9},{9,10},{10,1... | collective-permute-start | bytes 393224 | tf_op jit(solution)/shard_map/ppermute | solution.py:39
  39.3 2.5 %collective-permute-start.8 = (bf16[1024,128]{1,0:T(8,128)(2,1)S(1)}, bf16[1024,128]{1,0:T(8,128)(2,1)S(1)}, u32[]{:S(2)}, u32[]{:S(2)}) collective-permute-start(bf16[1024,128]{1,0:T(8,128)(2,1)S(1)} %get-tuple-element.58), channel_id=1, source_target_pairs={{0,128},{128,0},{1,129},{129,1},{2,130},{130,2},{3,131},{131,3},{4... | collective-permute-start | bytes 786440 | tf_op jit(solution)/shard_map/ppermute | solution.py:39
  40.6 17.1 %collective-permute-start = (bf16[4,128,256]{2,1,0:T(8,128)(2,1)S(1)}, bf16[4,128,256]{2,1,0:T(8,128)(2,1)S(1)}, u32[]{:S(2)}, u32[]{:S(2)}) collective-permute-start(bf16[4,128,256]{2,1,0:T(8,128)(2,1)S(1)} %get-tuple-element.44.own), channel_id=1, source_target_pairs={{0,1},{1,2},{2,3},{3,4},{4,5},{5,6},{6,7},{7,8},{8,9},{9,10},{10,1... | collective-permute-start | bytes 786440 | tf_op jit(solution)/shard_map/ppermute | solution.py:39
  40.6 17.1 %collective-permute-start.2 = (bf16[4,128,256]{2,1,0:T(8,128)(2,1)S(1)}, bf16[4,128,256]{2,1,0:T(8,128)(2,1)S(1)}, u32[]{:S(2)}, u32[]{:S(2)}) collective-permute-start(bf16[4,128,256]{2,1,0:T(8,128)(2,1)S(1)} %collective-permute-done.1), channel_id=1, source_target_pairs={{0,3},{1,4},{2,5},{3,2},{4,7},{5,8},{6,9},{7,6},{8,11},{9,12},{10,... | collective-permute-start | bytes 786440 | tf_op jit(solution)/shard_map/ppermute | solution.py:361
  61.1 3.1 %collective-permute-start.9 = (bf16[2048,128]{1,0:T(8,128)(2,1)S(1)}, bf16[2048,128]{1,0:T(8,128)(2,1)S(1)}, u32[]{:S(2)}, u32[]{:S(2)}) collective-permute-start(bf16[2048,128]{1,0:T(8,128)(2,1)S(1)} %get-tuple-element.69), channel_id=1, source_target_pairs={{0,128},{128,0},{1,129},{129,1},{2,130},{130,2},{3,131},{131,3},{4... | collective-permute-start | bytes 1572872 | tf_op jit(solution)/shard_map/ppermute | solution.py:39
  68.6 23.6 %collective-permute-start.10 = (bf16[2,128,512]{2,1,0:T(8,128)(2,1)S(1)}, bf16[2,128,512]{2,1,0:T(8,128)(2,1)S(1)}, u32[]{:S(2)}, u32[]{:S(2)}) collective-permute-start(bf16[2,128,512]{2,1,0:T(8,128)(2,1)S(1)} %get-tuple-element.77), channel_id=1, source_target_pairs={{0,127},{1,0},{2,1},{3,2},{4,3},{5,4},{6,5},{7,6},{8,7},{9,8},{10,... | collective-permute-start | bytes 786440 | tf_op jit(solution)/shard_map/ppermute | solution.py:39
  68.6 23.6 %collective-permute-start.11 = (bf16[2,128,512]{2,1,0:T(8,128)(2,1)S(1)}, bf16[2,128,512]{2,1,0:T(8,128)(2,1)S(1)}, u32[]{:S(2)}, u32[]{:S(2)}) collective-permute-start(bf16[2,128,512]{2,1,0:T(8,128)(2,1)S(1)} %get-tuple-element.78), channel_id=1, source_target_pairs={{0,126},{1,127},{2,0},{3,1},{4,2},{5,3},{6,4},{7,5},{8,6},{9,7},{1... | collective-permute-start | bytes 786440 | tf_op jit(solution)/shard_map/ppermute | solution.py:39

commit v4 on v3

--- a/solution.py
+++ b/solution.py
@@ -20,6 +20,14 @@
 VMEM_LIMIT = 16 << 20
 X_CHIPS = 4
 RELAYED = (2,)
+ORDER = (
+    ("attend", 0),
+    ("attend", 1),
+    ("grad", 0),
+    ("grad", 1),
+    ("attend", 2),
+    ("grad", 2),
+)
 
 NEG_FILL = -1e30
 SCALE = HEAD_DIM ** (-0.5)
@@ -363,24 +371,22 @@
             nb2 = rotate(block, "ctx", 2)
         near.append((nb1, nb2))
     carried = None
-    waiting = []
-
-    def close(carried):
-        part, outs, recv, lse = waiting.pop(0)
+    token = None
+    held = {}
+    for kind, part in ORDER:
         own, (nb1, nb2) = packs[part], near[part]
-        return backward(
-            part, stage, s_query, own, nb1, nb2, masks, outs, recv, lse, carried, senders
-        )
-
-    for part in range(PARTS):
-        own, (nb1, nb2) = packs[part], near[part]
-        mark = stage
-        if carried is not None:
-            mark, held = lax.optimization_barrier((stage, carried[-1]))
-            carried = (*carried[:-1], held)
-        s_out, t_out, send, lse = forward(part, mark, t_query, s_query, own, nb1, nb2, masks)
-        waiting.append((part, (s_out, t_out), (rotate(send, "pipe", 1)), lse))
-        carried = close(carried)
+        mark = lax.optimization_barrier((stage, token))[0] if token is not None else stage
+        if kind == "attend":
+            s_out, t_out, send, lse = forward(part, mark, t_query, s_query, own, nb1, nb2, masks)
+            recv = rotate(send, "pipe", 1)
+            held[part] = (s_out, t_out), recv, lse
+            token = lse
+        else:
+            outs, recv, lse = held.pop(part)
+            carried = backward(
+                part, mark, s_query, own, nb1, nb2, masks, outs, recv, lse, carried, senders
+            )
+            token = carried[-1]
     dq, local, back1, back2, squares = carried
     ret1, ret2 = (rotate(back1, "ctx", -1)), (rotate(back2, "ctx", -2))
     gathered = lax.all_to_all(squares, ("ctx", "pipe"), 0, 0, tiled=True)

time: 93.3 us -> 82 us (0.88)
  waiting for transfers between devices: 38.7 us -> 23.2 us
  starting transfers between devices: 9.95 us -> 13.4 us
    ppermute x10, waiting for transfers between devices: 38.7 us -> 23.2 us  [rotate(): lax.ppermute(block, axis, [(i, (i + distance) % count) for i in range(cou...]
    ppermute x1, starting transfers between devices: 0.01 us -> 3.38 us  [per_device(): nb2 = lax.ppermute(block, 'ctx', first)]
  transfers between devices with their start and end apart: 12 -> 12, of which waited for: 7 -> 4; matrix products, arithmetic and copies ran while one was open for 0% -> 0% of each run, Pallas kernels for 9% -> 12%
where the time goes in v4:
time: 82 us; the launch traced here: 81.7 us
  blocking collectives  24.2 us (30%)
  waiting for transfers between devices  23.2 us (28%)
  Pallas kernels  20.1 us (25%)
  starting transfers between devices  13.4 us (16%)
    all_to_all x1, blocking collectives, per_device(): gathered = lax.all_to_all(squares, ('ctx', 'pipe'), 0, 0, tiled=True)  24.2 us
    ppermute x10, waiting for transfers between devices, rotate(): lax.ppermute(block, axis, [(i, (i + distance) % count) for i in range(cou...  23.2 us
    pallas_call x3, Pallas kernels, backward(): pl.pallas_call(functools.partial(backward_body, groups > 1, carried is no...  10.2 us
    ppermute x10, starting transfers between devices, rotate(): lax.ppermute(block, axis, [(i, (i + distance) % count) for i in range(cou...  10.1 us
    pallas_call x3, Pallas kernels, forward(): pl.pallas_call(forward_body, grid_spec=pltpu.PrefetchScalarGridSpec(num_s...  7.78 us
    ppermute x1, starting transfers between devices, per_device(): nb2 = lax.ppermute(block, 'ctx', first)  3.38 us
  transfers between devices with their start and end apart: 12, of which 4 were waited for; matrix products, arithmetic and copies ran while one was open for 0% of the time, Pallas kernels for 12%

profile of v4, /device:TPU:1, one launch (start us, length us, event | category | flops | bytes accessed | tf_op | source)
XLA Modules:
  0.0 81.7 jit_solution(12481196643057563745)
XLA Ops:
  0.6 1.3 %pack.1 = (bf16[4,128,128]{2,1,0:T(8,128)(2,1)S(1)}, bf16[4,128,128]{2,1,0:T(8,128)(2,1)S(1)}, bf16[4,128,256]{2,1,0:T(8,128)(2,1)S(1)}, f32[256,128]{1,0:T(8,12...) custom-call(s32[1]{0:T(128)} %bitcast.1.pos_ref, bf16[1,128,512]{2,1,0:T(8,128)(2,1)} %tk.1, ...), custom_call_target="tpu_custom_call" | custom-call | tf_op jit(solution)/shard_map/pack/pallas_call | solution.py:86
  2.0 3.6 %collective-permute-start.1 = (bf16[4,128,128]{2,1,0:T(8,128)(2,1)S(1)}, bf16[4,128,128]{2,1,0:T(8,128)(2,1)S(1)}, u32[]{:S(2)}, u32[]{:S(2)}) collective-permute-start(bf16[4,128,128]{2,1,0:T(8,128)(2,1)S(1)} %get-tuple-element.45.own), channel_id=1, source_target_pairs={{0,2},{1,3},{2,4},{3,5},{4,6},{5,7},{6,8},{7,9},{8,10},{9,11},{10,... | collective-permute-start | bytes 393224 | tf_op jit(solution)/shard_map/ppermute | solution.py:47
  5.6 0.3 collective-permute-start
  5.9 3.4 %collective-permute-start.7 = (bf16[4,128,256]{2,1,0:T(8,128)(2,1)S(1)}, bf16[4,128,256]{2,1,0:T(8,128)(2,1)S(1)}, u32[]{:S(2)}, u32[]{:S(2)}) collective-permute-start(bf16[4,128,256]{2,1,0:T(8,128)(2,1)S(1)} %get-tuple-element.68.own), channel_id=1, source_target_pairs={{0,3},{1,0},{2,1},{3,2},{4,7},{5,4},{6,5},{7,6},{8,11},{9,8},{10,9... | collective-permute-start | bytes 786440 | tf_op jit(solution)/shard_map/ppermute | solution.py:368
  9.3 0.0 collective-permute-start.3
  9.3 0.6 collective-permute-start.2
  9.9 6.7 %collective-permute-done.1.nb2 = bf16[4,128,128]{2,1,0:T(8,128)(2,1)S(1)} collective-permute-done((bf16[4,128,128]{2,1,0:T(8,128)(2,1)S(1)}, bf16[4,128,128]{2,1,0:T(8,128)(2,1)S(1)}, u32[]{:S(2)}, u32[]{:S(2)}) %collective-permute-start.1) | collective-permute-done | bytes 131104 | tf_op jit(solution)/shard_map/ppermute | solution.py:47
  16.5 3.7 %collective-permute-done.nb1 = bf16[4,128,128]{2,1,0:T(8,128)(2,1)S(1)} collective-permute-done((bf16[4,128,128]{2,1,0:T(8,128)(2,1)S(1)}, bf16[4,128,128]{2,1,0:T(8,128)(2,1)S(1)}, u32[]{:S(2)}, u32[]{:S(2)}) %collective-permute-start) | collective-permute-done | bytes 131104 | tf_op jit(solution)/shard_map/ppermute | solution.py:47
  20.3 2.2 %forward.3 = (bf16[1024,128]{1,0:T(8,128)(2,1)S(1)}, bf16[1024,128]{1,0:T(8,128)(2,1)S(1)}, bf16[1024,128]{1,0:T(8,128)(2,1)S(1)}, f32[8,128]{1,0:T(8,128)S(1)}) custom-call(s32[1]{0:T(128)} %bitcast.stage_ref, bf16[1,128,4096]{2,1,0:T(8,128)(2,1)} %tq.5, bf16[1,128,4096]{2,1,0:T(8,128)(2,1)} %sq.11, bf16[4,128,128]{2,1,0:T(8,128)(2,1)S(1)} %get-tuple-element.45.own, ...), custom_call_target="tpu_custom_call" | custom-call | flops 402653184 | bytes 1572864 | tf_op jit(solution)/shard_map/forward/pallas_call | solution.py:191
  22.5 2.5 %collective-permute-start.4 = (bf16[1024,128]{1,0:T(8,128)(2,1)S(1)}, bf16[1024,128]{1,0:T(8,128)(2,1)S(1)}, u32[]{:S(2)}, u32[]{:S(2)}) collective-permute-start(bf16[1024,128]{1,0:T(8,128)(2,1)S(1)} %get-tuple-element.56), channel_id=1, source_target_pairs={{0,128},{128,0},{1,129},{129,1},{2,130},{130,2},{3,131},{131,3},{4... | collective-permute-start | bytes 786440 | tf_op jit(solution)/shard_map/ppermute | solution.py:47
  25.0 0.0 collective-permute-done.2.nb1
  25.0 2.2 %forward.4 = (bf16[1024,128]{1,0:T(8,128)(2,1)S(1)}, bf16[1024,128]{1,0:T(8,128)(2,1)S(1)}, bf16[1024,128]{1,0:T(8,128)(2,1)S(1)}, f32[8,128]{1,0:T(8,128)S(1)}) custom-call(s32[1]{0:T(128)} %bitcast.stage_ref, bf16[1,128,4096]{2,1,0:T(8,128)(2,1)} %tq.5, bf16[1,128,4096]{2,1,0:T(8,128)(2,1)} %sq.11, bf16[4,128,128]{2,1,0:T(8,128)(2,1)S(1)} %get-tuple-element.51.own, ...), custom_call_target="tpu_custom_call" | custom-call | flops 402653184 | bytes 1572864 | tf_op jit(solution)/shard_map/forward/pallas_call | solution.py:191
  27.2 1.4 %collective-permute-start.5 = (bf16[1024,128]{1,0:T(8,128)(2,1)S(1)}, bf16[1024,128]{1,0:T(8,128)(2,1)S(1)}, u32[]{:S(2)}, u32[]{:S(2)}) collective-permute-start(bf16[1024,128]{1,0:T(8,128)(2,1)S(1)} %get-tuple-element.61), channel_id=1, source_target_pairs={{0,128},{128,0},{1,129},{129,1},{2,130},{130,2},{3,131},{131,3},{4... | collective-permute-start | bytes 786440 | tf_op jit(solution)/shard_map/ppermute | solution.py:47
  28.6 0.0 collective-permute-start.8
  28.6 0.0 collective-permute-done.4.recv
  28.6 2.9 %backward.3 = (f32[1,128,4096]{2,1,0:T(8,128)}, f32[2,128,512]{2,1,0:T(8,128)S(1)}, bf16[2,128,512]{2,1,0:T(8,128)(2,1)S(1)}, bf16[2,128,512]{2,1,0:T(8,128)(2,1)S(1)}, f32[8,128]{1,0:T(8,128)S(1)}) custom-call(s32[1]{0:T(128)} %bitcast.stage_ref, bf16[1,128,4096]{2,1,0:T(8,128)(2,1)} %sq.11, bf16[4,128,128]{2,1,0:T(8,128)(2,1)S(1)} %get-tuple-element.45.own, ...), custom_call_target="tpu_custom_call" | custom-call | flops 503316480 | bytes 1572864 | tf_op jit(solution)/shard_map/backward/pallas_call | solution.py:302
  31.5 2.9 %backward.4 = (f32[1,128,4096]{2,1,0:T(8,128)}, f32[2,128,512]{2,1,0:T(8,128)S(1)}, bf16[2,128,512]{2,1,0:T(8,128)(2,1)S(1)}, bf16[2,128,512]{2,1,0:T(8,128)(2,1)S(1)}, f32[8,128]{1,0:T(8,128)S(1)}) custom-call(s32[1]{0:T(128)} %bitcast.stage_ref, ...), custom_call_target="tpu_custom_call", output_to_operand_aliasing={{0}: (13, {}), {1}: (14, {}), {2}: (15, {}), {3}: (16, {})} | custom-call | flops 503316480 | bytes 1572864 | tf_op jit(solution)/shard_map/backward/pallas_call | solution.py:302
  34.4 11.3 %collective-permute-done.6.nb1 = bf16[4,128,256]{2,1,0:T(8,128)(2,1)S(1)} collective-permute-done((bf16[4,128,256]{2,1,0:T(8,128)(2,1)S(1)}, bf16[4,128,256]{2,1,0:T(8,128)(2,1)S(1)}, u32[]{:S(2)}, u32[]{:S(2)}) %collective-permute-start.6) | collective-permute-done | bytes 262176 | tf_op jit(solution)/shard_map/ppermute | solution.py:47
  45.7 3.4 %forward.5 = (bf16[2048,128]{1,0:T(8,128)(2,1)S(1)}, bf16[2048,128]{1,0:T(8,128)(2,1)S(1)}, bf16[2048,128]{1,0:T(8,128)(2,1)S(1)}, f32[16,128]{1,0:T(8,128)S(1)}) custom-call(s32[1]{0:T(128)} %bitcast.stage_ref, bf16[1,128,4096]{2,1,0:T(8,128)(2,1)} %tq.5, bf16[1,128,4096]{2,1,0:T(8,128)(2,1)} %sq.11, bf16[4,128,256]{2,1,0:T(8,128)(2,1)S(1)} %get-tuple-element.68.own, ...), custom_call_target="tpu_custom_call" | custom-call | flops 805306368 | bytes 3145728 | tf_op jit(solution)/shard_map/forward/pallas_call | solution.py:191
  49.1 1.6 %collective-permute-start.9 = (bf16[2048,128]{1,0:T(8,128)(2,1)S(1)}, bf16[2048,128]{1,0:T(8,128)(2,1)S(1)}, u32[]{:S(2)}, u32[]{:S(2)}) collective-permute-start(bf16[2048,128]{1,0:T(8,128)(2,1)S(1)} %get-tuple-element.73), channel_id=1, source_target_pairs={{0,128},{128,0},{1,129},{129,1},{2,130},{130,2},{3,131},{131,3},{4... | collective-permute-start | bytes 1572872 | tf_op jit(solution)/shard_map/ppermute | solution.py:47
  50.7 1.5 %collective-permute-done.9.recv = bf16[2048,128]{1,0:T(8,128)(2,1)S(1)} collective-permute-done((bf16[2048,128]{1,0:T(8,128)(2,1)S(1)}, bf16[2048,128]{1,0:T(8,128)(2,1)S(1)}, u32[]{:S(2)}, u32[]{:S(2)}) %collective-permute-start.9) | collective-permute-done | bytes 524320 | tf_op jit(solution)/shard_map/ppermute | solution.py:47
  52.2 4.4 %backward.5 = (f32[1,128,4096]{2,1,0:T(8,128)}, f32[2,128,512]{2,1,0:T(8,128)S(1)}, bf16[2,128,512]{2,1,0:T(8,128)(2,1)S(1)}, bf16[2,128,512]{2,1,0:T(8,128)(2,1)S(1)}, f32[256,128]{1,0:T(8,128)S(1)}) custom-call(s32[1]{0:T(128)} %bitcast.stage_ref, ...), custom_call_target="tpu_custom_call", output_to_operand_aliasing={{0}: (13, {}), {1}: (14, {}), {2}: (15, {}), {3}: (16, {})} | custom-call | flops 1006632960 | bytes 3145728 | tf_op jit(solution)/shard_map/backward/pallas_call | solution.py:302
  56.6 24.2 %all_to_all.11 = f32[256,1,128]{2,1,0:T(1,128)S(1)} all-to-all(f32[256,1,128]{2,1,0:T(1,128)S(1)} %bitcast.9), channel_id=1, replica_groups=mesh['pipe'=2,'ctx'=128] {'ctx','pipe'}, dimensions={0} | all-to-all | bytes 262144 | tf_op jit(solution)/shard_map/all_to_all | solution.py:392
  80.8 0.9 %finish.1 = (f32[1,1]{1,0:T(1,128)}, f32[1,128,512]{2,1,0:T(8,128)}, f32[1,128,512]{2,1,0:T(8,128)}) custom-call(f32[2,128,512]{2,1,0:T(8,128)S(1)} %get-tuple-element.78.local, bf16[2,128,512]{2,1,0:T(8,128)(2,1)S(1)} %collective-permute-done.10.ret1, bf16[2,128,512]{2,1,0:T(8,128)(2,1)S(1)} %collective-permute-done.11.ret2, f32[256,128]{1,0:T(8,128)S(1)} %bitcast.8), custom_call_target="tpu_custom_call" | custom-call | tf_op jit(solution)/shard_map/finish/pallas_call | solution.py:340
  (9 shorter events, 0.0 us)
Async XLA Ops:
  2.0 14.6 %collective-permute-start.1 = (bf16[4,128,128]{2,1,0:T(8,128)(2,1)S(1)}, bf16[4,128,128]{2,1,0:T(8,128)(2,1)S(1)}, u32[]{:S(2)}, u32[]{:S(2)}) collective-permute-start(bf16[4,128,128]{2,1,0:T(8,128)(2,1)S(1)} %get-tuple-element.45.own), channel_id=1, source_target_pairs={{0,2},{1,3},{2,4},{3,5},{4,6},{5,7},{6,8},{7,9},{8,10},{9,11},{10,... | collective-permute-start | bytes 393224 | tf_op jit(solution)/shard_map/ppermute | solution.py:47
  5.6 14.7 %collective-permute-start = (bf16[4,128,128]{2,1,0:T(8,128)(2,1)S(1)}, bf16[4,128,128]{2,1,0:T(8,128)(2,1)S(1)}, u32[]{:S(2)}, u32[]{:S(2)}) collective-permute-start(bf16[4,128,128]{2,1,0:T(8,128)(2,1)S(1)} %get-tuple-element.45.own), channel_id=1, source_target_pairs={{0,1},{1,2},{2,3},{3,4},{4,5},{5,6},{6,7},{7,8},{8,9},{9,10},{10,1... | collective-permute-start | bytes 393224 | tf_op jit(solution)/shard_map/ppermute | solution.py:47
  5.9 22.7 %collective-permute-start.7 = (bf16[4,128,256]{2,1,0:T(8,128)(2,1)S(1)}, bf16[4,128,256]{2,1,0:T(8,128)(2,1)S(1)}, u32[]{:S(2)}, u32[]{:S(2)}) collective-permute-start(bf16[4,128,256]{2,1,0:T(8,128)(2,1)S(1)} %get-tuple-element.68.own), channel_id=1, source_target_pairs={{0,3},{1,0},{2,1},{3,2},{4,7},{5,4},{6,5},{7,6},{8,11},{9,8},{10,9... | collective-permute-start | bytes 786440 | tf_op jit(solution)/shard_map/ppermute | solution.py:368
  9.3 15.7 %collective-permute-start.3 = (bf16[4,128,128]{2,1,0:T(8,128)(2,1)S(1)}, bf16[4,128,128]{2,1,0:T(8,128)(2,1)S(1)}, u32[]{:S(2)}, u32[]{:S(2)}) collective-permute-start(bf16[4,128,128]{2,1,0:T(8,128)(2,1)S(1)} %get-tuple-element.51.own), channel_id=1, source_target_pairs={{0,2},{1,3},{2,4},{3,5},{4,6},{5,7},{6,8},{7,9},{8,10},{9,11},{10,... | collective-permute-start | bytes 393224 | tf_op jit(solution)/shard_map/ppermute | solution.py:47
  9.3 15.7 %collective-permute-start.2 = (bf16[4,128,128]{2,1,0:T(8,128)(2,1)S(1)}, bf16[4,128,128]{2,1,0:T(8,128)(2,1)S(1)}, u32[]{:S(2)}, u32[]{:S(2)}) collective-permute-start(bf16[4,128,128]{2,1,0:T(8,128)(2,1)S(1)} %get-tuple-element.51.own), channel_id=1, source_target_pairs={{0,1},{1,2},{2,3},{3,4},{4,5},{5,6},{6,7},{7,8},{8,9},{9,10},{10,1... | collective-permute-start | bytes 393224 | tf_op jit(solution)/shard_map/ppermute | solution.py:47
  22.5 6.2 %collective-permute-start.4 = (bf16[1024,128]{1,0:T(8,128)(2,1)S(1)}, bf16[1024,128]{1,0:T(8,128)(2,1)S(1)}, u32[]{:S(2)}, u32[]{:S(2)}) collective-permute-start(bf16[1024,128]{1,0:T(8,128)(2,1)S(1)} %get-tuple-element.56), channel_id=1, source_target_pairs={{0,128},{128,0},{1,129},{129,1},{2,130},{130,2},{3,131},{131,3},{4... | collective-permute-start | bytes 786440 | tf_op jit(solution)/shard_map/ppermute | solution.py:47
  27.2 4.3 %collective-permute-start.5 = (bf16[1024,128]{1,0:T(8,128)(2,1)S(1)}, bf16[1024,128]{1,0:T(8,128)(2,1)S(1)}, u32[]{:S(2)}, u32[]{:S(2)}) collective-permute-start(bf16[1024,128]{1,0:T(8,128)(2,1)S(1)} %get-tuple-element.61), channel_id=1, source_target_pairs={{0,128},{128,0},{1,129},{129,1},{2,130},{130,2},{3,131},{131,3},{4... | collective-permute-start | bytes 786440 | tf_op jit(solution)/shard_map/ppermute | solution.py:47
  28.6 17.1 %collective-permute-start.6 = (bf16[4,128,256]{2,1,0:T(8,128)(2,1)S(1)}, bf16[4,128,256]{2,1,0:T(8,128)(2,1)S(1)}, u32[]{:S(2)}, u32[]{:S(2)}) collective-permute-start(bf16[4,128,256]{2,1,0:T(8,128)(2,1)S(1)} %get-tuple-element.68.own), channel_id=1, source_target_pairs={{0,1},{1,2},{2,3},{3,4},{4,5},{5,6},{6,7},{7,8},{8,9},{9,10},{10,1... | collective-permute-start | bytes 786440 | tf_op jit(solution)/shard_map/ppermute | solution.py:47
  28.6 17.1 %collective-permute-start.8 = (bf16[4,128,256]{2,1,0:T(8,128)(2,1)S(1)}, bf16[4,128,256]{2,1,0:T(8,128)(2,1)S(1)}, u32[]{:S(2)}, u32[]{:S(2)}) collective-permute-start(bf16[4,128,256]{2,1,0:T(8,128)(2,1)S(1)} %collective-permute-done.7), channel_id=1, source_target_pairs={{0,3},{1,4},{2,5},{3,2},{4,7},{5,8},{6,9},{7,6},{8,11},{9,12},{10,... | collective-permute-start | bytes 786440 | tf_op jit(solution)/shard_map/ppermute | solution.py:369
  49.1 3.1 %collective-permute-start.9 = (bf16[2048,128]{1,0:T(8,128)(2,1)S(1)}, bf16[2048,128]{1,0:T(8,128)(2,1)S(1)}, u32[]{:S(2)}, u32[]{:S(2)}) collective-permute-start(bf16[2048,128]{1,0:T(8,128)(2,1)S(1)} %get-tuple-element.73), channel_id=1, source_target_pairs={{0,128},{128,0},{1,129},{129,1},{2,130},{130,2},{3,131},{131,3},{4... | collective-permute-start | bytes 1572872 | tf_op jit(solution)/shard_map/ppermute | solution.py:47
  56.6 24.2 %collective-permute-start.10 = (bf16[2,128,512]{2,1,0:T(8,128)(2,1)S(1)}, bf16[2,128,512]{2,1,0:T(8,128)(2,1)S(1)}, u32[]{:S(2)}, u32[]{:S(2)}) collective-permute-start(bf16[2,128,512]{2,1,0:T(8,128)(2,1)S(1)} %get-tuple-element.79), channel_id=1, source_target_pairs={{0,127},{1,0},{2,1},{3,2},{4,3},{5,4},{6,5},{7,6},{8,7},{9,8},{10,... | collective-permute-start | bytes 786440 | tf_op jit(solution)/shard_map/ppermute | solution.py:47
  56.6 24.2 %collective-permute-start.11 = (bf16[2,128,512]{2,1,0:T(8,128)(2,1)S(1)}, bf16[2,128,512]{2,1,0:T(8,128)(2,1)S(1)}, u32[]{:S(2)}, u32[]{:S(2)}) collective-permute-start(bf16[2,128,512]{2,1,0:T(8,128)(2,1)S(1)} %get-tuple-element.80), channel_id=1, source_target_pairs={{0,126},{1,127},{2,0},{3,1},{4,2},{5,3},{6,4},{7,5},{8,6},{9,7},{1... | collective-permute-start | bytes 786440 | tf_op jit(solution)/shard_map/ppermute | solution.py:47

commit v5 on v4

--- a/solution.py
+++ b/solution.py
@@ -9,6 +9,7 @@
 REACH = 2
 HEADS = 32
 KV_HEADS = 4
+SECTIONS = 2
 HEAD_DIM = 128
 GROUP = HEADS // KV_HEADS
 TOK = 128
@@ -275,12 +276,11 @@
     loss[...] = jnp.broadcast_to(total + before, loss.shape)
 
 
-def backward(part, stage, s_query, own, nb1, nb2, masks, outs, recv, lse, carried, senders):
+def backward(part, stage, s_query, own, nb1, nb2, masks, outs, recv, lse, carried):
     width = GROUP * HEAD_DIM
     groups = SPLIT[part]
     total = groups * width
-    last = part == PARTS - 1
-    flat = senders if last else 8
+    flat = 8
     query = pl.BlockSpec((1, TOK, width), lambda g, st: (0, 0, OFFSET[part] + g))
     kv = pl.BlockSpec((2, TOK, HEAD_DIM), lambda g, st: (1, 0, g))
     flipped = pl.BlockSpec((width, TOK), lambda g, st: (g, 0))
@@ -330,7 +330,7 @@
 def finish_body(local, ret1, ret2, squares, loss, key_grad, value_grad):
     for m, out in enumerate((key_grad, value_grad)):
         out[0] = local[m] + ret1[m].astype(jnp.float32) + ret2[m].astype(jnp.float32)
-    count = squares.shape[0] * TOK * HEADS * HEAD_DIM
+    count = SECTIONS * squares.shape[0] * TOK * HEADS * HEAD_DIM
     rows = jnp.sum(squares[...], axis=0, keepdims=True)
     loss[...] = jnp.sum(rows, axis=1, keepdims=True) * (1.0 / count)
 
@@ -357,7 +357,7 @@
 def per_device(t_query, t_key, t_value, s_query, s_key, s_value, segment_ids):
     pos = lax.axis_index("ctx").astype(jnp.int32).reshape(1)
     stage = lax.axis_index("pipe").astype(jnp.int32).reshape(1)
-    senders = lax.axis_size("pipe") * lax.axis_size("ctx")
+    senders = lax.axis_size("ctx")
     packed = pack(pos, (t_key, t_value, s_key, s_value), segment_ids)
     packs, masks = packed[:PARTS], packed[PARTS:]
     near = []
@@ -383,13 +383,13 @@
             token = lse
         else:
             outs, recv, lse = held.pop(part)
-            carried = backward(
-                part, mark, s_query, own, nb1, nb2, masks, outs, recv, lse, carried, senders
-            )
+            carried = backward(part, mark, s_query, own, nb1, nb2, masks, outs, recv, lse, carried)
             token = carried[-1]
     dq, local, back1, back2, squares = carried
     ret1, ret2 = (rotate(back1, "ctx", -1)), (rotate(back2, "ctx", -2))
-    gathered = lax.all_to_all(squares, ("ctx", "pipe"), 0, 0, tiled=True)
+    pooled = squares[:1] + rotate(squares, "pipe", 1)[:1]
+    sent = jnp.broadcast_to(pooled, (senders, TOK))
+    gathered = lax.all_to_all(sent, "ctx", 0, 0, tiled=True)
     loss, key_grad, value_grad = finish(local, ret1, ret2, gathered)
     return (loss.reshape(()), dq, key_grad, value_grad)
 

time: 82 us -> 80.6 us (0.983)
  blocking collectives: 24.2 us -> 21.6 us
    all_to_all x1, blocking collectives: 24.2 us -> 21.6 us  [per_device(): gathered = lax.all_to_all(sent, 'ctx', 0, 0, tiled=True)]
    ppermute x10 -> x11, waiting for transfers between devices: 23.2 us -> 24 us  [rotate(): lax.ppermute(block, axis, [(i, (i + distance) % count) for i in range(cou...]
    ppermute x10 -> x11, starting transfers between devices: 10.1 us -> 10.4 us  [rotate(): lax.ppermute(block, axis, [(i, (i + distance) % count) for i in range(cou...]
  transfers between devices with their start and end apart: 12 -> 13, of which waited for: 4 -> 5; matrix products, arithmetic and copies ran while one was open for 0% -> 0% of each run, Pallas kernels for 12% -> 13%
where the time goes in v5:
time: 80.6 us; the launch traced here: 80.3 us
  waiting for transfers between devices  24 us (30%)
  blocking collectives  21.6 us (27%)
  Pallas kernels  20.1 us (25%)
  starting transfers between devices  13.8 us (17%)
    ppermute x11, waiting for transfers between devices, rotate(): lax.ppermute(block, axis, [(i, (i + distance) % count) for i in range(cou...  24 us
    all_to_all x1, blocking collectives, per_device(): gathered = lax.all_to_all(sent, 'ctx', 0, 0, tiled=True)  21.6 us
    ppermute x11, starting transfers between devices, rotate(): lax.ppermute(block, axis, [(i, (i + distance) % count) for i in range(cou...  10.4 us
    pallas_call x3, Pallas kernels, backward(): pl.pallas_call(functools.partial(backward_body, groups > 1, carried is no...  10.1 us
    pallas_call x3, Pallas kernels, forward(): pl.pallas_call(forward_body, grid_spec=pltpu.PrefetchScalarGridSpec(num_s...  7.78 us
    ppermute x1, starting transfers between devices, per_device(): nb2 = lax.ppermute(block, 'ctx', first)  3.38 us
  transfers between devices with their start and end apart: 13, of which 5 were waited for; matrix products, arithmetic and copies ran while one was open for 0% of the time, Pallas kernels for 13%

profile of v5, /device:TPU:1, one launch (start us, length us, event | category | flops | bytes accessed | tf_op | source)
XLA Modules:
  0.0 80.3 jit_solution(6538802987010525536)
XLA Ops:
  0.6 1.3 %pack.1 = (bf16[4,128,128]{2,1,0:T(8,128)(2,1)S(1)}, bf16[4,128,128]{2,1,0:T(8,128)(2,1)S(1)}, bf16[4,128,256]{2,1,0:T(8,128)(2,1)S(1)}, f32[256,128]{1,0:T(8,12...) custom-call(s32[1]{0:T(128)} %bitcast.1.pos_ref, bf16[1,128,512]{2,1,0:T(8,128)(2,1)} %tk.1, ...), custom_call_target="tpu_custom_call" | custom-call | tf_op jit(solution)/shard_map/pack/pallas_call | solution.py:87
  2.0 3.6 %collective-permute-start.1 = (bf16[4,128,128]{2,1,0:T(8,128)(2,1)S(1)}, bf16[4,128,128]{2,1,0:T(8,128)(2,1)S(1)}, u32[]{:S(2)}, u32[]{:S(2)}) collective-permute-start(bf16[4,128,128]{2,1,0:T(8,128)(2,1)S(1)} %get-tuple-element.45.own), channel_id=1, source_target_pairs={{0,2},{1,3},{2,4},{3,5},{4,6},{5,7},{6,8},{7,9},{8,10},{9,11},{10,... | collective-permute-start | bytes 393224 | tf_op jit(solution)/shard_map/ppermute | solution.py:48
  5.6 0.3 collective-permute-start
  5.9 3.4 %collective-permute-start.7 = (bf16[4,128,256]{2,1,0:T(8,128)(2,1)S(1)}, bf16[4,128,256]{2,1,0:T(8,128)(2,1)S(1)}, u32[]{:S(2)}, u32[]{:S(2)}) collective-permute-start(bf16[4,128,256]{2,1,0:T(8,128)(2,1)S(1)} %get-tuple-element.68.own), channel_id=1, source_target_pairs={{0,3},{1,0},{2,1},{3,2},{4,7},{5,4},{6,5},{7,6},{8,11},{9,8},{10,9... | collective-permute-start | bytes 786440 | tf_op jit(solution)/shard_map/ppermute | solution.py:368
  9.3 0.0 collective-permute-start.3
  9.3 0.6 collective-permute-start.2
  9.9 6.7 %collective-permute-done.1.nb2 = bf16[4,128,128]{2,1,0:T(8,128)(2,1)S(1)} collective-permute-done((bf16[4,128,128]{2,1,0:T(8,128)(2,1)S(1)}, bf16[4,128,128]{2,1,0:T(8,128)(2,1)S(1)}, u32[]{:S(2)}, u32[]{:S(2)}) %collective-permute-start.1) | collective-permute-done | bytes 131104 | tf_op jit(solution)/shard_map/ppermute | solution.py:48
  16.5 3.7 %collective-permute-done.nb1 = bf16[4,128,128]{2,1,0:T(8,128)(2,1)S(1)} collective-permute-done((bf16[4,128,128]{2,1,0:T(8,128)(2,1)S(1)}, bf16[4,128,128]{2,1,0:T(8,128)(2,1)S(1)}, u32[]{:S(2)}, u32[]{:S(2)}) %collective-permute-start) | collective-permute-done | bytes 131104 | tf_op jit(solution)/shard_map/ppermute | solution.py:48
  20.3 2.2 %forward.3 = (bf16[1024,128]{1,0:T(8,128)(2,1)S(1)}, bf16[1024,128]{1,0:T(8,128)(2,1)S(1)}, bf16[1024,128]{1,0:T(8,128)(2,1)S(1)}, f32[8,128]{1,0:T(8,128)S(1)}) custom-call(s32[1]{0:T(128)} %bitcast.stage_ref, bf16[1,128,4096]{2,1,0:T(8,128)(2,1)} %tq.5, bf16[1,128,4096]{2,1,0:T(8,128)(2,1)} %sq.11, bf16[4,128,128]{2,1,0:T(8,128)(2,1)S(1)} %get-tuple-element.45.own, ...), custom_call_target="tpu_custom_call" | custom-call | flops 402653184 | bytes 1572864 | tf_op jit(solution)/shard_map/forward/pallas_call | solution.py:192
  22.5 2.5 %collective-permute-start.4 = (bf16[1024,128]{1,0:T(8,128)(2,1)S(1)}, bf16[1024,128]{1,0:T(8,128)(2,1)S(1)}, u32[]{:S(2)}, u32[]{:S(2)}) collective-permute-start(bf16[1024,128]{1,0:T(8,128)(2,1)S(1)} %get-tuple-element.56), channel_id=1, source_target_pairs={{0,128},{128,0},{1,129},{129,1},{2,130},{130,2},{3,131},{131,3},{4... | collective-permute-start | bytes 786440 | tf_op jit(solution)/shard_map/ppermute | solution.py:48
  25.0 2.2 %forward.4 = (bf16[1024,128]{1,0:T(8,128)(2,1)S(1)}, bf16[1024,128]{1,0:T(8,128)(2,1)S(1)}, bf16[1024,128]{1,0:T(8,128)(2,1)S(1)}, f32[8,128]{1,0:T(8,128)S(1)}) custom-call(s32[1]{0:T(128)} %bitcast.stage_ref, bf16[1,128,4096]{2,1,0:T(8,128)(2,1)} %tq.5, bf16[1,128,4096]{2,1,0:T(8,128)(2,1)} %sq.11, bf16[4,128,128]{2,1,0:T(8,128)(2,1)S(1)} %get-tuple-element.51.own, ...), custom_call_target="tpu_custom_call" | custom-call | flops 402653184 | bytes 1572864 | tf_op jit(solution)/shard_map/forward/pallas_call | solution.py:192
  27.2 1.4 %collective-permute-start.5 = (bf16[1024,128]{1,0:T(8,128)(2,1)S(1)}, bf16[1024,128]{1,0:T(8,128)(2,1)S(1)}, u32[]{:S(2)}, u32[]{:S(2)}) collective-permute-start(bf16[1024,128]{1,0:T(8,128)(2,1)S(1)} %get-tuple-element.61), channel_id=1, source_target_pairs={{0,128},{128,0},{1,129},{129,1},{2,130},{130,2},{3,131},{131,3},{4... | collective-permute-start | bytes 786440 | tf_op jit(solution)/shard_map/ppermute | solution.py:48
  28.6 0.0 collective-permute-start.8
  28.6 2.9 %backward.3 = (f32[1,128,4096]{2,1,0:T(8,128)}, f32[2,128,512]{2,1,0:T(8,128)S(1)}, bf16[2,128,512]{2,1,0:T(8,128)(2,1)S(1)}, bf16[2,128,512]{2,1,0:T(8,128)(2,1)S(1)}, f32[8,128]{1,0:T(8,128)S(1)}) custom-call(s32[1]{0:T(128)} %bitcast.stage_ref, bf16[1,128,4096]{2,1,0:T(8,128)(2,1)} %sq.11, bf16[4,128,128]{2,1,0:T(8,128)(2,1)S(1)} %get-tuple-element.45.own, ...), custom_call_target="tpu_custom_call" | custom-call | flops 503316480 | bytes 1572864 | tf_op jit(solution)/shard_map/backward/pallas_call | solution.py:302
  31.5 2.9 %backward.4 = (f32[1,128,4096]{2,1,0:T(8,128)}, f32[2,128,512]{2,1,0:T(8,128)S(1)}, bf16[2,128,512]{2,1,0:T(8,128)(2,1)S(1)}, bf16[2,128,512]{2,1,0:T(8,128)(2,1)S(1)}, f32[8,128]{1,0:T(8,128)S(1)}) custom-call(s32[1]{0:T(128)} %bitcast.stage_ref, ...), custom_call_target="tpu_custom_call", output_to_operand_aliasing={{0}: (13, {}), {1}: (14, {}), {2}: (15, {}), {3}: (16, {})} | custom-call | flops 503316480 | bytes 1572864 | tf_op jit(solution)/shard_map/backward/pallas_call | solution.py:302
  34.4 11.3 %collective-permute-done.6.nb1 = bf16[4,128,256]{2,1,0:T(8,128)(2,1)S(1)} collective-permute-done((bf16[4,128,256]{2,1,0:T(8,128)(2,1)S(1)}, bf16[4,128,256]{2,1,0:T(8,128)(2,1)S(1)}, u32[]{:S(2)}, u32[]{:S(2)}) %collective-permute-start.6) | collective-permute-done | bytes 262176 | tf_op jit(solution)/shard_map/ppermute | solution.py:48
  45.7 3.4 %forward.5 = (bf16[2048,128]{1,0:T(8,128)(2,1)S(1)}, bf16[2048,128]{1,0:T(8,128)(2,1)S(1)}, bf16[2048,128]{1,0:T(8,128)(2,1)S(1)}, f32[16,128]{1,0:T(8,128)S(1)}) custom-call(s32[1]{0:T(128)} %bitcast.stage_ref, bf16[1,128,4096]{2,1,0:T(8,128)(2,1)} %tq.5, bf16[1,128,4096]{2,1,0:T(8,128)(2,1)} %sq.11, bf16[4,128,256]{2,1,0:T(8,128)(2,1)S(1)} %get-tuple-element.68.own, ...), custom_call_target="tpu_custom_call" | custom-call | flops 805306368 | bytes 3145728 | tf_op jit(solution)/shard_map/forward/pallas_call | solution.py:192
  49.1 1.6 %collective-permute-start.9 = (bf16[2048,128]{1,0:T(8,128)(2,1)S(1)}, bf16[2048,128]{1,0:T(8,128)(2,1)S(1)}, u32[]{:S(2)}, u32[]{:S(2)}) collective-permute-start(bf16[2048,128]{1,0:T(8,128)(2,1)S(1)} %get-tuple-element.73), channel_id=1, source_target_pairs={{0,128},{128,0},{1,129},{129,1},{2,130},{130,2},{3,131},{131,3},{4... | collective-permute-start | bytes 1572872 | tf_op jit(solution)/shard_map/ppermute | solution.py:48
  50.7 1.5 %collective-permute-done.9.recv = bf16[2048,128]{1,0:T(8,128)(2,1)S(1)} collective-permute-done((bf16[2048,128]{1,0:T(8,128)(2,1)S(1)}, bf16[2048,128]{1,0:T(8,128)(2,1)S(1)}, u32[]{:S(2)}, u32[]{:S(2)}) %collective-permute-start.9) | collective-permute-done | bytes 524320 | tf_op jit(solution)/shard_map/ppermute | solution.py:48
  52.2 4.4 %backward.5 = (f32[1,128,4096]{2,1,0:T(8,128)}, f32[2,128,512]{2,1,0:T(8,128)S(1)}, bf16[2,128,512]{2,1,0:T(8,128)(2,1)S(1)}, bf16[2,128,512]{2,1,0:T(8,128)(2,1)S(1)}, f32[8,128]{1,0:T(8,128)S(1)}) custom-call(s32[1]{0:T(128)} %bitcast.stage_ref, ...), custom_call_target="tpu_custom_call", output_to_operand_aliasing={{0}: (13, {}), {1}: (14, {}), {2}: (15, {}), {3}: (16, {})} | custom-call | flops 1006632960 | bytes 3145728 | tf_op jit(solution)/shard_map/backward/pallas_call | solution.py:302
  56.6 0.4 collective-permute-start.12
  56.9 0.8 %collective-permute-done.12 = f32[8,128]{1,0:T(8,128)S(1)} collective-permute-done((f32[8,128]{1,0:T(8,128)S(1)}, f32[8,128]{1,0:T(8,128)S(1)}, u32[]{:S(2)}, u32[]{:S(2)}) %collective-permute-start.12) | collective-permute-done | bytes 4128 | tf_op jit(solution)/shard_map/ppermute | solution.py:48
  57.8 21.6 %all_to_all.8 = f32[128,1,128]{2,1,0:T(1,128)S(1)} all-to-all(f32[128,1,128]{2,1,0:T(1,128)S(1)} %broadcast_in_dim.2), channel_id=1, replica_groups=mesh['pipe'=2,'ctx'=128] {'ctx'}, dimensions={0} | all-to-all | bytes 131072 | tf_op jit(solution)/shard_map/all_to_all | solution.py:392
  79.4 0.9 %finish.1 = (f32[1,1]{1,0:T(1,128)}, f32[1,128,512]{2,1,0:T(8,128)}, f32[1,128,512]{2,1,0:T(8,128)}) custom-call(f32[2,128,512]{2,1,0:T(8,128)S(1)} %get-tuple-element.78.local, bf16[2,128,512]{2,1,0:T(8,128)(2,1)S(1)} %collective-permute-done.10.ret1, bf16[2,128,512]{2,1,0:T(8,128)(2,1)S(1)} %collective-permute-done.11.ret2, f32[128,128]{1,0:T(8,128)S(1)} %bitcast.7), custom_call_target="tpu_custom_call" | custom-call | tf_op jit(solution)/shard_map/finish/pallas_call | solution.py:340
  (13 shorter events, 0.1 us)
Async XLA Ops:
  2.0 14.6 %collective-permute-start.1 = (bf16[4,128,128]{2,1,0:T(8,128)(2,1)S(1)}, bf16[4,128,128]{2,1,0:T(8,128)(2,1)S(1)}, u32[]{:S(2)}, u32[]{:S(2)}) collective-permute-start(bf16[4,128,128]{2,1,0:T(8,128)(2,1)S(1)} %get-tuple-element.45.own), channel_id=1, source_target_pairs={{0,2},{1,3},{2,4},{3,5},{4,6},{5,7},{6,8},{7,9},{8,10},{9,11},{10,... | collective-permute-start | bytes 393224 | tf_op jit(solution)/shard_map/ppermute | solution.py:48
  5.6 14.7 %collective-permute-start = (bf16[4,128,128]{2,1,0:T(8,128)(2,1)S(1)}, bf16[4,128,128]{2,1,0:T(8,128)(2,1)S(1)}, u32[]{:S(2)}, u32[]{:S(2)}) collective-permute-start(bf16[4,128,128]{2,1,0:T(8,128)(2,1)S(1)} %get-tuple-element.45.own), channel_id=1, source_target_pairs={{0,1},{1,2},{2,3},{3,4},{4,5},{5,6},{6,7},{7,8},{8,9},{9,10},{10,1... | collective-permute-start | bytes 393224 | tf_op jit(solution)/shard_map/ppermute | solution.py:48
  5.9 22.7 %collective-permute-start.7 = (bf16[4,128,256]{2,1,0:T(8,128)(2,1)S(1)}, bf16[4,128,256]{2,1,0:T(8,128)(2,1)S(1)}, u32[]{:S(2)}, u32[]{:S(2)}) collective-permute-start(bf16[4,128,256]{2,1,0:T(8,128)(2,1)S(1)} %get-tuple-element.68.own), channel_id=1, source_target_pairs={{0,3},{1,0},{2,1},{3,2},{4,7},{5,4},{6,5},{7,6},{8,11},{9,8},{10,9... | collective-permute-start | bytes 786440 | tf_op jit(solution)/shard_map/ppermute | solution.py:368
  9.3 15.7 %collective-permute-start.3 = (bf16[4,128,128]{2,1,0:T(8,128)(2,1)S(1)}, bf16[4,128,128]{2,1,0:T(8,128)(2,1)S(1)}, u32[]{:S(2)}, u32[]{:S(2)}) collective-permute-start(bf16[4,128,128]{2,1,0:T(8,128)(2,1)S(1)} %get-tuple-element.51.own), channel_id=1, source_target_pairs={{0,2},{1,3},{2,4},{3,5},{4,6},{5,7},{6,8},{7,9},{8,10},{9,11},{10,... | collective-permute-start | bytes 393224 | tf_op jit(solution)/shard_map/ppermute | solution.py:48
  9.3 15.7 %collective-permute-start.2 = (bf16[4,128,128]{2,1,0:T(8,128)(2,1)S(1)}, bf16[4,128,128]{2,1,0:T(8,128)(2,1)S(1)}, u32[]{:S(2)}, u32[]{:S(2)}) collective-permute-start(bf16[4,128,128]{2,1,0:T(8,128)(2,1)S(1)} %get-tuple-element.51.own), channel_id=1, source_target_pairs={{0,1},{1,2},{2,3},{3,4},{4,5},{5,6},{6,7},{7,8},{8,9},{9,10},{10,1... | collective-permute-start | bytes 393224 | tf_op jit(solution)/shard_map/ppermute | solution.py:48
  22.5 6.2 %collective-permute-start.4 = (bf16[1024,128]{1,0:T(8,128)(2,1)S(1)}, bf16[1024,128]{1,0:T(8,128)(2,1)S(1)}, u32[]{:S(2)}, u32[]{:S(2)}) collective-permute-start(bf16[1024,128]{1,0:T(8,128)(2,1)S(1)} %get-tuple-element.56), channel_id=1, source_target_pairs={{0,128},{128,0},{1,129},{129,1},{2,130},{130,2},{3,131},{131,3},{4... | collective-permute-start | bytes 786440 | tf_op jit(solution)/shard_map/ppermute | solution.py:48
  27.2 4.3 %collective-permute-start.5 = (bf16[1024,128]{1,0:T(8,128)(2,1)S(1)}, bf16[1024,128]{1,0:T(8,128)(2,1)S(1)}, u32[]{:S(2)}, u32[]{:S(2)}) collective-permute-start(bf16[1024,128]{1,0:T(8,128)(2,1)S(1)} %get-tuple-element.61), channel_id=1, source_target_pairs={{0,128},{128,0},{1,129},{129,1},{2,130},{130,2},{3,131},{131,3},{4... | collective-permute-start | bytes 786440 | tf_op jit(solution)/shard_map/ppermute | solution.py:48
  28.6 17.1 %collective-permute-start.6 = (bf16[4,128,256]{2,1,0:T(8,128)(2,1)S(1)}, bf16[4,128,256]{2,1,0:T(8,128)(2,1)S(1)}, u32[]{:S(2)}, u32[]{:S(2)}) collective-permute-start(bf16[4,128,256]{2,1,0:T(8,128)(2,1)S(1)} %get-tuple-element.68.own), channel_id=1, source_target_pairs={{0,1},{1,2},{2,3},{3,4},{4,5},{5,6},{6,7},{7,8},{8,9},{9,10},{10,1... | collective-permute-start | bytes 786440 | tf_op jit(solution)/shard_map/ppermute | solution.py:48
  28.6 17.1 %collective-permute-start.8 = (bf16[4,128,256]{2,1,0:T(8,128)(2,1)S(1)}, bf16[4,128,256]{2,1,0:T(8,128)(2,1)S(1)}, u32[]{:S(2)}, u32[]{:S(2)}) collective-permute-start(bf16[4,128,256]{2,1,0:T(8,128)(2,1)S(1)} %collective-permute-done.7), channel_id=1, source_target_pairs={{0,3},{1,4},{2,5},{3,2},{4,7},{5,8},{6,9},{7,6},{8,11},{9,12},{10,... | collective-permute-start | bytes 786440 | tf_op jit(solution)/shard_map/ppermute | solution.py:369
  49.1 3.1 %collective-permute-start.9 = (bf16[2048,128]{1,0:T(8,128)(2,1)S(1)}, bf16[2048,128]{1,0:T(8,128)(2,1)S(1)}, u32[]{:S(2)}, u32[]{:S(2)}) collective-permute-start(bf16[2048,128]{1,0:T(8,128)(2,1)S(1)} %get-tuple-element.73), channel_id=1, source_target_pairs={{0,128},{128,0},{1,129},{129,1},{2,130},{130,2},{3,131},{131,3},{4... | collective-permute-start | bytes 1572872 | tf_op jit(solution)/shard_map/ppermute | solution.py:48
  56.6 1.2 %collective-permute-start.12 = (f32[8,128]{1,0:T(8,128)S(1)}, f32[8,128]{1,0:T(8,128)S(1)}, u32[]{:S(2)}, u32[]{:S(2)}) collective-permute-start(f32[8,128]{1,0:T(8,128)S(1)} %get-tuple-element.81), channel_id=1, source_target_pairs={{0,128},{128,0},{1,129},{129,1},{2,130},{130,2},{3,131},{131,3},{4... | collective-permute-start | bytes 12296 | tf_op jit(solution)/shard_map/ppermute | solution.py:48
  56.9 22.5 %collective-permute-start.10 = (bf16[2,128,512]{2,1,0:T(8,128)(2,1)S(1)}, bf16[2,128,512]{2,1,0:T(8,128)(2,1)S(1)}, u32[]{:S(2)}, u32[]{:S(2)}) collective-permute-start(bf16[2,128,512]{2,1,0:T(8,128)(2,1)S(1)} %get-tuple-element.79), channel_id=1, source_target_pairs={{0,127},{1,0},{2,1},{3,2},{4,3},{5,4},{6,5},{7,6},{8,7},{9,8},{10,... | collective-permute-start | bytes 786440 | tf_op jit(solution)/shard_map/ppermute | solution.py:48
  56.9 22.5 %collective-permute-start.11 = (bf16[2,128,512]{2,1,0:T(8,128)(2,1)S(1)}, bf16[2,128,512]{2,1,0:T(8,128)(2,1)S(1)}, u32[]{:S(2)}, u32[]{:S(2)}) collective-permute-start(bf16[2,128,512]{2,1,0:T(8,128)(2,1)S(1)} %get-tuple-element.80), channel_id=1, source_target_pairs={{0,126},{1,127},{2,0},{3,1},{4,2},{5,3},{6,4},{7,5},{8,6},{9,7},{1... | collective-permute-start | bytes 786440 | tf_op jit(solution)/shard_map/ppermute | solution.py:48
